TPU v7x, 256 devices: a whole 4x4x8 slice. The times are simulated.
256 devices in a mesh: req: 8 (over z_hi, x), tile: 16 (over z_lo, y), tp: 2 (over core).
Axes of the slice: x: 4, y: 4, z: 8 (z_hi: 2, z_lo: 4; z = z_hi * 4 + z_lo), core: 2. Of those that a mesh axis runs over, the one named last changes fastest.
Arguments:
- image_qkv: bfloat16 [128, 144, 3, 2048], P(('req', 'tile'), None, None, 'tp'), parts along dimension 0, may hold values from -6 to 6
- text_kv: bfloat16 [4096, 2, 2048], P(('req', 'tile'), None, 'tp'), parts along dimension 0, may hold values from -6 to 6
- q_gain: float32 [128], replicated, may hold values from 0.7 to 5
- k_gain: float32 [128], replicated, may hold values from 0.7 to 5
- out_weight: bfloat16 [2048, 3072], P('tp'), may hold values from -0.125 to 0.125
- hidden: bfloat16 [128, 144, 3072], P(('req', 'tile')), parts along dimension 0, may hold values from -6 to 6
- mlp_term: bfloat16 [128, 144, 3072], P(('req', 'tile')), parts along dimension 0, may hold values from -3 to 3
- gate: float32 [24576], P('req'), parts along dimension 0, may hold values from -4 to 4
- final_shift: float32 [24576], P('req'), parts along dimension 0, may hold values from -3 to 3
- final_scale: float32 [24576], P('req'), parts along dimension 0, may hold values from -3 to 3
- final_weight: bfloat16 [3072, 64], replicated, may hold values from -0.109375 to 0.109375
- final_bias: float32 [64], replicated, may hold values from -3 to 3
- latent: float32 [128, 144, 64], P(('req', 'tile')), parts along dimension 0, may hold values from -6 to 6
- image_size: int32 [16], P('req'), parts along dimension 0, may hold values from 24 to 48, as said below
- text_len: int32 [8], P('req'), parts along dimension 0, may hold values from 64 to 512
- timestep: int32 [8], P('req'), parts along dimension 0, may hold values from 0 to 27
Outputs:
- velocity: float32 [128, 144, 64], P(('req', 'tile')), parts along dimension 0
- latent_next: float32 [128, 144, 64], P(('req', 'tile')), parts along dimension 0
There are 8 independent parts, one for each index of `req`. A program takes and returns all parts, laid end to end along the dimension named above; an argument that names none is the same for every part. Nothing has to cross between parts.
Inputs may be any that keep to these rules, and one draw needn't show every extreme that they name: The larger of image_size[0] and image_size[1] equals 48.
All inputs are finite; a program needn't handle non-finite values.
Results may differ from a plain program's by a relative error of at most 0.014.
The roundings to bfloat16 on the way count: a program that leaves them out, or rounds other values in their place, can miss the bound.
Values may be sent and summed in bfloat16 or wider, within the bound.
No kernel may reach another device: no remote copies, remote signals or barrier semaphores. Data moves between devices by JAX's collectives and lax.ppermute only.
A program may use at most 128 MiB of HBM per device.

v0:
```python
import jax
import jax.numpy as jnp
from jax import lax
from jax.sharding import PartitionSpec as P

HEAD = 128
STEPS = 28
CANVAS = 48


def angle_table(row_pos, col_pos, head_size):
    first_part = head_size // 8
    side_dims = (head_size - first_part) // 2
    side_index = jnp.arange(side_dims // 2, dtype=jnp.float32)
    frequency = jnp.power(10000.0, -2.0 * side_index / side_dims)
    still = jnp.zeros(row_pos.shape + (first_part // 2,), jnp.float32)
    return jnp.concatenate(
        [still, row_pos[..., None] * frequency, col_pos[..., None] * frequency], axis=-1
    )


def norm_rope(vectors, gain_vector, angles):
    values_wide = vectors.astype(jnp.float32)
    scaled = (
        values_wide
        * lax.rsqrt(jnp.mean(values_wide * values_wide, axis=-1, keepdims=True) + 1e-06)
        * gain_vector
    )
    paired = scaled.reshape(scaled.shape[:-1] + (scaled.shape[-1] // 2, 2))
    cosine = jnp.cos(angles)[:, None, :]
    sine = jnp.sin(angles)[:, None, :]
    first_part = paired[..., 0]
    second_part = paired[..., 1]
    rotated = jnp.stack(
        [first_part * cosine - second_part * sine, first_part * sine + second_part * cosine],
        axis=-1,
    )
    return rotated.reshape(scaled.shape).astype(jnp.bfloat16)


def euler_step(image_size, timestep):
    area = (image_size[0] * image_size[1]).astype(jnp.float32)
    shift_factor = jnp.exp(0.5 + 0.65 * (area - 256.0) / 3840.0)
    now_time = 1.0 - timestep[0].astype(jnp.float32) / STEPS
    next_time = 1.0 - (timestep[0] + 1).astype(jnp.float32) / STEPS

    def sigma_of(moment):
        return shift_factor * moment / (shift_factor * moment + 1.0 - moment)

    return sigma_of(next_time) - sigma_of(now_time)


def grid_position(tile_number, local_index, grid_x, tile_h, tile_w):
    row_pos = tile_number // grid_x * tile_h + local_index // tile_w
    col_pos = tile_number % grid_x * tile_w + local_index % tile_w
    return (row_pos, col_pos)


def attend_block(state_carry, query_block, piece_keys, piece_values, key_mask):
    running_max, totals, blended = state_carry
    scale_factor = query_block.shape[-1] ** (-0.5)
    scores = (
        jnp.einsum("hqd,khd->hqk", query_block, piece_keys, preferred_element_type=jnp.float32)
        * scale_factor
    )
    scores = jnp.where(key_mask[None, None, :], scores, -jnp.inf)
    new_max = jnp.max(scores, axis=2)
    safe_max = jnp.where(new_max == -jnp.inf, 0.0, new_max)
    factor = jnp.exp(running_max - safe_max)
    weights = jnp.exp(scores - safe_max[..., None])
    totals = totals * factor + jnp.sum(weights, axis=2)
    blended = blended * factor[..., None] + jnp.einsum(
        "hqk,khd->hqd",
        weights.astype(jnp.bfloat16),
        piece_values,
        preferred_element_type=jnp.float32,
    )
    return (new_max, totals, blended)


def guarded(active, state_carry, query_block, piece_keys, piece_values, key_mask):

    def compute(inner_state):
        return attend_block(inner_state, query_block, piece_keys, piece_values, key_mask)

    def unchanged(inner_state):
        return inner_state

    return lax.cond(active, compute, unchanged, state_carry)


def shards(
    image_qkv,
    text_kv,
    q_gain,
    k_gain,
    out_weight,
    hidden,
    mlp_term,
    gate,
    final_shift,
    final_scale,
    final_weight,
    final_bias,
    latent,
    image_size,
    text_len,
    timestep,
):
    tile_count = lax.axis_size("tile")
    grid_x = min(tile_count, 4)
    grid_y = tile_count // grid_x
    tile_w = CANVAS // grid_x
    tile_h = CANVAS // grid_y
    pixels = tile_h * tile_w
    head_size = HEAD
    feature_width = image_qkv.shape[3]
    head_count = feature_width // head_size
    text_rows = text_kv.shape[0]
    model_width = hidden.shape[2]
    latent_width = final_weight.shape[1]
    tile_index = lax.axis_index("tile")
    local_index = jnp.arange(pixels, dtype=jnp.int32)
    row_pos, col_pos = grid_position(tile_index, local_index, grid_x, tile_h, tile_w)
    patch_live = (row_pos < image_size[0]) & (col_pos < image_size[1])
    angles = angle_table(row_pos.astype(jnp.float32), col_pos.astype(jnp.float32), head_size)
    triple = image_qkv.reshape(pixels, 3, head_count, head_size)
    text_pair = text_kv.reshape(text_rows, 2, head_count, head_size)
    own_query = norm_rope(triple[:, 0], q_gain, angles)
    text_keys = norm_rope(
        text_pair[:, 0], k_gain, jnp.zeros((text_rows, head_size // 2), jnp.float32)
    )
    block_keys = jnp.concatenate([norm_rope(triple[:, 1], k_gain, angles), text_keys], axis=0)
    block_values = jnp.concatenate([triple[:, 2], text_pair[:, 1]], axis=0)
    key_rows = pixels + text_rows
    query_live = (row_pos < image_size[0]) & (col_pos < image_size[1])
    query_heads = own_query.transpose(1, 0, 2)
    block_rows = pixels // 4
    piece_keys = lax.all_gather(block_keys, "tile", axis=0, tiled=True)
    piece_values = lax.all_gather(block_values, "tile", axis=0, tiled=True)
    index = jnp.arange(piece_keys.shape[0], dtype=jnp.int32)
    source = index // key_rows
    within = index % key_rows
    key_row, key_col = grid_position(source, within, grid_x, tile_h, tile_w)
    image_ok = (within < pixels) & (key_row < image_size[0]) & (key_col < image_size[1])
    slot = source * text_rows + within - pixels
    text_ok = (within >= pixels) & (slot < text_len[0])
    key_mask = image_ok | text_ok
    any_key = jnp.any(key_mask)
    running_max = jnp.full((head_count, pixels), -jnp.inf, jnp.float32)
    totals = jnp.zeros((head_count, pixels), jnp.float32)
    blended = jnp.zeros((head_count, pixels, head_size), jnp.float32)
    parts_max = []
    parts_total = []
    parts_blend = []
    for block_index in range(4):
        row_start = block_index * block_rows
        row_stop = row_start + block_rows
        active = any_key & jnp.any(query_live[row_start:row_stop])
        piece_state = (
            running_max[:, row_start:row_stop],
            totals[:, row_start:row_stop],
            blended[:, row_start:row_stop],
        )
        new_max, new_total, new_blend = guarded(
            active,
            piece_state,
            query_heads[:, row_start:row_stop],
            piece_keys,
            piece_values,
            key_mask,
        )
        parts_max.append(new_max)
        parts_total.append(new_total)
        parts_blend.append(new_blend)
    totals = jnp.concatenate(parts_total, axis=1)
    blended = jnp.concatenate(parts_blend, axis=1)
    safe_total = jnp.where(totals > 0, totals, 1.0)
    result = jnp.where(totals[..., None] > 0, blended / safe_total[..., None], 0.0)
    result = result.transpose(1, 0, 2).reshape(pixels, feature_width).astype(jnp.bfloat16)
    projected = lax.psum(
        jnp.dot(result, out_weight, preferred_element_type=jnp.float32).astype(jnp.bfloat16), "tp"
    ).astype(jnp.float32)
    state = hidden.reshape(pixels, model_width).astype(jnp.float32) + gate * (
        projected + mlp_term.reshape(pixels, model_width).astype(jnp.float32)
    )
    centered = state - jnp.mean(state, axis=-1, keepdims=True)
    normed = centered * lax.rsqrt(jnp.mean(centered * centered, axis=-1, keepdims=True) + 1e-06)
    modulated = (normed * (1.0 + final_scale) + final_shift).astype(jnp.bfloat16)
    velocity = jnp.dot(modulated, final_weight, preferred_element_type=jnp.float32) + final_bias
    velocity = jnp.where(patch_live[:, None], velocity, 0.0)
    latent_next = latent.reshape(pixels, latent_width) + euler_step(image_size, timestep) * velocity
    return (velocity.reshape(1, pixels, latent_width), latent_next.reshape(1, pixels, latent_width))


def solution(mesh):
    placed = (
        P(("req", "tile"), None, None, "tp"),
        P(("req", "tile"), None, "tp"),
        P(),
        P(),
        P("tp", None),
        P(("req", "tile"), None, None),
        P(("req", "tile"), None, None),
        P("req"),
        P("req"),
        P("req"),
        P(),
        P(),
        P(("req", "tile"), None, None),
        P("req"),
        P("req"),
        P("req"),
    )
    return jax.shard_map(
        shards,
        mesh=mesh,
        in_specs=placed,
        out_specs=(P(("req", "tile"), None, None), P(("req", "tile"), None, None)),
        check_vma=False,
    )
```

profile of v0, /device:TPU:1, one launch (start us, length us, event | category | flops | bytes accessed | tf_op | source)
XLA Modules:
  0.0 287.4 jit_solution(2902120326532575079)
XLA Ops:
  7.2 0.0 all-gather.3.cloned.1.call-start
  7.3 1.4 copy.81
  8.7 0.1 slice_bitcast_fusion
  8.8 1.0 multiply_reduce_fusion.1
  9.8 0.1 reshape.374
  9.9 0.6 slice_bitcast_fusion.1
  10.6 0.1 multiply_reduce_fusion.3
  10.7 0.5 copy.56
  11.2 0.5 copy.58
  11.7 0.9 copy.59
  12.7 1.0 copy.57
  13.6 0.1 mul.293
  13.8 0.1 mul.276
  13.9 0.3 copy.61
  14.2 0.1 copy.62
  14.3 0.2 multiply_multiply_fusion.2
  14.5 0.1 subtract_convert_fusion.2
  14.6 0.1 broadcast_multiply_fusion.1
  14.7 0.3 fusion.100
  15.0 0.3 multiply_multiply_fusion
  15.3 0.4 subtract_convert_fusion
  15.7 0.1 pad_maximum_fusion.1
  15.8 0.1 pad_maximum_fusion.4
  15.9 0.2 pad_maximum_fusion.2
  16.1 1.2 copy.63
  17.3 0.0 all-gather.5.cloned.1.call-start
  17.4 0.8 pad_maximum_fusion.3
  18.2 0.0 all-reduce.2.cloned.1.call-start
  18.9 0.6 fusion.136
  19.4 1.9 fusion.131
  21.3 1.2 compare_and_fusion
  22.5 0.8 slice_reduce_fusion.3
  28.0 1.2 fusion.121
  29.3 0.1 pad_maximum_fusion
  29.4 76.1 %all-gather.3.cloned.1.call-done = bf16[2816,8,128]{2,1,0:T(8,128)(2,1)} async-done(((bf16[176,8,128]{2,1,0:T(8,128)(2,1)}), bf16[2816,8,128]{2,1,0:T(8,128)(2,1)}) %all-gather.3.cloned.1.call-update) | async-done | bytes 5767184 | tf_op jit(solution)/shard_map/all_gather | solution.py:139
  105.4 91.0 %all-gather.5.cloned.1.call-done = bf16[2816,8,128]{2,1,0:T(8,128)(2,1)} async-done(((bf16[176,8,128]{2,1,0:T(8,128)(2,1)}), bf16[2816,8,128]{2,1,0:T(8,128)(2,1)}) %all-gather.5.cloned.1.call-update) | async-done | bytes 5767184 | tf_op jit(solution)/shard_map/all_gather | solution.py:140
  196.5 9.6 %conditional.4 = (f32[8,36,128]{2,1,0:T(8,128)S(1)}, f32[8,36]{1,0:T(8,128)S(1)}) conditional(s32[]{:T(128)} %convert_element_type.123, () %tuple.56, (pred[2816]{0:T(1024)(128)(4,1)S(1)}, bf16[8,144,128]{1,0,2:T(8,128)(2,1)S(1)}, bf16[2816,8,128]{2,1,0:T(8,128)(2,1)}, bf16[2816,8,128]{2,1,0:T(8,128)(2,1)}) %tuple.113), branch_computations={%region_5.6_spmd, %region_6.9_spmd} | conditional | flops 420951456 | bytes 39402944 | solution.py:89
  196.5 0.4 copy.64
  196.9 6.4 %fusion.132 = (f32[8,36]{1,0:T(8,128)S(1)}, f32[8,36,2816]{2,1,0:T(8,128)S(1)}) fusion(bf16[2816,8,128]{2,1,0:T(8,128)(2,1)} %get-tuple-element.112, bf16[8,144,128]{2,1,0:T(8,128)(2,1)S(1)} %copy.64, pred[2816]{0:T(1024)(128)(4,1)S(1)} %get-tuple-element.44), kind=kOutput, calls=%fused_computation.174 | convolution fusion | flops 210050784 | bytes 9097344 | tf_op jit(solution)/shard_map/cond/branch_1_fun/hqd,khd->hqk/dot_general | solution.py:63
  203.3 0.6 fusion.10
  204.0 2.1 fusion.14
  206.1 9.8 %conditional.5 = (f32[8,36,128]{2,1,0:T(8,128)S(1)}, f32[8,36]{1,0:T(8,128)S(1)}) conditional(s32[]{:T(128)} %convert_element_type.138, () %tuple.58, (pred[2816]{0:T(1024)(128)(4,1)S(1)}, bf16[8,144,128]{1,0,2:T(8,128)(2,1)S(1)}, bf16[2816,8,128]{2,1,0:T(8,128)(2,1)}, bf16[2816,8,128]{2,1,0:T(8,128)(2,1)}) %tuple.114), branch_computations={%region_10.11_spmd, %region_11.14_spmd} | conditional | flops 420951456 | bytes 39402944 | solution.py:89
  206.3 0.4 copy.67
  206.7 6.4 %fusion.133 = (f32[8,36]{1,0:T(8,128)S(1)}, f32[8,36,2816]{2,1,0:T(8,128)S(1)}) fusion(bf16[2816,8,128]{2,1,0:T(8,128)(2,1)} %get-tuple-element.116, bf16[8,144,128]{2,1,0:T(8,128)(2,1)S(1)} %copy.67, pred[2816]{0:T(1024)(128)(4,1)S(1)} %get-tuple-element.48), kind=kOutput, calls=%fused_computation.175 | convolution fusion | flops 210050784 | bytes 9097344 | tf_op jit(solution)/shard_map/cond/branch_1_fun/hqd,khd->hqk/dot_general | solution.py:63
  213.1 0.6 fusion.31
  213.8 2.1 fusion.35
  215.9 9.6 %conditional.6 = (f32[8,36,128]{2,1,0:T(8,128)S(1)}, f32[8,36]{1,0:T(8,128)S(1)}) conditional(s32[]{:T(128)} %convert_element_type.139, () %tuple.59, (pred[2816]{0:T(1024)(128)(4,1)S(1)}, bf16[8,144,128]{1,0,2:T(8,128)(2,1)S(1)}, bf16[2816,8,128]{2,1,0:T(8,128)(2,1)}, bf16[2816,8,128]{2,1,0:T(8,128)(2,1)}) %tuple.115), branch_computations={%region_15.16_spmd, %region_16.19_spmd} | conditional | flops 420951456 | bytes 39402944 | solution.py:89
  215.9 0.4 copy.70
  216.4 6.4 %fusion.134 = (f32[8,36]{1,0:T(8,128)S(1)}, f32[8,36,2816]{2,1,0:T(8,128)S(1)}) fusion(bf16[2816,8,128]{2,1,0:T(8,128)(2,1)} %get-tuple-element.120, bf16[8,144,128]{2,1,0:T(8,128)(2,1)S(1)} %copy.70, pred[2816]{0:T(1024)(128)(4,1)S(1)} %get-tuple-element.52), kind=kOutput, calls=%fused_computation.176 | convolution fusion | flops 210050784 | bytes 9097344 | tf_op jit(solution)/shard_map/cond/branch_1_fun/hqd,khd->hqk/dot_general | solution.py:63
  222.8 0.6 fusion.52
  223.4 2.1 fusion.56
  225.5 9.8 %conditional.7 = (f32[8,36,128]{2,1,0:T(8,128)S(1)}, f32[8,36]{1,0:T(8,128)S(1)}) conditional(s32[]{:T(128)} %convert_element_type.140, () %tuple.60, (pred[2816]{0:T(1024)(128)(4,1)S(1)}, bf16[8,144,128]{1,0,2:T(8,128)(2,1)S(1)}, bf16[2816,8,128]{2,1,0:T(8,128)(2,1)}, bf16[2816,8,128]{2,1,0:T(8,128)(2,1)}) %tuple.116), branch_computations={%region_20.21_spmd, %region_21.24_spmd} | conditional | flops 420951456 | bytes 39402944 | solution.py:89
  225.8 0.4 copy.73
  226.2 6.4 %fusion.135 = (f32[8,36]{1,0:T(8,128)S(1)}, f32[8,36,2816]{2,1,0:T(8,128)S(1)}) fusion(bf16[2816,8,128]{2,1,0:T(8,128)(2,1)} %get-tuple-element.124, bf16[8,144,128]{2,1,0:T(8,128)(2,1)S(1)} %copy.73, pred[2816]{0:T(1024)(128)(4,1)S(1)} %get-tuple-element.56), kind=kOutput, calls=%fused_computation.177 | convolution fusion | flops 210050784 | bytes 9097344 | tf_op jit(solution)/shard_map/cond/branch_1_fun/hqd,khd->hqk/dot_general | solution.py:63
  232.6 0.6 fusion.73
  233.3 2.1 fusion.77
  235.4 0.1 broadcast_compare_fusion
  235.5 0.1 broadcast_select_fusion
  235.6 5.1 %convolution_convert_fusion = bf16[144,3072]{1,0:T(8,128)(2,1)} fusion(bf16[1024,3072]{1,0:T(8,128)(2,1)} %param.28, f32[8,144]{1,0:T(8,128)S(1)} %broadcast_select_fusion, f32[8,36,128]{2,1,0:T(8,128)S(1)} %get-tuple-element.77, f32[8,36,128]{2,1,0:T(8,128)S(1)} %get-tuple-element.76, f32[8,36,128]{2,1,0:T(8,128)S(1)} %get-tuple-element.75, ...), kind=kOutput, calls=%fused_computation.60 | convolution fusion | flops 907296768 | bytes 7771776 | tf_op jit(solution)/shard_map/dot_general | solution.py:182
  242.7 33.1 %all-reduce.2.cloned.1.call-done = bf16[144,3072]{1,0:T(8,128)(2,1)} async-done(((bf16[144,3072]{1,0:T(8,128)(2,1)}), bf16[144,3072]{1,0:T(8,128)(2,1)}) %all-reduce.2.cloned.1.call-update) | async-done | bytes 884752 | tf_op jit(solution)/shard_map/psum | solution.py:181
  275.8 1.7 fusion.96
  277.6 1.8 multiply_reduce_fusion
  279.4 0.8 fusion.86
  280.2 0.6 fusion.98
  (71 shorter events, 0.3 us)
Async XLA Ops:
  7.2 272.2 %copy-start = (bf16[3072,64]{0,1:T(8,128)(2,1)S(1)}, bf16[3072,64]{0,1:T(8,128)(2,1)}, u32[]{:S(2)}) copy-start(bf16[3072,64]{0,1:T(8,128)(2,1)} %param.34) | copy-start | bytes 1179652
  7.2 2.6 copy-start.5
  7.2 98.3 %all-gather.3.cloned.1.call-start = ((), (), s32[]{:S(2)}) async-start(), calls=%async_computation | async-start | bytes 6127616 | tf_op jit(solution)/shard_map/all_gather | solution.py:139
  8.7 4.9 %copy-start.11 = (f32[128]{0:T(128)S(1)}, f32[128]{0:T(128)}, u32[]{:S(2)}) copy-start(f32[128]{0:T(128)} %param.27) | copy-start | bytes 1540
  8.7 5.1 %copy-start.12 = (f32[128]{0:T(128)S(1)}, f32[128]{0:T(128)}, u32[]{:S(2)}) copy-start(f32[128]{0:T(128)} %param.26) | copy-start | bytes 1540
  15.3 2.0 copy-start.4
  15.3 3.5 %copy-start.10 = (s32[2]{0:T(128)S(1)}, s32[2]{0:T(128)}, u32[]{:S(2)}) copy-start(s32[2]{0:T(128)} %param.37) | copy-start | bytes 28
  17.3 179.2 %all-gather.5.cloned.1.call-start = ((), (), s32[]{:S(2)}) async-start(), calls=%async_computation.1 | async-start | bytes 6127616 | tf_op jit(solution)/shard_map/all_gather | solution.py:140
  18.2 257.7 %all-reduce.2.cloned.1.call-start = ((), (), s32[]{:S(2)}) async-start(), calls=%async_computation.2 | async-start | bytes 1769472 | tf_op jit(solution)/shard_map/psum | solution.py:181
  196.9 7.1 %slice-start = ((s8[5767168]{0:T(1024)(128)(4,1)}), s8[4194304]{0:T(1024)(128)(4,1)S(1)}, s32[]{:S(2)}) async-start(s8[5767168]{0:T(1024)(128)(4,1)} %bitcast.71), calls=%async_computation.3 | async-start | bytes 8388608 | tf_op jit(solution)/shard_map/cond
  196.9 7.1 %slice-start.1 = ((s8[5767168]{0:T(1024)(128)(4,1)}), s8[1572864]{0:T(1024)(128)(4,1)S(1)}, s32[]{:S(2)}) async-start(s8[5767168]{0:T(1024)(128)(4,1)} %bitcast.71), calls=%async_computation.4 | async-start | bytes 3145728 | tf_op jit(solution)/shard_map/cond
  206.7 7.1 %slice-start.2 = ((s8[5767168]{0:T(1024)(128)(4,1)}), s8[4194304]{0:T(1024)(128)(4,1)S(1)}, s32[]{:S(2)}) async-start(s8[5767168]{0:T(1024)(128)(4,1)} %bitcast.73), calls=%async_computation.5 | async-start | bytes 8388608 | tf_op jit(solution)/shard_map/cond
  206.7 7.1 %slice-start.3 = ((s8[5767168]{0:T(1024)(128)(4,1)}), s8[1572864]{0:T(1024)(128)(4,1)S(1)}, s32[]{:S(2)}) async-start(s8[5767168]{0:T(1024)(128)(4,1)} %bitcast.73), calls=%async_computation.6 | async-start | bytes 3145728 | tf_op jit(solution)/shard_map/cond
  216.3 7.1 %slice-start.4 = ((s8[5767168]{0:T(1024)(128)(4,1)}), s8[4194304]{0:T(1024)(128)(4,1)S(1)}, s32[]{:S(2)}) async-start(s8[5767168]{0:T(1024)(128)(4,1)} %bitcast.75), calls=%async_computation.7 | async-start | bytes 8388608 | tf_op jit(solution)/shard_map/cond
  216.3 7.1 %slice-start.5 = ((s8[5767168]{0:T(1024)(128)(4,1)}), s8[1572864]{0:T(1024)(128)(4,1)S(1)}, s32[]{:S(2)}) async-start(s8[5767168]{0:T(1024)(128)(4,1)} %bitcast.75), calls=%async_computation.8 | async-start | bytes 3145728 | tf_op jit(solution)/shard_map/cond
  226.2 7.1 %slice-start.6 = ((s8[5767168]{0:T(1024)(128)(4,1)}), s8[4194304]{0:T(1024)(128)(4,1)S(1)}, s32[]{:S(2)}) async-start(s8[5767168]{0:T(1024)(128)(4,1)} %bitcast.77), calls=%async_computation.9 | async-start | bytes 8388608 | tf_op jit(solution)/shard_map/cond
  226.2 7.1 %slice-start.7 = ((s8[5767168]{0:T(1024)(128)(4,1)}), s8[1572864]{0:T(1024)(128)(4,1)S(1)}, s32[]{:S(2)}) async-start(s8[5767168]{0:T(1024)(128)(4,1)} %bitcast.77), calls=%async_computation.10 | async-start | bytes 3145728 | tf_op jit(solution)/shard_map/cond
  235.5 7.2 %copy-start.9 = (f32[3072]{0:T(1024)S(1)}, f32[3072]{0:T(1024)}, u32[]{:S(2)}) copy-start(f32[3072]{0:T(1024)} %param.33) | copy-start | bytes 36868
  235.5 40.3 %copy-start.1 = (bf16[1,144,3072]{2,1,0:T(8,128)(2,1)S(1)}, bf16[1,144,3072]{2,1,0:T(8,128)(2,1)}, u32[]{:S(2)}) copy-start(bf16[1,144,3072]{2,1,0:T(8,128)(2,1)} %param.30) | copy-start | bytes 2654212
  235.5 40.3 %copy-start.2 = (bf16[1,144,3072]{2,1,0:T(8,128)(2,1)S(1)}, bf16[1,144,3072]{2,1,0:T(8,128)(2,1)}, u32[]{:S(2)}) copy-start(bf16[1,144,3072]{2,1,0:T(8,128)(2,1)} %param.29) | copy-start | bytes 2654212
  235.6 40.3 %copy-start.8 = (f32[3072]{0:T(1024)S(1)}, f32[3072]{0:T(1024)}, u32[]{:S(2)}) copy-start(f32[3072]{0:T(1024)} %param.31) | copy-start | bytes 36868
  240.7 38.7 %copy-start.13 = (f32[3072]{0:T(1024)S(1)}, f32[3072]{0:T(1024)}, u32[]{:S(2)}) copy-start(f32[3072]{0:T(1024)} %param.32) | copy-start | bytes 36868
  240.7 38.7 %copy-start.14 = (f32[64]{0:T(128)S(1)}, f32[64]{0:T(128)}, u32[]{:S(2)}) copy-start(f32[64]{0:T(128)} %param.35) | copy-start | bytes 772
  275.8 3.6 %copy-start.3 = (bf16[144,3072]{1,0:T(8,128)(2,1)S(1)}, bf16[144,3072]{1,0:T(8,128)(2,1)}, u32[]{:S(2)}) copy-start(bf16[144,3072]{1,0:T(8,128)(2,1)} %all-reduce.2.cloned.1.call-done) | copy-start | bytes 2654212
  277.6 2.6 copy-start.6
  280.2 0.7 copy-start.7
Sparse Core Ops, SparseCore 0:
  17.4 87.9 all-gather.2
  107.2 89.2 all-gather.4
  240.8 34.9 all-reduce.1
where the time goes:
time: 288 us; the launch traced here: 287 us
  waiting for transfers between devices  200 us (69%)
  matrix products  39.8 us (14%)
  between operations  21.5 us (7%)
  other arithmetic  16.5 us (6%)
  local copies, waits for them, and re-layouts  8.54 us (3%)
    all_gather x1, waiting for transfers between devices, shards(): piece_values = lax.all_gather(block_values, 'tile', axis=0, tiled=True)  91 us
    all_gather x1, waiting for transfers between devices, shards(): piece_keys = lax.all_gather(block_keys, 'tile', axis=0, tiled=True)  76.1 us
    psum x1, waiting for transfers between devices, shards(): lax.psum(jnp.dot(result, out_weight, preferred_element_type=jnp.float32)....  33.1 us
    dot_general x4, matrix products, attend_block(): jnp.einsum('hqd,khd->hqk', query_block, piece_keys, preferred_element_typ...  25.6 us
    dot_general x4, matrix products, attend_block(): jnp.einsum('hqk,khd->hqd', weights.astype(jnp.bfloat16), piece_values, pr...  8.29 us
  transfers between devices with their start and end apart: 3, of which 3 were waited for; matrix products, arithmetic and copies ran while one was open for 2% of the time, Pallas kernels for 0%

commit v1 on v0

v1 whole, which is shorter than its diff:
```python
import math

import jax
import jax.numpy as jnp
import numpy as np
from jax import lax
from jax.experimental import pallas as pl
from jax.experimental.pallas import tpu as pltpu
from jax.sharding import PartitionSpec as P

HEAD = 128
STEPS = 28
CANVAS = 48
TILES = 16
GRID_X = 4
TILE_H = 12
TILE_W = 12
PIX = TILE_H * TILE_W
SLOTS = 32
KEYS = PIX + SLOTS
GROUP = 8
HALF_KEYS = GROUP * KEYS
DEAD = -1e30
EXP_SCALE = HEAD ** (-0.5) * math.log2(math.e)
VMEM_LIMIT = 48 * 1024 * 1024


def position_tables():
    tile = np.arange(TILES)[:, None]
    local = np.arange(PIX)[None, :]
    row = tile // GRID_X * TILE_H + local // TILE_W
    col = tile % GRID_X * TILE_W + local % TILE_W
    return row, col


def rope_tables():
    row, col = position_tables()
    side_dims = (HEAD - HEAD // 8) // 2
    side_index = np.arange(side_dims // 2, dtype=np.float32)
    frequency = np.power(np.float32(10000.0), np.float32(-2.0) * side_index / np.float32(side_dims)).astype(np.float32)
    still = np.zeros(row.shape + (HEAD // 16,), np.float32)
    angles = np.concatenate(
        [
            still,
            row[..., None].astype(np.float32) * frequency,
            col[..., None].astype(np.float32) * frequency,
        ],
        axis=-1,
    ).astype(np.float64)
    cosine = np.repeat(np.cos(angles), 2, axis=-1)
    sine = np.repeat(np.sin(angles), 2, axis=-1)
    sine[..., 0::2] *= -1.0
    return cosine.astype(np.float32), sine.astype(np.float32)


def key_tables():
    row, col = position_tables()
    row = row[:GROUP]
    col = col[:GROUP]
    far = np.full((GROUP, SLOTS), 1 << 20)
    slot = np.arange(GROUP * SLOTS).reshape(GROUP, SLOTS)
    key_row = np.concatenate([row, far], axis=1).reshape(1, HALF_KEYS)
    key_col = np.concatenate([col, far], axis=1).reshape(1, HALF_KEYS)
    key_slot = np.concatenate([np.full((GROUP, PIX), 1 << 20), slot], axis=1).reshape(1, HALF_KEYS)
    return np.concatenate([key_row, key_col, key_slot], axis=0).astype(np.int32)


def value_kernel(image_ref, text_ref, out_ref):
    for head in range(GROUP):
        lanes = slice(head * HEAD, (head + 1) * HEAD)
        out_ref[head, 0:PIX, :] = image_ref[0, :, lanes]
        out_ref[head, PIX:KEYS, :] = text_ref[0, :, lanes]


def normed(vectors, gain):
    wide = vectors.astype(jnp.float32)
    return wide * lax.rsqrt(jnp.mean(wide * wide, axis=-1, keepdims=True) + 1e-06) * gain


def query_key_kernel(tile_ref, query_ref, key_ref, text_ref, q_gain_ref, k_gain_ref, cos_ref, sin_ref, out_ref):
    cosine = cos_ref[0]
    sine = sin_ref[0]
    even = lax.broadcasted_iota(jnp.int32, (PIX, HEAD), 1) % 2 == 0

    def rotated(vectors, gain):
        scaled = normed(vectors, gain)
        swapped = jnp.where(even, pltpu.roll(scaled, HEAD - 1, 1), pltpu.roll(scaled, 1, 1))
        return (scaled * cosine + swapped * sine).astype(jnp.bfloat16)

    for head in range(GROUP):
        lanes = slice(head * HEAD, (head + 1) * HEAD)
        out_ref[head, 0:PIX, :] = rotated(query_ref[0, :, lanes], q_gain_ref[...])
        out_ref[head, PIX : 2 * PIX, :] = rotated(key_ref[0, :, lanes], k_gain_ref[...])
        out_ref[head, 2 * PIX :, :] = normed(text_ref[0, :, lanes], k_gain_ref[...]).astype(jnp.bfloat16)


def key_bias(table_ref, size_ref, text_len_ref, half):
    rows = size_ref[0] - half * (CANVAS // 2)
    slots = text_len_ref[0] - half * (GROUP * SLOTS)
    image_ok = (table_ref[0:1, :] < rows) & (table_ref[1:2, :] < size_ref[1])
    text_ok = table_ref[2:3, :] < slots
    return jnp.where(image_ok | text_ok, 0.0, DEAD)


def scores_of(queries, keys, bias):
    scores = lax.dot_general(queries, keys, (((1,), (1,)), ((), ())), preferred_element_type=jnp.float32)
    return scores + bias


def local_kernel(half_ref, size_ref, text_len_ref, table_ref, qk_ref, values_ref, acc_ref, peak_ref, key_s, value_s):
    bias = key_bias(table_ref, size_ref, text_len_ref, half_ref[0])
    for tile in range(GROUP):
        key_s[tile * KEYS : (tile + 1) * KEYS, :] = qk_ref[tile, PIX:, :]
        value_s[tile * KEYS : (tile + 1) * KEYS, 0:HEAD] = values_ref[tile, 0:KEYS, :]
    value_s[:, HEAD:] = jnp.ones((HALF_KEYS, HEAD), jnp.bfloat16)
    for tile in range(GROUP):
        scores = scores_of(qk_ref[tile, 0:PIX, :], key_s[...], bias)
        peak = jnp.max(scores, axis=1, keepdims=True)
        weights = jnp.exp2((scores - peak) * EXP_SCALE).astype(jnp.bfloat16)
        acc_ref[tile] = jnp.dot(weights, value_s[...], preferred_element_type=jnp.float32)
        peak_ref[tile] = jnp.broadcast_to(peak, (PIX, HEAD))


def remote_kernel(
    half_ref, size_ref, text_len_ref, table_ref, qk_ref, keys_ref, values_ref, acc_ref, peak_ref, out_ref, key_s, value_s
):
    bias = key_bias(table_ref, size_ref, text_len_ref, 1 - half_ref[0])
    for tile in range(GROUP):
        key_s[tile * KEYS : (tile + 1) * KEYS, :] = keys_ref[tile]
        value_s[tile * KEYS : (tile + 1) * KEYS, 0:HEAD] = values_ref[tile, KEYS:, :]
    value_s[:, HEAD:] = jnp.ones((HALF_KEYS, HEAD), jnp.bfloat16)
    for tile in range(GROUP):
        scores = scores_of(qk_ref[tile, 0:PIX, :], key_s[...], bias)
        before = peak_ref[tile]
        peak = jnp.maximum(before[:, 0:1], jnp.max(scores, axis=1, keepdims=True))
        weights = jnp.exp2((scores - peak) * EXP_SCALE).astype(jnp.bfloat16)
        factor = jnp.exp2((before - peak) * EXP_SCALE)
        added = jnp.dot(weights, value_s[...], preferred_element_type=jnp.float32)
        blended = acc_ref[tile, :, 0:HEAD] * factor + added[:, 0:HEAD]
        total = acc_ref[tile, :, HEAD:] * factor + added[:, HEAD:]
        out_ref[tile] = (blended / total).astype(jnp.bfloat16)


def project_kernel(attended_ref, weight_ref, out_ref):
    attended = jnp.concatenate([attended_ref[head] for head in range(GROUP)], axis=1)
    out_ref[...] = jnp.dot(attended, weight_ref[...], preferred_element_type=jnp.float32).astype(jnp.bfloat16)


def final_kernel(
    tile_ref,
    size_ref,
    timestep_ref,
    local_ref,
    own_ref,
    other_ref,
    hidden_ref,
    mlp_ref,
    gate_ref,
    shift_ref,
    scale_ref,
    weight_ref,
    bias_ref,
    latent_ref,
    velocity_ref,
    next_ref,
    modulated_s,
):
    rows = 16
    for start in range(0, PIX, rows):
        block = slice(start, start + rows)
        projected = own_ref[block, :].astype(jnp.float32) + other_ref[block, :].astype(jnp.float32)
        state = hidden_ref[block, :].astype(jnp.float32) + gate_ref[...] * (
            projected + mlp_ref[block, :].astype(jnp.float32)
        )
        centered = state - jnp.mean(state, axis=-1, keepdims=True)
        scaled = centered * lax.rsqrt(jnp.mean(centered * centered, axis=-1, keepdims=True) + 1e-06)
        modulated_s[block, :] = (scaled * (1.0 + scale_ref[...]) + shift_ref[...]).astype(jnp.bfloat16)
    latents = weight_ref.shape[0]
    diagonal = lax.broadcasted_iota(jnp.int32, (latents, latents), 0) == lax.broadcasted_iota(
        jnp.int32, (latents, latents), 1
    )
    bias = jnp.sum(jnp.where(diagonal, bias_ref[...], 0.0), axis=1, keepdims=True)
    velocity = (
        lax.dot_general(
            weight_ref[...], modulated_s[...], (((1,), (1,)), ((), ())), preferred_element_type=jnp.float32
        )
        + bias
    )
    tile = tile_ref[0]
    tile_row = tile // GRID_X
    tile_col = tile - tile_row * GRID_X
    live = (local_ref[0:1, :] < size_ref[0] - tile_row * TILE_H) & (local_ref[1:2, :] < size_ref[1] - tile_col * TILE_W)
    velocity = jnp.where(live, velocity, 0.0)
    area = jnp.full((1, PIX), size_ref[0] * size_ref[1], jnp.int32).astype(jnp.float32)
    moment = jnp.full((1, PIX), timestep_ref[0], jnp.int32).astype(jnp.float32)
    shift_factor = jnp.exp(0.5 + 0.65 * (area - 256.0) / 3840.0)
    now_time = 1.0 - moment / STEPS
    next_time = 1.0 - (moment + 1.0) / STEPS

    def sigma_of(at):
        return shift_factor * at / (shift_factor * at + 1.0 - at)

    step = sigma_of(next_time) - sigma_of(now_time)
    velocity_ref[...] = velocity
    next_ref[...] = latent_ref[...] + step * velocity


def whole(shape, index=None):
    at = index if index is not None else (0,) * len(shape)
    return pl.BlockSpec(shape, lambda *_: at)


SMEM = pl.BlockSpec(memory_space=pltpu.SMEM)


def params():
    return pltpu.CompilerParams(vmem_limit_bytes=VMEM_LIMIT)


def shards(
    image_qkv,
    text_kv,
    q_gain,
    k_gain,
    out_weight,
    hidden,
    mlp_term,
    gate,
    final_shift,
    final_scale,
    final_weight,
    final_bias,
    latent,
    image_size,
    text_len,
    timestep,
):
    bf16 = jnp.bfloat16
    width = GROUP * HEAD
    model = hidden.shape[2]
    latents = final_weight.shape[1]
    tile = lax.axis_index("tile").astype(jnp.int32).reshape(1)
    half = tile // GROUP
    triple = image_qkv.reshape(PIX, 3, width).transpose(1, 0, 2)
    text = text_kv.transpose(1, 0, 2)
    groups = [list(range(GROUP)), list(range(GROUP, 2 * GROUP))]
    across = [(t, (t + GROUP) % TILES) for t in range(TILES)]

    values = pl.pallas_call(
        value_kernel,
        grid=(1,),
        in_specs=[whole((1, PIX, width), (2, 0, 0)), whole((1, SLOTS, width), (1, 0, 0))],
        out_specs=whole((GROUP, KEYS, HEAD)),
        out_shape=jax.ShapeDtypeStruct((GROUP, KEYS, HEAD), bf16),
        name="value_layout",
    )(triple, text)
    far_values = lax.ppermute(values, "tile", across)

    cosine, sine = rope_tables()
    spot = pl.BlockSpec((1, PIX, HEAD), lambda i, tile_ref: (tile_ref[0], 0, 0))
    query_key = pl.pallas_call(
        query_key_kernel,
        grid_spec=pltpu.PrefetchScalarGridSpec(
            num_scalar_prefetch=1,
            grid=(1,),
            in_specs=[
                whole((1, PIX, width), (0, 0, 0)),
                whole((1, PIX, width), (1, 0, 0)),
                whole((1, SLOTS, width), (0, 0, 0)),
                whole((1, HEAD)),
                whole((1, HEAD)),
                spot,
                spot,
            ],
            out_specs=whole((GROUP, PIX + KEYS, HEAD)),
        ),
        out_shape=jax.ShapeDtypeStruct((GROUP, PIX + KEYS, HEAD), bf16),
        name="query_key_norm",
    )(tile, triple, triple, text, q_gain.reshape(1, HEAD), k_gain.reshape(1, HEAD), jnp.asarray(cosine), jnp.asarray(sine))
    query_key = lax.all_to_all(query_key, "tile", 0, 0, axis_index_groups=groups, tiled=True)
    far_keys = lax.ppermute(query_key[:, PIX:, :], "tile", across)
    value_pair = lax.all_to_all(
        jnp.concatenate([values, far_values], axis=1), "tile", 0, 0, axis_index_groups=groups, tiled=True
    )

    table = jnp.asarray(key_tables())
    acc, peak = pl.pallas_call(
        local_kernel,
        in_specs=[SMEM, SMEM, SMEM] + [pl.BlockSpec(memory_space=pltpu.VMEM)] * 3,
        out_specs=(pl.BlockSpec(memory_space=pltpu.VMEM),) * 2,
        out_shape=(
            jax.ShapeDtypeStruct((GROUP, PIX, 2 * HEAD), jnp.float32),
            jax.ShapeDtypeStruct((GROUP, PIX, HEAD), jnp.float32),
        ),
        scratch_shapes=[pltpu.VMEM((HALF_KEYS, HEAD), bf16), pltpu.VMEM((HALF_KEYS, 2 * HEAD), bf16)],
        compiler_params=params(),
        name="attend_local",
    )(half, image_size, text_len, table, query_key, value_pair)
    attended = pl.pallas_call(
        remote_kernel,
        in_specs=[SMEM, SMEM, SMEM] + [pl.BlockSpec(memory_space=pltpu.VMEM)] * 6,
        out_specs=pl.BlockSpec(memory_space=pltpu.VMEM),
        out_shape=jax.ShapeDtypeStruct((GROUP, PIX, HEAD), bf16),
        scratch_shapes=[pltpu.VMEM((HALF_KEYS, HEAD), bf16), pltpu.VMEM((HALF_KEYS, 2 * HEAD), bf16)],
        compiler_params=params(),
        name="attend_far",
    )(half, image_size, text_len, table, query_key, far_keys, value_pair, acc, peak)
    attended = lax.all_to_all(attended, "tile", 0, 0, axis_index_groups=groups, tiled=True)

    columns = 768
    own = pl.pallas_call(
        project_kernel,
        grid=(model // columns,),
        in_specs=[whole((GROUP, PIX, HEAD)), pl.BlockSpec((width, columns), lambda i: (0, i))],
        out_specs=pl.BlockSpec((PIX, columns), lambda i: (0, i)),
        out_shape=jax.ShapeDtypeStruct((PIX, model), bf16),
        compiler_params=params(),
        name="project",
    )(attended, out_weight)
    other = lax.ppermute(own, "tp", [(0, 1), (1, 0)])

    local = np.stack([np.arange(PIX) // TILE_W, np.arange(PIX) % TILE_W]).astype(np.int32)
    velocity, latent_next = pl.pallas_call(
        final_kernel,
        in_specs=[SMEM, SMEM, SMEM] + [pl.BlockSpec(memory_space=pltpu.VMEM)] * 11,
        out_specs=(pl.BlockSpec(memory_space=pltpu.VMEM),) * 2,
        out_shape=(jax.ShapeDtypeStruct((latents, PIX), jnp.float32),) * 2,
        scratch_shapes=[pltpu.VMEM((PIX, model), bf16)],
        compiler_params=params(),
        name="final_layer",
    )(
        tile,
        image_size,
        timestep,
        jnp.asarray(local),
        own,
        other,
        hidden.reshape(PIX, model),
        mlp_term.reshape(PIX, model),
        gate.reshape(1, model),
        final_shift.reshape(1, model),
        final_scale.reshape(1, model),
        final_weight.T,
        final_bias.reshape(1, latents),
        latent.reshape(PIX, latents).T,
    )
    return (velocity.T.reshape(1, PIX, latents), latent_next.T.reshape(1, PIX, latents))


def solution(mesh):
    placed = (
        P(("req", "tile"), None, None, "tp"),
        P(("req", "tile"), None, "tp"),
        P(),
        P(),
        P("tp", None),
        P(("req", "tile"), None, None),
        P(("req", "tile"), None, None),
        P("req"),
        P("req"),
        P("req"),
        P(),
        P(),
        P(("req", "tile"), None, None),
        P("req"),
        P("req"),
        P("req"),
    )
    return jax.shard_map(
        shards,
        mesh=mesh,
        in_specs=placed,
        out_specs=(P(("req", "tile"), None, None), P(("req", "tile"), None, None)),
        check_vma=False,
    )
```

time: 288 us -> 86.7 us (0.30)
  waiting for transfers between devices: 200 us -> 29.9 us
  matrix products: 39.8 us -> 0 us
  starting transfers between devices: 0.12 us -> 20.6 us
  Pallas kernels: 0 us -> 19.7 us
  between operations: 21.5 us -> 2.07 us
  other arithmetic: 16.5 us -> 1.92 us
  blocking collectives: 0 us -> 10.3 us
  local copies, waits for them, and re-layouts: 8.54 us -> 1.66 us
    all_gather x2 -> x0, waiting for transfers between devices: 167 us -> none  [the longest x1 91 us: shards(): piece_values = lax.all_gather(block_values, 'tile', axis=0, tiled=True)]
    dot_general x10 -> x0, matrix products: 39.8 us -> none  [the longest x4 25.6 us: attend_block(): jnp.einsum('hqd,khd->hqk', query_block, piece_keys, preferred_element_typ...]
    psum x1 -> x0, waiting for transfers between devices: 33.1 us -> none  [shards(): lax.psum(jnp.dot(result, out_weight, preferred_element_type=jnp.float32)....]
    pallas_call x0 -> x6, Pallas kernels: none -> 19.7 us  [the longest x1 4.41 us: shards(): pl.pallas_call(project_kernel, grid=(model // columns,), in_specs=[whole(...]
    ppermute x0 -> x3, waiting for transfers between devices: none -> 17.2 us  [the longest x1 15.8 us: shards(): far_values = lax.ppermute(values, 'tile', across)]
    all_to_all x0 -> x2, waiting for transfers between devices: none -> 12.7 us  [the longest x1 12.7 us: shards(): lax.all_to_all(jnp.concatenate([values, far_values], axis=1), 'tile', 0,...]
    all_to_all x0 -> x2, starting transfers between devices: none -> 10.8 us  [the longest x1 6.37 us: shards(): lax.all_to_all(query_key, 'tile', 0, 0, axis_index_groups=groups, tiled=T...]
    all_to_all x0 -> x1, blocking collectives: none -> 10.3 us  [shards(): lax.all_to_all(attended, 'tile', 0, 0, axis_index_groups=groups, tiled=True)]
  transfers between devices with their start and end apart: 3 -> 5, of which waited for: 3 -> 3; matrix products, arithmetic and copies ran while one was open for 2% -> 2% of each run, Pallas kernels for 0% -> 6%
where the time goes in v1:
time: 86.7 us; the launch traced here: 86.3 us
  waiting for transfers between devices  29.9 us (34%)
  starting transfers between devices  20.6 us (24%)
  Pallas kernels  19.7 us (23%)
  blocking collectives  10.3 us (12%)
  between operations  2.07 us (2%)
  other arithmetic  1.92 us (2%)
  local copies, waits for them, and re-layouts  1.66 us (2%)
    ppermute x1, waiting for transfers between devices, shards(): far_values = lax.ppermute(values, 'tile', across)  15.8 us
    all_to_all x1, waiting for transfers between devices, shards(): lax.all_to_all(jnp.concatenate([values, far_values], axis=1), 'tile', 0,...  12.7 us
    all_to_all x1, blocking collectives, shards(): lax.all_to_all(attended, 'tile', 0, 0, axis_index_groups=groups, tiled=True)  10.3 us
    all_to_all x1, starting transfers between devices, shards(): lax.all_to_all(query_key, 'tile', 0, 0, axis_index_groups=groups, tiled=T...  6.37 us
    pallas_call x1, Pallas kernels, shards(): pl.pallas_call(project_kernel, grid=(model // columns,), in_specs=[whole(...  4.41 us
    all_to_all x1, starting transfers between devices, shards(): lax.all_to_all(jnp.concatenate([values, far_values], axis=1), 'tile', 0,...  4.4 us
    pallas_call x1, Pallas kernels, shards(): pl.pallas_call(query_key_kernel, grid_spec=pltpu.PrefetchScalarGridSpec(n...  4.32 us
    ppermute x1, starting transfers between devices, shards(): other = lax.ppermute(own, 'tp', [(0, 1), (1, 0)])  3.8 us
  transfers between devices with their start and end apart: 5, of which 3 were waited for; matrix products, arithmetic and copies ran while one was open for 2% of the time, Pallas kernels for 6%

profile of v1, /device:TPU:1, one launch (start us, length us, event | category | flops | bytes accessed | tf_op | source)
XLA Modules:
  0.0 86.3 jit_solution(5035439657192746380)
XLA Ops:
  0.6 1.6 %copy.24 = bf16[32,2,1024]{2,0,1:T(8,128)(2,1)} copy(bf16[32,2,1024]{2,1,0:T(2,128)(2,1)} %param.21) | data formatting | bytes 262144 | tf_op args[1]
  2.2 4.3 %query_key_norm.1 = bf16[8,320,128]{2,1,0:T(8,128)(2,1)} custom-call(s32[1]{0:T(128)} %bitcast.tile_ref, bf16[3,144,1024]{2,1,0:T(8,128)(2,1)} %bitcast.33, bf16[3,144,1024]{2,1,0:T(8,128)(2,1)} %bitcast.34, bf16[2,32,1024]{2,1,0:T(8,128)(2,1)} %bitcast.36, f32[1,128]{1,0:T(1,128)} %bitcast.38, f32[1,128]{1,0:T(1,128)} %bitcast.39, ...), custom_call_target="tpu_custom_call" | custom-call | tf_op jit(solution)/shard_map/query_key_norm/pallas_call | solution.py:261
  6.5 6.4 %all-to-all-start = ((bf16[8,320,128]{2,1,0:T(8,128)(2,1)}), bf16[8,320,128]{2,1,0:T(8,128)(2,1)S(1)}, u32[]{:S(2)}, u32[]{:S(2)}) async-start(bf16[8,320,128]{2,1,0:T(8,128)(2,1)} %query_key_norm.1), calls=%async_computation | async-start | bytes 1310720 | tf_op jit(solution)/shard_map/all_to_all | solution.py:280
  12.9 1.8 %value_layout.1 = bf16[8,176,128]{2,1,0:T(8,128)(2,1)} custom-call(bf16[3,144,1024]{2,1,0:T(8,128)(2,1)} %bitcast.35, bf16[2,32,1024]{2,1,0:T(8,128)(2,1)} %bitcast.37), custom_call_target="tpu_custom_call" | custom-call | tf_op jit(solution)/shard_map/value_layout/pallas_call | solution.py:249
  14.7 3.0 %collective-permute-start.1 = (bf16[8,176,128]{2,1,0:T(8,128)(2,1)}, bf16[8,176,128]{2,1,0:T(8,128)(2,1)S(1)}, u32[]{:S(2)}, u32[]{:S(2)}) collective-permute-start(bf16[8,176,128]{2,1,0:T(8,128)(2,1)} %value_layout.1), channel_id=1, source_target_pairs={{0,16},{2,18},{4,20},{6,22},{8,24},{10,26},{12,28},{14,30},{16,0},... | collective-permute-start | bytes 1081352 | tf_op jit(solution)/shard_map/ppermute | solution.py:257
  17.7 15.8 %collective-permute-done.1 = bf16[8,176,128]{2,1,0:T(8,128)(2,1)S(1)} collective-permute-done((bf16[8,176,128]{2,1,0:T(8,128)(2,1)}, bf16[8,176,128]{2,1,0:T(8,128)(2,1)S(1)}, u32[]{:S(2)}, u32[]{:S(2)}) %collective-permute-start.1) | collective-permute-done | bytes 360480 | tf_op jit(solution)/shard_map/ppermute | solution.py:257
  33.5 1.9 %pad_maximum_fusion = bf16[8,352,128]{2,1,0:T(8,128)(2,1)} fusion(bf16[8,176,128]{2,1,0:T(8,128)(2,1)S(1)} %collective-permute-done.1, bf16[8,176,128]{2,1,0:T(8,128)(2,1)} %value_layout.1), kind=kLoop, calls=%fused_computation | loop fusion | flops 1441792 | bytes 1441792 | tf_op jit(solution)/shard_map/concatenate | solution.py:283
  35.4 0.0 copy-start.3
  35.4 0.0 copy-start.8
  35.4 0.0 all-to-all-done.qk_ref
  35.4 4.4 %all-to-all-start.1 = ((bf16[8,352,128]{2,1,0:T(8,128)(2,1)}), bf16[8,352,128]{2,1,0:T(8,128)(2,1)S(1)}, u32[]{:S(2)}, u32[]{:S(2)}) async-start(bf16[8,352,128]{2,1,0:T(8,128)(2,1)} %pad_maximum_fusion), calls=%async_computation.1 | async-start | bytes 1441792 | tf_op jit(solution)/shard_map/all_to_all | solution.py:282
  39.9 3.1 %collective-permute-start = (bf16[8,176,128]{2,1,0:T(8,128)(2,1)S(1)}, bf16[8,176,128]{2,1,0:T(8,128)(2,1)S(1)}, u32[]{:S(2)}, u32[]{:S(2)}) collective-permute-start(bf16[8,176,128]{2,1,0:T(8,128)(2,1)S(1)} %slice.4), channel_id=1, source_target_pairs={{0,16},{2,18},{4,20},{6,22},{8,24},{10,26},{12,28},{14,30},{16,0},... | collective-permute-start | bytes 1081352 | tf_op jit(solution)/shard_map/ppermute | solution.py:281
  43.6 12.7 %all-to-all-done.1.values_ref = bf16[8,352,128]{2,1,0:T(8,128)(2,1)S(1)} async-done(((bf16[8,352,128]{2,1,0:T(8,128)(2,1)}), bf16[8,352,128]{2,1,0:T(8,128)(2,1)S(1)}, u32[]{:S(2)}, u32[]{:S(2)}) %all-to-all-start.1) | async-done | bytes 720928 | tf_op jit(solution)/shard_map/all_to_all | solution.py:282
  56.3 0.0 copy-done.3
  56.3 0.0 copy-done.8
  56.3 3.4 %attend_local.1 = (f32[8,144,256]{2,1,0:T(8,128)S(1)}, f32[8,144,128]{2,1,0:T(8,128)S(1)}) custom-call(s32[1]{0:T(128)S(6)} %select_n.5.half_ref, s32[2]{0:T(128)S(1)} %copy-done.8, s32[1]{0:T(128)S(6)} %copy.25.text_len_ref, s32[3,1408]{1,0:T(4,128)S(1)} %copy-done.3, bf16[8,320,128]{2,1,0:T(8,128)(2,1)S(1)} %all-to-all-done.qk_ref, ...), custom_call_target="tpu_custom_call" | custom-call | tf_op jit(solution)/shard_map/attend_local/pallas_call | solution.py:287
  59.7 0.0 collective-permute-done.keys_ref
  59.7 3.4 %attend_far.1 = bf16[8,144,128]{2,1,0:T(8,128)(2,1)S(1)} custom-call(s32[1]{0:T(128)S(6)} %select_n.5.half_ref, s32[2]{0:T(128)S(1)} %copy-done.8, s32[1]{0:T(128)S(6)} %copy.25.text_len_ref, s32[3,1408]{1,0:T(4,128)S(1)} %copy-done.3, bf16[8,320,128]{2,1,0:T(8,128)(2,1)S(1)} %all-to-all-done.qk_ref, bf16[8,176,128]{2,1,0:T(8,128)(2,1)S(1)} %collective-permute-done.keys_ref, ...), custom_call_target="tpu_custom_call" | custom-call | tf_op jit(solution)/shard_map/attend_far/pallas_call | solution.py:299
  63.1 10.3 %all_to_all.15.attended_ref = bf16[8,144,128]{2,1,0:T(8,128)(2,1)S(1)} all-to-all(bf16[8,144,128]{2,1,0:T(8,128)(2,1)S(1)} %attend_far.1), channel_id=1, replica_groups={{0,2,4,6,8,10,12,14},{16,18,20,22,24,26,28,30},{1,3,5,7,9,11,13,15},{17..., dimensions={0} | all-to-all | bytes 589824 | tf_op jit(solution)/shard_map/all_to_all | solution.py:308
  73.4 0.0 copy-start
  73.4 0.0 copy-start.1
  73.4 0.0 copy-start.2
  73.4 0.0 copy-start.4
  73.4 0.0 copy-start.5
  73.4 0.0 copy-start.6
  73.5 0.0 copy-start.7
  73.5 0.0 copy-start.9
  73.5 0.0 copy-start.10
  73.5 4.4 %project.1.own_ref = bf16[144,3072]{1,0:T(8,128)(2,1)S(1)} custom-call(bf16[8,144,128]{2,1,0:T(8,128)(2,1)S(1)} %all_to_all.15.attended_ref, bf16[1024,3072]{1,0:T(8,128)(2,1)} %weight_ref.1), custom_call_target="tpu_custom_call" | custom-call | tf_op jit(solution)/shard_map/project/pallas_call | solution.py:311
  77.9 3.8 %collective-permute-start.2 = (bf16[144,3072]{1,0:T(8,128)(2,1)S(1)}, bf16[144,3072]{1,0:T(8,128)(2,1)S(1)}, u32[]{:S(2)}, u32[]{:S(2)}) collective-permute-start(bf16[144,3072]{1,0:T(8,128)(2,1)S(1)} %project.1.own_ref), channel_id=1, source_target_pairs={{0,1},{1,0},{2,3},{3,2},{4,5},{5,4},{6,7},{7,6},{8,9},{9,8},{10,11... | collective-permute-start | bytes 2654216 | tf_op jit(solution)/shard_map/ppermute | solution.py:320
  82.4 1.4 %collective-permute-done.2.other_ref = bf16[144,3072]{1,0:T(8,128)(2,1)S(1)} collective-permute-done((bf16[144,3072]{1,0:T(8,128)(2,1)S(1)}, bf16[144,3072]{1,0:T(8,128)(2,1)S(1)}, u32[]{:S(2)}, u32[]{:S(2)}) %collective-permute-start.2) | collective-permute-done | bytes 884768 | tf_op jit(solution)/shard_map/ppermute | solution.py:320
  83.8 0.0 copy-done
  83.8 0.0 copy-done.1
  83.8 0.0 copy-done.2
  83.8 0.0 copy-done.4
  83.8 0.0 copy-done.5
  83.8 0.0 copy-done.6
  83.8 0.0 copy-done.7
  83.8 0.0 copy-done.9
  83.8 0.0 copy-done.10
  83.8 2.5 %final_layer.1 = (f32[64,144]{1,0:T(8,128)}, f32[64,144]{1,0:T(8,128)}) custom-call(s32[1]{0:T(128)} %bitcast.tile_ref, s32[2]{0:T(128)S(1)} %copy-done.8, s32[1]{0:T(128)S(6)} %copy.26.timestep_ref, s32[2,144]{1,0:T(2,128)S(1)} %copy-done.9, bf16[144,3072]{1,0:T(8,128)(2,1)S(1)} %project.1.own_ref, bf16[144,3072]{1,0:T(8,128)(2,1)S(1)} %collective-permute-done.2.other_ref, ...), custom_call_target="tpu_custom_call" | custom-call | tf_op jit(solution)/shard_map/final_layer/pallas_call | solution.py:323
  (1 shorter events, 0.0 us)
Async XLA Ops:
  6.5 28.9 %all-to-all-start = ((bf16[8,320,128]{2,1,0:T(8,128)(2,1)}), bf16[8,320,128]{2,1,0:T(8,128)(2,1)S(1)}, u32[]{:S(2)}, u32[]{:S(2)}) async-start(bf16[8,320,128]{2,1,0:T(8,128)(2,1)} %query_key_norm.1), calls=%async_computation | async-start | bytes 1310720 | tf_op jit(solution)/shard_map/all_to_all | solution.py:280
  14.7 18.8 %collective-permute-start.1 = (bf16[8,176,128]{2,1,0:T(8,128)(2,1)}, bf16[8,176,128]{2,1,0:T(8,128)(2,1)S(1)}, u32[]{:S(2)}, u32[]{:S(2)}) collective-permute-start(bf16[8,176,128]{2,1,0:T(8,128)(2,1)} %value_layout.1), channel_id=1, source_target_pairs={{0,16},{2,18},{4,20},{6,22},{8,24},{10,26},{12,28},{14,30},{16,0},... | collective-permute-start | bytes 1081352 | tf_op jit(solution)/shard_map/ppermute | solution.py:257
  35.4 20.9 %copy-start.3 = (s32[3,1408]{1,0:T(4,128)S(1)}, s32[3,1408]{1,0:T(4,128)}, u32[]{:S(2)}) copy-start(s32[3,1408]{1,0:T(4,128)} %constant.38.clone.table_ref) | copy-start | bytes 50692
  35.4 20.9 %copy-start.8 = (s32[2]{0:T(128)S(1)}, s32[2]{0:T(128)}, u32[]{:S(2)}) copy-start(s32[2]{0:T(128)} %size_ref.5) | copy-start | bytes 28
  35.4 20.9 %all-to-all-start.1 = ((bf16[8,352,128]{2,1,0:T(8,128)(2,1)}), bf16[8,352,128]{2,1,0:T(8,128)(2,1)S(1)}, u32[]{:S(2)}, u32[]{:S(2)}) async-start(bf16[8,352,128]{2,1,0:T(8,128)(2,1)} %pad_maximum_fusion), calls=%async_computation.1 | async-start | bytes 1441792 | tf_op jit(solution)/shard_map/all_to_all | solution.py:282
  39.9 19.8 %collective-permute-start = (bf16[8,176,128]{2,1,0:T(8,128)(2,1)S(1)}, bf16[8,176,128]{2,1,0:T(8,128)(2,1)S(1)}, u32[]{:S(2)}, u32[]{:S(2)}) collective-permute-start(bf16[8,176,128]{2,1,0:T(8,128)(2,1)S(1)} %slice.4), channel_id=1, source_target_pairs={{0,16},{2,18},{4,20},{6,22},{8,24},{10,26},{12,28},{14,30},{16,0},... | collective-permute-start | bytes 1081352 | tf_op jit(solution)/shard_map/ppermute | solution.py:281
  73.4 10.3 %copy-start = (bf16[1,144,3072]{2,1,0:T(8,128)(2,1)S(1)}, bf16[1,144,3072]{2,1,0:T(8,128)(2,1)}, u32[]{:S(2)}) copy-start(bf16[1,144,3072]{2,1,0:T(8,128)(2,1)} %param.25) | copy-start | bytes 2654212
  73.4 10.3 %copy-start.1 = (bf16[1,144,3072]{2,1,0:T(8,128)(2,1)S(1)}, bf16[1,144,3072]{2,1,0:T(8,128)(2,1)}, u32[]{:S(2)}) copy-start(bf16[1,144,3072]{2,1,0:T(8,128)(2,1)} %param.26) | copy-start | bytes 2654212
  73.4 10.3 %copy-start.2 = (bf16[3072,64]{0,1:T(8,128)(2,1)S(1)}, bf16[3072,64]{0,1:T(8,128)(2,1)}, u32[]{:S(2)}) copy-start(bf16[3072,64]{0,1:T(8,128)(2,1)} %param.30) | copy-start | bytes 1179652
  73.4 10.3 %copy-start.4 = (f32[1,144,64]{1,2,0:T(8,128)S(1)}, f32[1,144,64]{1,2,0:T(8,128)}, u32[]{:S(2)}) copy-start(f32[1,144,64]{1,2,0:T(8,128)} %param.32) | copy-start | bytes 110596
  73.4 10.3 %copy-start.5 = (f32[3072]{0:T(1024)S(1)}, f32[3072]{0:T(1024)}, u32[]{:S(2)}) copy-start(f32[3072]{0:T(1024)} %param.27) | copy-start | bytes 36868
  73.4 10.3 %copy-start.6 = (f32[3072]{0:T(1024)S(1)}, f32[3072]{0:T(1024)}, u32[]{:S(2)}) copy-start(f32[3072]{0:T(1024)} %param.28) | copy-start | bytes 36868
  73.5 10.3 %copy-start.7 = (f32[3072]{0:T(1024)S(1)}, f32[3072]{0:T(1024)}, u32[]{:S(2)}) copy-start(f32[3072]{0:T(1024)} %param.29) | copy-start | bytes 36868
  73.5 10.3 %copy-start.9 = (s32[2,144]{1,0:T(2,128)S(1)}, s32[2,144]{1,0:T(2,128)}, u32[]{:S(2)}) copy-start(s32[2,144]{1,0:T(2,128)} %constant.39.clone.local_ref) | copy-start | bytes 3460
  73.5 10.3 %copy-start.10 = (f32[64]{0:T(128)S(1)}, f32[64]{0:T(128)}, u32[]{:S(2)}) copy-start(f32[64]{0:T(128)} %param.31) | copy-start | bytes 772
  77.9 5.9 %collective-permute-start.2 = (bf16[144,3072]{1,0:T(8,128)(2,1)S(1)}, bf16[144,3072]{1,0:T(8,128)(2,1)S(1)}, u32[]{:S(2)}, u32[]{:S(2)}) collective-permute-start(bf16[144,3072]{1,0:T(8,128)(2,1)S(1)} %project.1.own_ref), channel_id=1, source_target_pairs={{0,1},{1,0},{2,3},{3,2},{4,5},{5,4},{6,7},{7,6},{8,9},{9,8},{10,11... | collective-permute-start | bytes 2654216 | tf_op jit(solution)/shard_map/ppermute | solution.py:320

commit v2 on v1

--- a/solution.py
+++ b/solution.py
@@ -22,7 +22,6 @@
 HALF_KEYS = GROUP * KEYS
 DEAD = -1e30
 EXP_SCALE = HEAD ** (-0.5) * math.log2(math.e)
-VMEM_LIMIT = 48 * 1024 * 1024
 
 
 def position_tables():
@@ -50,7 +49,7 @@
     cosine = np.repeat(np.cos(angles), 2, axis=-1)
     sine = np.repeat(np.sin(angles), 2, axis=-1)
     sine[..., 0::2] *= -1.0
-    return cosine.astype(np.float32), sine.astype(np.float32)
+    return np.stack([cosine, sine], axis=1).astype(np.float32)
 
 
 def key_tables():
@@ -65,21 +64,16 @@
     return np.concatenate([key_row, key_col, key_slot], axis=0).astype(np.int32)
 
 
-def value_kernel(image_ref, text_ref, out_ref):
-    for head in range(GROUP):
-        lanes = slice(head * HEAD, (head + 1) * HEAD)
-        out_ref[head, 0:PIX, :] = image_ref[0, :, lanes]
-        out_ref[head, PIX:KEYS, :] = text_ref[0, :, lanes]
-
-
 def normed(vectors, gain):
     wide = vectors.astype(jnp.float32)
     return wide * lax.rsqrt(jnp.mean(wide * wide, axis=-1, keepdims=True) + 1e-06) * gain
 
 
-def query_key_kernel(tile_ref, query_ref, key_ref, text_ref, q_gain_ref, k_gain_ref, cos_ref, sin_ref, out_ref):
-    cosine = cos_ref[0]
-    sine = sin_ref[0]
+def prepare_kernel(
+    tile_ref, image_ref, text_ref, q_gain_ref, k_gain_ref, table_ref, out_ref, value_ref
+):
+    cosine = table_ref[0, 0]
+    sine = table_ref[0, 1]
     even = lax.broadcasted_iota(jnp.int32, (PIX, HEAD), 1) % 2 == 0
 
     def rotated(vectors, gain):
@@ -87,11 +81,17 @@
         swapped = jnp.where(even, pltpu.roll(scaled, HEAD - 1, 1), pltpu.roll(scaled, 1, 1))
         return (scaled * cosine + swapped * sine).astype(jnp.bfloat16)
 
-    for head in range(GROUP):
+    text = text_ref[...]
+    text_keys = text[:, 0, :]
+    text_values = text[:, 1, :]
+    for head in range(out_ref.shape[0]):
         lanes = slice(head * HEAD, (head + 1) * HEAD)
-        out_ref[head, 0:PIX, :] = rotated(query_ref[0, :, lanes], q_gain_ref[...])
-        out_ref[head, PIX : 2 * PIX, :] = rotated(key_ref[0, :, lanes], k_gain_ref[...])
-        out_ref[head, 2 * PIX :, :] = normed(text_ref[0, :, lanes], k_gain_ref[...]).astype(jnp.bfloat16)
+        out_ref[head, 0:PIX, :] = rotated(image_ref[0, :, lanes], q_gain_ref[...])
+        out_ref[head, PIX : 2 * PIX, :] = rotated(image_ref[1, :, lanes], k_gain_ref[...])
+        out_ref[head, 2 * PIX : PIX + KEYS, :] = normed(text_keys[:, lanes], k_gain_ref[...]).astype(jnp.bfloat16)
+        for ref, start in ((out_ref, PIX + KEYS), (value_ref, 0)):
+            ref[head, start : start + PIX, :] = image_ref[2, :, lanes]
+            ref[head, start + PIX : start + KEYS, :] = text_values[:, lanes]
 
 
 def key_bias(table_ref, size_ref, text_len_ref, half):
@@ -107,14 +107,19 @@
     return scores + bias
 
 
-def local_kernel(half_ref, size_ref, text_len_ref, table_ref, qk_ref, values_ref, acc_ref, peak_ref, key_s, value_s):
+def stage(keys_ref, key_start, values_ref, value_start, key_s, value_s):
+    for tile in range(GROUP):
+        at = tile * KEYS
+        key_s[at : at + KEYS, :] = keys_ref[tile, key_start : key_start + KEYS, :]
+        value_s[at : at + KEYS, 0:HEAD] = values_ref[tile, value_start : value_start + KEYS, :]
+    value_s[:, HEAD:] = jnp.ones((HALF_KEYS, HEAD), jnp.bfloat16)
+
+
+def local_kernel(half_ref, size_ref, text_len_ref, table_ref, own_ref, acc_ref, peak_ref, key_s, value_s):
     bias = key_bias(table_ref, size_ref, text_len_ref, half_ref[0])
+    stage(own_ref, PIX, own_ref, PIX + KEYS, key_s, value_s)
     for tile in range(GROUP):
-        key_s[tile * KEYS : (tile + 1) * KEYS, :] = qk_ref[tile, PIX:, :]
-        value_s[tile * KEYS : (tile + 1) * KEYS, 0:HEAD] = values_ref[tile, 0:KEYS, :]
-    value_s[:, HEAD:] = jnp.ones((HALF_KEYS, HEAD), jnp.bfloat16)
-    for tile in range(GROUP):
-        scores = scores_of(qk_ref[tile, 0:PIX, :], key_s[...], bias)
+        scores = scores_of(own_ref[tile, 0:PIX, :], key_s[...], bias)
         peak = jnp.max(scores, axis=1, keepdims=True)
         weights = jnp.exp2((scores - peak) * EXP_SCALE).astype(jnp.bfloat16)
         acc_ref[tile] = jnp.dot(weights, value_s[...], preferred_element_type=jnp.float32)
@@ -122,15 +127,12 @@
 
 
 def remote_kernel(
-    half_ref, size_ref, text_len_ref, table_ref, qk_ref, keys_ref, values_ref, acc_ref, peak_ref, out_ref, key_s, value_s
+    half_ref, size_ref, text_len_ref, table_ref, own_ref, keys_ref, values_ref, acc_ref, peak_ref, out_ref, key_s, value_s
 ):
     bias = key_bias(table_ref, size_ref, text_len_ref, 1 - half_ref[0])
+    stage(keys_ref, 0, values_ref, 0, key_s, value_s)
     for tile in range(GROUP):
-        key_s[tile * KEYS : (tile + 1) * KEYS, :] = keys_ref[tile]
-        value_s[tile * KEYS : (tile + 1) * KEYS, 0:HEAD] = values_ref[tile, KEYS:, :]
-    value_s[:, HEAD:] = jnp.ones((HALF_KEYS, HEAD), jnp.bfloat16)
-    for tile in range(GROUP):
-        scores = scores_of(qk_ref[tile, 0:PIX, :], key_s[...], bias)
+        scores = scores_of(own_ref[tile, 0:PIX, :], key_s[...], bias)
         before = peak_ref[tile]
         peak = jnp.maximum(before[:, 0:1], jnp.max(scores, axis=1, keepdims=True))
         weights = jnp.exp2((scores - peak) * EXP_SCALE).astype(jnp.bfloat16)
@@ -205,16 +207,13 @@
     next_ref[...] = latent_ref[...] + step * velocity
 
 
-def whole(shape, index=None):
-    at = index if index is not None else (0,) * len(shape)
-    return pl.BlockSpec(shape, lambda *_: at)
-
-
 SMEM = pl.BlockSpec(memory_space=pltpu.SMEM)
-
-
-def params():
-    return pltpu.CompilerParams(vmem_limit_bytes=VMEM_LIMIT)
+VMEM = pl.BlockSpec(memory_space=pltpu.VMEM)
+HBM = pl.BlockSpec(memory_space=pltpu.HBM)
+
+
+def params(mebibytes):
+    return pltpu.CompilerParams(vmem_limit_bytes=mebibytes * 1024 * 1024)
 
 
 def shards(
@@ -242,98 +241,88 @@
     tile = lax.axis_index("tile").astype(jnp.int32).reshape(1)
     half = tile // GROUP
     triple = image_qkv.reshape(PIX, 3, width).transpose(1, 0, 2)
-    text = text_kv.transpose(1, 0, 2)
     groups = [list(range(GROUP)), list(range(GROUP, 2 * GROUP))]
     across = [(t, (t + GROUP) % TILES) for t in range(TILES)]
 
-    values = pl.pallas_call(
-        value_kernel,
-        grid=(1,),
-        in_specs=[whole((1, PIX, width), (2, 0, 0)), whole((1, SLOTS, width), (1, 0, 0))],
-        out_specs=whole((GROUP, KEYS, HEAD)),
-        out_shape=jax.ShapeDtypeStruct((GROUP, KEYS, HEAD), bf16),
-        name="value_layout",
-    )(triple, text)
-    far_values = lax.ppermute(values, "tile", across)
-
-    cosine, sine = rope_tables()
-    spot = pl.BlockSpec((1, PIX, HEAD), lambda i, tile_ref: (tile_ref[0], 0, 0))
-    query_key = pl.pallas_call(
-        query_key_kernel,
+    per_step = 2
+    prepared, values = pl.pallas_call(
+        prepare_kernel,
         grid_spec=pltpu.PrefetchScalarGridSpec(
             num_scalar_prefetch=1,
-            grid=(1,),
+            grid=(GROUP // per_step,),
             in_specs=[
-                whole((1, PIX, width), (0, 0, 0)),
-                whole((1, PIX, width), (1, 0, 0)),
-                whole((1, SLOTS, width), (0, 0, 0)),
-                whole((1, HEAD)),
-                whole((1, HEAD)),
-                spot,
-                spot,
+                pl.BlockSpec((3, PIX, per_step * HEAD), lambda i, tile_ref: (0, 0, i)),
+                pl.BlockSpec((SLOTS, 2, per_step * HEAD), lambda i, tile_ref: (0, 0, i)),
+                pl.BlockSpec((1, HEAD), lambda i, tile_ref: (0, 0)),
+                pl.BlockSpec((1, HEAD), lambda i, tile_ref: (0, 0)),
+                pl.BlockSpec((1, 2, PIX, HEAD), lambda i, tile_ref: (tile_ref[0], 0, 0, 0)),
             ],
-            out_specs=whole((GROUP, PIX + KEYS, HEAD)),
+            out_specs=(
+                pl.BlockSpec((per_step, PIX + 2 * KEYS, HEAD), lambda i, tile_ref: (i, 0, 0)),
+                pl.BlockSpec((per_step, KEYS, HEAD), lambda i, tile_ref: (i, 0, 0)),
+            ),
         ),
-        out_shape=jax.ShapeDtypeStruct((GROUP, PIX + KEYS, HEAD), bf16),
-        name="query_key_norm",
-    )(tile, triple, triple, text, q_gain.reshape(1, HEAD), k_gain.reshape(1, HEAD), jnp.asarray(cosine), jnp.asarray(sine))
-    query_key = lax.all_to_all(query_key, "tile", 0, 0, axis_index_groups=groups, tiled=True)
-    far_keys = lax.ppermute(query_key[:, PIX:, :], "tile", across)
-    value_pair = lax.all_to_all(
-        jnp.concatenate([values, far_values], axis=1), "tile", 0, 0, axis_index_groups=groups, tiled=True
-    )
+        out_shape=(
+            jax.ShapeDtypeStruct((GROUP, PIX + 2 * KEYS, HEAD), bf16),
+            jax.ShapeDtypeStruct((GROUP, KEYS, HEAD), bf16),
+        ),
+        compiler_params=params(8),
+        name="prepare",
+    )(tile, triple, text_kv, q_gain.reshape(1, HEAD), k_gain.reshape(1, HEAD), jnp.asarray(rope_tables()))
+    far_values = lax.ppermute(values, "tile", across)
+    own = lax.all_to_all(prepared, "tile", 0, 0, axis_index_groups=groups, tiled=True)
+    far_keys = lax.ppermute(own[:, PIX : PIX + KEYS, :], "tile", across)
+    far_values = lax.all_to_all(far_values, "tile", 0, 0, axis_index_groups=groups, tiled=True)
 
     table = jnp.asarray(key_tables())
     acc, peak = pl.pallas_call(
         local_kernel,
-        in_specs=[SMEM, SMEM, SMEM] + [pl.BlockSpec(memory_space=pltpu.VMEM)] * 3,
-        out_specs=(pl.BlockSpec(memory_space=pltpu.VMEM),) * 2,
+        in_specs=[SMEM, SMEM, SMEM] + [VMEM] * 2,
+        out_specs=(VMEM, VMEM),
         out_shape=(
             jax.ShapeDtypeStruct((GROUP, PIX, 2 * HEAD), jnp.float32),
             jax.ShapeDtypeStruct((GROUP, PIX, HEAD), jnp.float32),
         ),
         scratch_shapes=[pltpu.VMEM((HALF_KEYS, HEAD), bf16), pltpu.VMEM((HALF_KEYS, 2 * HEAD), bf16)],
-        compiler_params=params(),
+        compiler_params=params(16),
         name="attend_local",
-    )(half, image_size, text_len, table, query_key, value_pair)
+    )(half, image_size, text_len, table, own)
     attended = pl.pallas_call(
         remote_kernel,
-        in_specs=[SMEM, SMEM, SMEM] + [pl.BlockSpec(memory_space=pltpu.VMEM)] * 6,
-        out_specs=pl.BlockSpec(memory_space=pltpu.VMEM),
+        in_specs=[SMEM, SMEM, SMEM] + [VMEM] * 6,
+        out_specs=VMEM,
         out_shape=jax.ShapeDtypeStruct((GROUP, PIX, HEAD), bf16),
         scratch_shapes=[pltpu.VMEM((HALF_KEYS, HEAD), bf16), pltpu.VMEM((HALF_KEYS, 2 * HEAD), bf16)],
-        compiler_params=params(),
+        compiler_params=params(16),
         name="attend_far",
-    )(half, image_size, text_len, table, query_key, far_keys, value_pair, acc, peak)
+    )(half, image_size, text_len, table, own, far_keys, far_values, acc, peak)
     attended = lax.all_to_all(attended, "tile", 0, 0, axis_index_groups=groups, tiled=True)
 
-    columns = 768
-    own = pl.pallas_call(
+    partial = pl.pallas_call(
         project_kernel,
-        grid=(model // columns,),
-        in_specs=[whole((GROUP, PIX, HEAD)), pl.BlockSpec((width, columns), lambda i: (0, i))],
-        out_specs=pl.BlockSpec((PIX, columns), lambda i: (0, i)),
+        in_specs=[VMEM, VMEM],
+        out_specs=VMEM,
         out_shape=jax.ShapeDtypeStruct((PIX, model), bf16),
-        compiler_params=params(),
+        compiler_params=params(16),
         name="project",
     )(attended, out_weight)
-    other = lax.ppermute(own, "tp", [(0, 1), (1, 0)])
+    other = lax.ppermute(partial, "tp", [(0, 1), (1, 0)])
 
     local = np.stack([np.arange(PIX) // TILE_W, np.arange(PIX) % TILE_W]).astype(np.int32)
     velocity, latent_next = pl.pallas_call(
         final_kernel,
-        in_specs=[SMEM, SMEM, SMEM] + [pl.BlockSpec(memory_space=pltpu.VMEM)] * 11,
-        out_specs=(pl.BlockSpec(memory_space=pltpu.VMEM),) * 2,
+        in_specs=[SMEM, SMEM, SMEM] + [VMEM] * 11,
+        out_specs=(VMEM, VMEM),
         out_shape=(jax.ShapeDtypeStruct((latents, PIX), jnp.float32),) * 2,
         scratch_shapes=[pltpu.VMEM((PIX, model), bf16)],
-        compiler_params=params(),
+        compiler_params=params(12),
         name="final_layer",
     )(
         tile,
         image_size,
         timestep,
         jnp.asarray(local),
-        own,
+        partial,
         other,
         hidden.reshape(PIX, model),
         mlp_term.reshape(PIX, model),

time: 86.7 us -> 87.3 us (level)
  local copies, waits for them, and re-layouts: 1.66 us -> 8.64 us
  Pallas kernels: 19.7 us -> 13.5 us
  waiting for transfers between devices: 29.9 us -> 32 us
  other arithmetic: 1.92 us -> 0 us
    ppermute x2, waiting for transfers between devices: 1.4 us -> 13.1 us  [the longest x1 11.7 us: shards(): far_keys = lax.ppermute(own[:, PIX:PIX + KEYS, :], 'tile', across)]
    all_to_all x2, waiting for transfers between devices: 12.7 us -> 3.62 us  [the longest x1 1.93 us: shards(): lax.all_to_all(prepared, 'tile', 0, 0, axis_index_groups=groups, tiled=True)]
    pallas_call x6 -> x5, Pallas kernels: 19.7 us -> 13.5 us  [the longest x1 3.39 us: shards(): pl.pallas_call(prepare_kernel, grid_spec=pltpu.PrefetchScalarGridSpec(num...]
    unnamed x23 -> x34, local copies, waits for them, and re-layouts: 1.64 us -> 7.88 us
    ppermute x2, starting transfers between devices: 6.88 us -> 3.89 us  [the longest x1 3.81 us: shards(): other = lax.ppermute(partial, 'tp', [(0, 1), (1, 0)])]
    all_to_all x2, starting transfers between devices: 10.8 us -> 13.3 us  [the longest x1 6.77 us: shards(): lax.all_to_all(far_values, 'tile', 0, 0, axis_index_groups=groups, tiled=...]
    concatenate x1 -> x0, other arithmetic: 1.92 us -> none  [shards(): jnp.concatenate([values, far_values], axis=1)]
  transfers between devices with their start and end apart: 5 -> 5, of which waited for: 3 -> 5; matrix products, arithmetic and copies ran while one was open for 2% -> 1% of each run, Pallas kernels for 6% -> 4%
where the time goes in v2:
time: 87.3 us; the launch traced here: 86.8 us
  waiting for transfers between devices  32 us (37%)
  starting transfers between devices  20.2 us (23%)
  Pallas kernels  13.5 us (15%)
  blocking collectives  10.5 us (12%)
  local copies, waits for them, and re-layouts  8.64 us (10%)
  between operations  2.09 us (2%)
    ppermute x1, waiting for transfers between devices, shards(): far_values = lax.ppermute(values, 'tile', across)  15.2 us
    ppermute x1, waiting for transfers between devices, shards(): far_keys = lax.ppermute(own[:, PIX:PIX + KEYS, :], 'tile', across)  11.7 us
    all_to_all x1, blocking collectives, shards(): lax.all_to_all(attended, 'tile', 0, 0, axis_index_groups=groups, tiled=True)  10.5 us
    unnamed x34, local copies, waits for them, and re-layouts  7.88 us
    all_to_all x1, starting transfers between devices, shards(): lax.all_to_all(far_values, 'tile', 0, 0, axis_index_groups=groups, tiled=...  6.77 us
    all_to_all x1, starting transfers between devices, shards(): lax.all_to_all(prepared, 'tile', 0, 0, axis_index_groups=groups, tiled=True)  6.51 us
    ppermute x1, starting transfers between devices, shards(): other = lax.ppermute(partial, 'tp', [(0, 1), (1, 0)])  3.81 us
    pallas_call x1, Pallas kernels, shards(): pl.pallas_call(prepare_kernel, grid_spec=pltpu.PrefetchScalarGridSpec(num...  3.39 us
  transfers between devices with their start and end apart: 5, of which 5 were waited for; matrix products, arithmetic and copies ran while one was open for 1% of the time, Pallas kernels for 4%

profile of v2, /device:TPU:1, one launch (start us, length us, event | category | flops | bytes accessed | tf_op | source)
XLA Modules:
  0.0 86.8 jit_solution(17443826943281377096)
XLA Ops:
  0.6 0.0 copy-start.1
  0.6 1.7 %copy-done.1 = f32[16,2,144,128]{3,2,1,0:T(8,128)S(1)} copy-done((f32[16,2,144,128]{3,2,1,0:T(8,128)S(1)}, f32[16,2,144,128]{3,2,1,0:T(8,128)}, u32[]{:S(2)}) %copy-start.1) | copy-done | bytes 2359320
  2.3 0.0 copy-start.2
  2.3 1.2 %copy-done.2 = bf16[1,144,3,1024]{3,1,2,0:T(8,128)(2,1)S(1)} copy-done((bf16[1,144,3,1024]{3,1,2,0:T(8,128)(2,1)S(1)}, bf16[1,144,3,1024]{3,1,2,0:T(8,128)(2,1)}, u32[]{:S(2)}) %copy-start.2) | copy-done | bytes 884760
  3.5 0.0 copy-start.6
  3.5 0.9 %copy-done.6 = bf16[32,2,1024]{2,1,0:T(2,128)(2,1)S(1)} copy-done((bf16[32,2,1024]{2,1,0:T(2,128)(2,1)S(1)}, bf16[32,2,1024]{2,1,0:T(2,128)(2,1)}, u32[]{:S(2)}) %copy-start.6) | copy-done | bytes 131096
  4.4 0.0 copy-start.14
  4.4 0.7 copy-done.14
  5.0 0.0 copy-start.15
  5.0 0.7 copy-done.15
  5.7 3.4 %prepare.1 = (bf16[8,496,128]{2,1,0:T(8,128)(2,1)}, bf16[8,176,128]{2,1,0:T(8,128)(2,1)S(1)}) custom-call(s32[1]{0:T(128)} %bitcast.tile_ref, bf16[3,144,1024]{2,1,0:T(8,128)(2,1)S(1)} %bitcast.22, bf16[32,2,1024]{2,1,0:T(2,128)(2,1)S(1)} %copy-done.6, f32[1,128]{1,0:T(1,128)S(1)} %bitcast.30, f32[1,128]{1,0:T(1,128)S(1)} %bitcast.31, ...), custom_call_target="tpu_custom_call" | custom-call | tf_op jit(solution)/shard_map/prepare/pallas_call | solution.py:248
  9.1 0.0 copy-start.7
  9.1 0.0 copy-start.12
  9.1 6.5 %all-to-all-start = ((bf16[8,496,128]{2,1,0:T(8,128)(2,1)}), bf16[8,496,128]{2,1,0:T(8,128)(2,1)S(1)}, u32[]{:S(2)}, u32[]{:S(2)}) async-start(bf16[8,496,128]{2,1,0:T(8,128)(2,1)} %get-tuple-element.8), calls=%async_computation | async-start | bytes 2031616 | tf_op jit(solution)/shard_map/all_to_all | solution.py:273
  15.6 3.0 %collective-permute-start.1 = (bf16[8,176,128]{2,1,0:T(8,128)(2,1)S(1)}, bf16[8,176,128]{2,1,0:T(8,128)(2,1)}, u32[]{:S(2)}, u32[]{:S(2)}) collective-permute-start(bf16[8,176,128]{2,1,0:T(8,128)(2,1)S(1)} %get-tuple-element.9), channel_id=1, source_target_pairs={{0,16},{2,18},{4,20},{6,22},{8,24},{10,26},{12,28},{14,30},{16,0},... | collective-permute-start | bytes 1081352 | tf_op jit(solution)/shard_map/ppermute | solution.py:272
  18.6 15.2 %collective-permute-done.1 = bf16[8,176,128]{2,1,0:T(8,128)(2,1)} collective-permute-done((bf16[8,176,128]{2,1,0:T(8,128)(2,1)S(1)}, bf16[8,176,128]{2,1,0:T(8,128)(2,1)}, u32[]{:S(2)}, u32[]{:S(2)}) %collective-permute-start.1) | collective-permute-done | bytes 360480 | tf_op jit(solution)/shard_map/ppermute | solution.py:272
  33.8 1.9 %all-to-all-done.own_ref = bf16[8,496,128]{2,1,0:T(8,128)(2,1)S(1)} async-done(((bf16[8,496,128]{2,1,0:T(8,128)(2,1)}), bf16[8,496,128]{2,1,0:T(8,128)(2,1)S(1)}, u32[]{:S(2)}, u32[]{:S(2)}) %all-to-all-start) | async-done | bytes 1015840 | tf_op jit(solution)/shard_map/all_to_all | solution.py:273
  35.7 6.8 %all-to-all-start.1 = ((bf16[8,176,128]{2,1,0:T(8,128)(2,1)}), bf16[8,176,128]{2,1,0:T(8,128)(2,1)S(1)}, u32[]{:S(2)}, u32[]{:S(2)}) async-start(bf16[8,176,128]{2,1,0:T(8,128)(2,1)} %collective-permute-done.1), calls=%async_computation.1 | async-start | bytes 720896 | tf_op jit(solution)/shard_map/all_to_all | solution.py:275
  42.5 0.8 slice.4
  43.3 0.1 collective-permute-start
  44.0 0.0 copy-done.7
  44.0 0.0 copy-done.12
  44.0 3.3 %attend_local.1 = (f32[8,144,256]{2,1,0:T(8,128)S(1)}, f32[8,144,128]{2,1,0:T(8,128)S(1)}) custom-call(s32[1]{0:T(128)S(6)} %select_n.5.half_ref, s32[2]{0:T(128)S(1)} %copy-done.12, s32[1]{0:T(128)S(6)} %copy.21.text_len_ref, s32[3,1408]{1,0:T(4,128)S(1)} %copy-done.7, bf16[8,496,128]{2,1,0:T(8,128)(2,1)S(1)} %all-to-all-done.own_ref), custom_call_target="tpu_custom_call" | custom-call | tf_op jit(solution)/shard_map/attend_local/pallas_call | solution.py:278
  47.3 1.7 %all-to-all-done.1.values_ref = bf16[8,176,128]{2,1,0:T(8,128)(2,1)S(1)} async-done(((bf16[8,176,128]{2,1,0:T(8,128)(2,1)}), bf16[8,176,128]{2,1,0:T(8,128)(2,1)S(1)}, u32[]{:S(2)}, u32[]{:S(2)}) %all-to-all-start.1) | async-done | bytes 360480 | tf_op jit(solution)/shard_map/all_to_all | solution.py:275
  49.0 11.7 %collective-permute-done.keys_ref = bf16[8,176,128]{2,1,0:T(8,128)(2,1)S(1)} collective-permute-done((bf16[8,176,128]{2,1,0:T(8,128)(2,1)}, bf16[8,176,128]{2,1,0:T(8,128)(2,1)S(1)}, u32[]{:S(2)}, u32[]{:S(2)}) %collective-permute-start) | collective-permute-done | bytes 360480 | tf_op jit(solution)/shard_map/ppermute | solution.py:274
  60.7 3.3 %attend_far.1 = bf16[8,144,128]{2,1,0:T(8,128)(2,1)S(1)} custom-call(s32[1]{0:T(128)S(6)} %select_n.5.half_ref, s32[2]{0:T(128)S(1)} %copy-done.12, s32[1]{0:T(128)S(6)} %copy.21.text_len_ref, s32[3,1408]{1,0:T(4,128)S(1)} %copy-done.7, bf16[8,496,128]{2,1,0:T(8,128)(2,1)S(1)} %all-to-all-done.own_ref, ...), custom_call_target="tpu_custom_call" | custom-call | tf_op jit(solution)/shard_map/attend_far/pallas_call | solution.py:290
  64.0 10.5 %all_to_all.15.attended_ref = bf16[8,144,128]{2,1,0:T(8,128)(2,1)S(1)} all-to-all(bf16[8,144,128]{2,1,0:T(8,128)(2,1)S(1)} %attend_far.1), channel_id=1, replica_groups={{0,2,4,6,8,10,12,14},{16,18,20,22,24,26,28,30},{1,3,5,7,9,11,13,15},{17..., dimensions={0} | all-to-all | bytes 589824 | tf_op jit(solution)/shard_map/all_to_all | solution.py:299
  74.5 0.0 copy-start
  74.5 2.8 %copy-done = bf16[1024,3072]{1,0:T(8,128)(2,1)S(1)} copy-done((bf16[1024,3072]{1,0:T(8,128)(2,1)S(1)}, bf16[1024,3072]{1,0:T(8,128)(2,1)}, u32[]{:S(2)}) %copy-start) | copy-done | bytes 6291480
  77.3 0.0 copy-start.3
  77.3 0.0 copy-start.4
  77.3 0.0 copy-start.5
  77.3 0.0 copy-start.8
  77.3 0.0 copy-start.9
  77.3 0.0 copy-start.10
  77.3 0.0 copy-start.11
  77.3 0.0 copy-start.13
  77.3 0.0 copy-start.16
  77.4 1.1 %project.1.own_ref = bf16[144,3072]{1,0:T(8,128)(2,1)S(1)} custom-call(bf16[8,144,128]{2,1,0:T(8,128)(2,1)S(1)} %all_to_all.15.attended_ref, bf16[1024,3072]{1,0:T(8,128)(2,1)S(1)} %copy-done), custom_call_target="tpu_custom_call" | custom-call | tf_op jit(solution)/shard_map/project/pallas_call | solution.py:301
  78.5 3.8 %collective-permute-start.2 = (bf16[144,3072]{1,0:T(8,128)(2,1)S(1)}, bf16[144,3072]{1,0:T(8,128)(2,1)S(1)}, u32[]{:S(2)}, u32[]{:S(2)}) collective-permute-start(bf16[144,3072]{1,0:T(8,128)(2,1)S(1)} %project.1.own_ref), channel_id=1, source_target_pairs={{0,1},{1,0},{2,3},{3,2},{4,5},{5,4},{6,7},{7,6},{8,9},{9,8},{10,11... | collective-permute-start | bytes 2654216 | tf_op jit(solution)/shard_map/ppermute | solution.py:309
  82.9 1.4 %collective-permute-done.2.other_ref = bf16[144,3072]{1,0:T(8,128)(2,1)S(1)} collective-permute-done((bf16[144,3072]{1,0:T(8,128)(2,1)S(1)}, bf16[144,3072]{1,0:T(8,128)(2,1)S(1)}, u32[]{:S(2)}, u32[]{:S(2)}) %collective-permute-start.2) | collective-permute-done | bytes 884768 | tf_op jit(solution)/shard_map/ppermute | solution.py:309
  84.3 0.0 copy-done.3
  84.3 0.0 copy-done.4
  84.3 0.0 copy-done.5
  84.3 0.0 copy-done.8
  84.3 0.0 copy-done.9
  84.3 0.0 copy-done.10
  84.3 0.0 copy-done.11
  84.4 0.0 copy-done.13
  84.4 0.0 copy-done.16
  84.4 2.5 %final_layer.1 = (f32[64,144]{1,0:T(8,128)}, f32[64,144]{1,0:T(8,128)}) custom-call(s32[1]{0:T(128)} %bitcast.tile_ref, s32[2]{0:T(128)S(1)} %copy-done.12, s32[1]{0:T(128)S(6)} %copy.22.timestep_ref, s32[2,144]{1,0:T(2,128)S(1)} %copy-done.13, bf16[144,3072]{1,0:T(8,128)(2,1)S(1)} %project.1.own_ref, ...), custom_call_target="tpu_custom_call" | custom-call | tf_op jit(solution)/shard_map/final_layer/pallas_call | solution.py:312
Async XLA Ops:
  0.6 1.7 %copy-start.1 = (f32[16,2,144,128]{3,2,1,0:T(8,128)S(1)}, f32[16,2,144,128]{3,2,1,0:T(8,128)}, u32[]{:S(2)}) copy-start(f32[16,2,144,128]{3,2,1,0:T(8,128)} %constant.34.clone.table_ref) | copy-start | bytes 7077892
  2.3 1.2 %copy-start.2 = (bf16[1,144,3,1024]{3,1,2,0:T(8,128)(2,1)S(1)}, bf16[1,144,3,1024]{3,1,2,0:T(8,128)(2,1)}, u32[]{:S(2)}) copy-start(bf16[1,144,3,1024]{3,1,2,0:T(8,128)(2,1)} %param.19) | copy-start | bytes 2654212
  3.5 0.9 %copy-start.6 = (bf16[32,2,1024]{2,1,0:T(2,128)(2,1)S(1)}, bf16[32,2,1024]{2,1,0:T(2,128)(2,1)}, u32[]{:S(2)}) copy-start(bf16[32,2,1024]{2,1,0:T(2,128)(2,1)} %text_ref.1) | copy-start | bytes 393220
  4.4 0.7 copy-start.14
  5.0 0.7 copy-start.15
  9.1 34.9 %copy-start.7 = (s32[3,1408]{1,0:T(4,128)S(1)}, s32[3,1408]{1,0:T(4,128)}, u32[]{:S(2)}) copy-start(s32[3,1408]{1,0:T(4,128)} %constant.35.clone.table_ref) | copy-start | bytes 50692
  9.1 34.9 %copy-start.12 = (s32[2]{0:T(128)S(1)}, s32[2]{0:T(128)}, u32[]{:S(2)}) copy-start(s32[2]{0:T(128)} %size_ref.5) | copy-start | bytes 28
  9.1 26.7 %all-to-all-start = ((bf16[8,496,128]{2,1,0:T(8,128)(2,1)}), bf16[8,496,128]{2,1,0:T(8,128)(2,1)S(1)}, u32[]{:S(2)}, u32[]{:S(2)}) async-start(bf16[8,496,128]{2,1,0:T(8,128)(2,1)} %get-tuple-element.8), calls=%async_computation | async-start | bytes 2031616 | tf_op jit(solution)/shard_map/all_to_all | solution.py:273
  15.6 18.2 %collective-permute-start.1 = (bf16[8,176,128]{2,1,0:T(8,128)(2,1)S(1)}, bf16[8,176,128]{2,1,0:T(8,128)(2,1)}, u32[]{:S(2)}, u32[]{:S(2)}) collective-permute-start(bf16[8,176,128]{2,1,0:T(8,128)(2,1)S(1)} %get-tuple-element.9), channel_id=1, source_target_pairs={{0,16},{2,18},{4,20},{6,22},{8,24},{10,26},{12,28},{14,30},{16,0},... | collective-permute-start | bytes 1081352 | tf_op jit(solution)/shard_map/ppermute | solution.py:272
  35.7 13.3 %all-to-all-start.1 = ((bf16[8,176,128]{2,1,0:T(8,128)(2,1)}), bf16[8,176,128]{2,1,0:T(8,128)(2,1)S(1)}, u32[]{:S(2)}, u32[]{:S(2)}) async-start(bf16[8,176,128]{2,1,0:T(8,128)(2,1)} %collective-permute-done.1), calls=%async_computation.1 | async-start | bytes 720896 | tf_op jit(solution)/shard_map/all_to_all | solution.py:275
  43.3 17.5 %collective-permute-start = (bf16[8,176,128]{2,1,0:T(8,128)(2,1)}, bf16[8,176,128]{2,1,0:T(8,128)(2,1)S(1)}, u32[]{:S(2)}, u32[]{:S(2)}) collective-permute-start(bf16[8,176,128]{2,1,0:T(8,128)(2,1)} %slice.4), channel_id=1, source_target_pairs={{0,16},{2,18},{4,20},{6,22},{8,24},{10,26},{12,28},{14,30},{16,0},... | collective-permute-start | bytes 1081352 | tf_op jit(solution)/shard_map/ppermute | solution.py:274
  74.5 2.8 %copy-start = (bf16[1024,3072]{1,0:T(8,128)(2,1)S(1)}, bf16[1024,3072]{1,0:T(8,128)(2,1)}, u32[]{:S(2)}) copy-start(bf16[1024,3072]{1,0:T(8,128)(2,1)} %weight_ref.1) | copy-start | bytes 18874372
  77.3 7.0 %copy-start.3 = (bf16[1,144,3072]{2,1,0:T(8,128)(2,1)S(1)}, bf16[1,144,3072]{2,1,0:T(8,128)(2,1)}, u32[]{:S(2)}) copy-start(bf16[1,144,3072]{2,1,0:T(8,128)(2,1)} %param.24) | copy-start | bytes 2654212
  77.3 7.0 %copy-start.4 = (bf16[1,144,3072]{2,1,0:T(8,128)(2,1)S(1)}, bf16[1,144,3072]{2,1,0:T(8,128)(2,1)}, u32[]{:S(2)}) copy-start(bf16[1,144,3072]{2,1,0:T(8,128)(2,1)} %param.25) | copy-start | bytes 2654212
  77.3 7.0 %copy-start.5 = (bf16[3072,64]{0,1:T(8,128)(2,1)S(1)}, bf16[3072,64]{0,1:T(8,128)(2,1)}, u32[]{:S(2)}) copy-start(bf16[3072,64]{0,1:T(8,128)(2,1)} %param.29) | copy-start | bytes 1179652
  77.3 7.0 %copy-start.8 = (f32[1,144,64]{1,2,0:T(8,128)S(1)}, f32[1,144,64]{1,2,0:T(8,128)}, u32[]{:S(2)}) copy-start(f32[1,144,64]{1,2,0:T(8,128)} %param.31) | copy-start | bytes 110596
  77.3 7.0 %copy-start.9 = (f32[3072]{0:T(1024)S(1)}, f32[3072]{0:T(1024)}, u32[]{:S(2)}) copy-start(f32[3072]{0:T(1024)} %param.26) | copy-start | bytes 36868
  77.3 7.0 %copy-start.10 = (f32[3072]{0:T(1024)S(1)}, f32[3072]{0:T(1024)}, u32[]{:S(2)}) copy-start(f32[3072]{0:T(1024)} %param.27) | copy-start | bytes 36868
  77.3 7.0 %copy-start.11 = (f32[3072]{0:T(1024)S(1)}, f32[3072]{0:T(1024)}, u32[]{:S(2)}) copy-start(f32[3072]{0:T(1024)} %param.28) | copy-start | bytes 36868
  77.3 7.0 %copy-start.13 = (s32[2,144]{1,0:T(2,128)S(1)}, s32[2,144]{1,0:T(2,128)}, u32[]{:S(2)}) copy-start(s32[2,144]{1,0:T(2,128)} %constant.36.clone.local_ref) | copy-start | bytes 3460
  77.3 7.0 %copy-start.16 = (f32[64]{0:T(128)S(1)}, f32[64]{0:T(128)}, u32[]{:S(2)}) copy-start(f32[64]{0:T(128)} %param.30) | copy-start | bytes 772
  78.5 5.9 %collective-permute-start.2 = (bf16[144,3072]{1,0:T(8,128)(2,1)S(1)}, bf16[144,3072]{1,0:T(8,128)(2,1)S(1)}, u32[]{:S(2)}, u32[]{:S(2)}) collective-permute-start(bf16[144,3072]{1,0:T(8,128)(2,1)S(1)} %project.1.own_ref), channel_id=1, source_target_pairs={{0,1},{1,0},{2,3},{3,2},{4,5},{5,4},{6,7},{7,6},{8,9},{9,8},{10,11... | collective-permute-start | bytes 2654216 | tf_op jit(solution)/shard_map/ppermute | solution.py:309

commit v3 on v2

--- a/solution.py
+++ b/solution.py
@@ -18,6 +18,9 @@
 PIX = TILE_H * TILE_W
 SLOTS = 32
 KEYS = PIX + SLOTS
+EARLY = 128
+LATE = PIX - EARLY
+SENT = KEYS + SLOTS + LATE
 GROUP = 8
 HALF_KEYS = GROUP * KEYS
 DEAD = -1e30
@@ -89,9 +92,9 @@
         out_ref[head, 0:PIX, :] = rotated(image_ref[0, :, lanes], q_gain_ref[...])
         out_ref[head, PIX : 2 * PIX, :] = rotated(image_ref[1, :, lanes], k_gain_ref[...])
         out_ref[head, 2 * PIX : PIX + KEYS, :] = normed(text_keys[:, lanes], k_gain_ref[...]).astype(jnp.bfloat16)
-        for ref, start in ((out_ref, PIX + KEYS), (value_ref, 0)):
-            ref[head, start : start + PIX, :] = image_ref[2, :, lanes]
-            ref[head, start + PIX : start + KEYS, :] = text_values[:, lanes]
+        out_ref[head, PIX + KEYS : PIX + KEYS + SLOTS, :] = text_values[:, lanes]
+        out_ref[head, PIX + KEYS + SLOTS :, :] = image_ref[2, :, lanes]
+        value_ref[head] = image_ref[2, LATE:, lanes]
 
 
 def key_bias(table_ref, size_ref, text_len_ref, half):
@@ -108,16 +111,20 @@
 
 
 def stage(keys_ref, key_start, values_ref, value_start, key_s, value_s):
+    text_start = key_start + KEYS
+    late_start = text_start + SLOTS
     for tile in range(GROUP):
         at = tile * KEYS
-        key_s[at : at + KEYS, :] = keys_ref[tile, key_start : key_start + KEYS, :]
-        value_s[at : at + KEYS, 0:HEAD] = values_ref[tile, value_start : value_start + KEYS, :]
+        key_s[at : at + KEYS, :] = keys_ref[tile, key_start:text_start, :]
+        value_s[at : at + LATE, 0:HEAD] = keys_ref[tile, late_start : late_start + LATE, :]
+        value_s[at + LATE : at + PIX, 0:HEAD] = values_ref[tile, value_start : value_start + EARLY, :]
+        value_s[at + PIX : at + KEYS, 0:HEAD] = keys_ref[tile, text_start:late_start, :]
     value_s[:, HEAD:] = jnp.ones((HALF_KEYS, HEAD), jnp.bfloat16)
 
 
 def local_kernel(half_ref, size_ref, text_len_ref, table_ref, own_ref, acc_ref, peak_ref, key_s, value_s):
     bias = key_bias(table_ref, size_ref, text_len_ref, half_ref[0])
-    stage(own_ref, PIX, own_ref, PIX + KEYS, key_s, value_s)
+    stage(own_ref, PIX, own_ref, PIX + SENT, key_s, value_s)
     for tile in range(GROUP):
         scores = scores_of(own_ref[tile, 0:PIX, :], key_s[...], bias)
         peak = jnp.max(scores, axis=1, keepdims=True)
@@ -143,9 +150,19 @@
         out_ref[tile] = (blended / total).astype(jnp.bfloat16)
 
 
-def project_kernel(attended_ref, weight_ref, out_ref):
+def project_kernel(attended_ref, weight_ref, out_ref, weight_s, sems):
+    chunks = sems.shape[0]
+    columns = weight_s.shape[1] // chunks
+    copies = []
+    for chunk in range(chunks):
+        part = pl.ds(chunk * columns, columns)
+        copies.append(pltpu.make_async_copy(weight_ref.at[:, part], weight_s.at[:, part], sems.at[chunk]))
+        copies[chunk].start()
     attended = jnp.concatenate([attended_ref[head] for head in range(GROUP)], axis=1)
-    out_ref[...] = jnp.dot(attended, weight_ref[...], preferred_element_type=jnp.float32).astype(jnp.bfloat16)
+    for chunk in range(chunks):
+        part = slice(chunk * columns, (chunk + 1) * columns)
+        copies[chunk].wait()
+        out_ref[:, part] = jnp.dot(attended, weight_s[:, part], preferred_element_type=jnp.float32).astype(jnp.bfloat16)
 
 
 def final_kernel(
@@ -259,21 +276,18 @@
             ],
             out_specs=(
                 pl.BlockSpec((per_step, PIX + 2 * KEYS, HEAD), lambda i, tile_ref: (i, 0, 0)),
-                pl.BlockSpec((per_step, KEYS, HEAD), lambda i, tile_ref: (i, 0, 0)),
+                pl.BlockSpec((per_step, EARLY, HEAD), lambda i, tile_ref: (i, 0, 0)),
             ),
         ),
         out_shape=(
             jax.ShapeDtypeStruct((GROUP, PIX + 2 * KEYS, HEAD), bf16),
-            jax.ShapeDtypeStruct((GROUP, KEYS, HEAD), bf16),
+            jax.ShapeDtypeStruct((GROUP, EARLY, HEAD), bf16),
         ),
-        compiler_params=params(8),
         name="prepare",
     )(tile, triple, text_kv, q_gain.reshape(1, HEAD), k_gain.reshape(1, HEAD), jnp.asarray(rope_tables()))
     far_values = lax.ppermute(values, "tile", across)
     own = lax.all_to_all(prepared, "tile", 0, 0, axis_index_groups=groups, tiled=True)
-    far_keys = lax.ppermute(own[:, PIX : PIX + KEYS, :], "tile", across)
-    far_values = lax.all_to_all(far_values, "tile", 0, 0, axis_index_groups=groups, tiled=True)
-
+    far_keys = lax.ppermute(own[:, PIX : PIX + SENT, :], "tile", across)
     table = jnp.asarray(key_tables())
     acc, peak = pl.pallas_call(
         local_kernel,
@@ -287,6 +301,8 @@
         compiler_params=params(16),
         name="attend_local",
     )(half, image_size, text_len, table, own)
+    far_values, peak = lax.optimization_barrier((far_values, peak))
+    far_values = lax.all_to_all(far_values, "tile", 0, 0, axis_index_groups=groups, tiled=True)
     attended = pl.pallas_call(
         remote_kernel,
         in_specs=[SMEM, SMEM, SMEM] + [VMEM] * 6,
@@ -300,10 +316,11 @@
 
     partial = pl.pallas_call(
         project_kernel,
-        in_specs=[VMEM, VMEM],
+        in_specs=[VMEM, HBM],
         out_specs=VMEM,
         out_shape=jax.ShapeDtypeStruct((PIX, model), bf16),
-        compiler_params=params(16),
+        scratch_shapes=[pltpu.VMEM((width, model), bf16), pltpu.SemaphoreType.DMA((6,))],
+        compiler_params=params(48),
         name="project",
     )(attended, out_weight)
     other = lax.ppermute(partial, "tp", [(0, 1), (1, 0)])

time: 87.3 us -> 80.6 us (0.923)
  local copies, waits for them, and re-layouts: 8.64 us -> 1.55 us
  Pallas kernels: 13.5 us -> 17.4 us
  starting transfers between devices: 20.2 us -> 18.9 us
  blocking collectives: 10.5 us -> 9.3 us
  waiting for transfers between devices: 32 us -> 31 us
    ppermute x1, waiting for transfers between devices: 15.2 us -> 0.01 us  [shards(): far_values = lax.ppermute(values, 'tile', across)]
    all_to_all x1, waiting for transfers between devices: 1.93 us -> 14.4 us  [shards(): lax.all_to_all(prepared, 'tile', 0, 0, axis_index_groups=groups, tiled=True)]
    unnamed x34 -> x24, local copies, waits for them, and re-layouts: 7.88 us -> 0.75 us
    pallas_call x1, Pallas kernels: 1.09 us -> 3.4 us  [shards(): pl.pallas_call(project_kernel, in_specs=[VMEM, HBM], out_specs=VMEM, out_...]
    all_to_all x1, waiting for transfers between devices: 1.69 us -> 3.44 us  [shards(): lax.all_to_all(far_values, 'tile', 0, 0, axis_index_groups=groups, tiled=...]
    pallas_call x1, Pallas kernels: 3.39 us -> 4.72 us  [shards(): pl.pallas_call(prepare_kernel, grid_spec=pltpu.PrefetchScalarGridSpec(num...]
    all_to_all x1, blocking collectives: 10.5 us -> 9.3 us  [shards(): lax.all_to_all(attended, 'tile', 0, 0, axis_index_groups=groups, tiled=True)]
    ppermute x1, starting transfers between devices: 3.81 us -> 2.67 us  [shards(): other = lax.ppermute(partial, 'tp', [(0, 1), (1, 0)])]
  transfers between devices with their start and end apart: 5 -> 5, of which waited for: 5 -> 4; matrix products, arithmetic and copies ran while one was open for 1% -> 1% of each run, Pallas kernels for 4% -> 4%
where the time goes in v3:
time: 80.6 us; the launch traced here: 80.2 us
  waiting for transfers between devices  31 us (38%)
  starting transfers between devices  18.9 us (23%)
  Pallas kernels  17.4 us (22%)
  blocking collectives  9.3 us (12%)
  between operations  2.09 us (3%)
  local copies, waits for them, and re-layouts  1.55 us (2%)
    all_to_all x1, waiting for transfers between devices, shards(): lax.all_to_all(prepared, 'tile', 0, 0, axis_index_groups=groups, tiled=True)  14.4 us
    ppermute x1, waiting for transfers between devices, shards(): far_keys = lax.ppermute(own[:, PIX:PIX + SENT, :], 'tile', across)  11.8 us
    all_to_all x1, blocking collectives, shards(): lax.all_to_all(attended, 'tile', 0, 0, axis_index_groups=groups, tiled=True)  9.3 us
    all_to_all x1, starting transfers between devices, shards(): lax.all_to_all(prepared, 'tile', 0, 0, axis_index_groups=groups, tiled=True)  6.37 us
    all_to_all x1, starting transfers between devices, shards(): lax.all_to_all(far_values, 'tile', 0, 0, axis_index_groups=groups, tiled=...  5.74 us
    pallas_call x1, Pallas kernels, shards(): pl.pallas_call(prepare_kernel, grid_spec=pltpu.PrefetchScalarGridSpec(num...  4.72 us
    all_to_all x1, waiting for transfers between devices, shards(): lax.all_to_all(far_values, 'tile', 0, 0, axis_index_groups=groups, tiled=...  3.44 us
    pallas_call x1, Pallas kernels, shards(): pl.pallas_call(remote_kernel, in_specs=[SMEM, SMEM, SMEM] + [VMEM] * 6, o...  3.43 us
  transfers between devices with their start and end apart: 5, of which 4 were waited for; matrix products, arithmetic and copies ran while one was open for 1% of the time, Pallas kernels for 4%

profile of v3, /device:TPU:1, one launch (start us, length us, event | category | flops | bytes accessed | tf_op | source)
XLA Modules:
  0.0 80.2 jit_solution(12484348476891822020)
XLA Ops:
  0.6 0.0 copy-start.3
  0.6 0.0 copy-start.8
  0.7 4.7 %prepare.1 = (bf16[8,496,128]{2,1,0:T(8,128)(2,1)}, bf16[8,128,128]{2,1,0:T(8,128)(2,1)}) custom-call(s32[1]{0:T(128)} %bitcast.tile_ref, bf16[3,144,1024]{2,1,0:T(8,128)(2,1)} %bitcast.30, bf16[32,2,1024]{2,1,0:T(2,128)(2,1)} %text_ref.1, f32[1,128]{1,0:T(1,128)} %bitcast.31, f32[1,128]{1,0:T(1,128)} %bitcast.32, f32[16,2,144,128]{3,2,1,0:T(8,128)} %constant.34.clone.table_ref), custom_call_target="tpu_custom_call" | custom-call | tf_op jit(solution)/shard_map/prepare/pallas_call | solution.py:265
  5.4 6.4 %all-to-all-start = ((bf16[8,496,128]{2,1,0:T(8,128)(2,1)}), bf16[8,496,128]{2,1,0:T(8,128)(2,1)S(1)}, u32[]{:S(2)}, u32[]{:S(2)}) async-start(bf16[8,496,128]{2,1,0:T(8,128)(2,1)} %get-tuple-element.10), calls=%async_computation | async-start | bytes 2031616 | tf_op jit(solution)/shard_map/all_to_all | solution.py:289
  11.8 3.0 %collective-permute-start.1 = (bf16[8,128,128]{2,1,0:T(8,128)(2,1)}, bf16[8,128,128]{2,1,0:T(8,128)(2,1)S(1)}, u32[]{:S(2)}, u32[]{:S(2)}) collective-permute-start(bf16[8,128,128]{2,1,0:T(8,128)(2,1)} %get-tuple-element.11), channel_id=1, source_target_pairs={{0,16},{2,18},{4,20},{6,22},{8,24},{10,26},{12,28},{14,30},{16,0},... | collective-permute-start | bytes 786440 | tf_op jit(solution)/shard_map/ppermute | solution.py:288
  15.4 14.4 %all-to-all-done.own_ref = bf16[8,496,128]{2,1,0:T(8,128)(2,1)S(1)} async-done(((bf16[8,496,128]{2,1,0:T(8,128)(2,1)}), bf16[8,496,128]{2,1,0:T(8,128)(2,1)S(1)}, u32[]{:S(2)}, u32[]{:S(2)}) %all-to-all-start) | async-done | bytes 1015840 | tf_op jit(solution)/shard_map/all_to_all | solution.py:289
  29.8 0.8 slice.4
  30.6 1.1 %collective-permute-start = (bf16[8,224,128]{2,1,0:T(8,128)(2,1)}, bf16[8,224,128]{2,1,0:T(8,128)(2,1)S(1)}, u32[]{:S(2)}, u32[]{:S(2)}) collective-permute-start(bf16[8,224,128]{2,1,0:T(8,128)(2,1)} %slice.4), channel_id=1, source_target_pairs={{0,16},{2,18},{4,20},{6,22},{8,24},{10,26},{12,28},{14,30},{16,0},... | collective-permute-start | bytes 1376264 | tf_op jit(solution)/shard_map/ppermute | solution.py:290
  31.7 0.0 copy-done.3
  31.7 0.0 copy-done.8
  31.7 3.4 %attend_local.1 = (f32[8,144,256]{2,1,0:T(8,128)S(1)}, f32[8,144,128]{2,1,0:T(8,128)S(1)}) custom-call(s32[1]{0:T(128)S(6)} %select_n.5.half_ref, s32[2]{0:T(128)S(1)} %copy-done.8, s32[1]{0:T(128)S(6)} %copy.21.text_len_ref, s32[3,1408]{1,0:T(4,128)S(1)} %copy-done.3, bf16[8,496,128]{2,1,0:T(8,128)(2,1)S(1)} %all-to-all-done.own_ref), custom_call_target="tpu_custom_call" | custom-call | tf_op jit(solution)/shard_map/attend_local/pallas_call | solution.py:292
  35.1 0.0 collective-permute-done.1
  35.1 0.0 copy-start.11
  35.1 0.7 copy-done.11
  35.8 5.7 %all-to-all-start.1 = ((bf16[8,128,128]{2,1,0:T(8,128)(2,1)}), bf16[8,128,128]{2,1,0:T(8,128)(2,1)S(1)}, u32[]{:S(2)}, u32[]{:S(2)}) async-start(bf16[8,128,128]{2,1,0:T(8,128)(2,1)} %copy-done.11), calls=%async_computation.1 | async-start | bytes 524288 | tf_op jit(solution)/shard_map/all_to_all | solution.py:305
  41.5 11.8 %collective-permute-done.keys_ref = bf16[8,224,128]{2,1,0:T(8,128)(2,1)S(1)} collective-permute-done((bf16[8,224,128]{2,1,0:T(8,128)(2,1)}, bf16[8,224,128]{2,1,0:T(8,128)(2,1)S(1)}, u32[]{:S(2)}, u32[]{:S(2)}) %collective-permute-start) | collective-permute-done | bytes 458784 | tf_op jit(solution)/shard_map/ppermute | solution.py:290
  53.4 3.4 %all-to-all-done.1.values_ref = bf16[8,128,128]{2,1,0:T(8,128)(2,1)S(1)} async-done(((bf16[8,128,128]{2,1,0:T(8,128)(2,1)}), bf16[8,128,128]{2,1,0:T(8,128)(2,1)S(1)}, u32[]{:S(2)}, u32[]{:S(2)}) %all-to-all-start.1) | async-done | bytes 262176 | tf_op jit(solution)/shard_map/all_to_all | solution.py:305
  56.8 3.4 %attend_far.1 = bf16[8,144,128]{2,1,0:T(8,128)(2,1)S(1)} custom-call(s32[1]{0:T(128)S(6)} %select_n.5.half_ref, s32[2]{0:T(128)S(1)} %copy-done.8, s32[1]{0:T(128)S(6)} %copy.21.text_len_ref, s32[3,1408]{1,0:T(4,128)S(1)} %copy-done.3, bf16[8,496,128]{2,1,0:T(8,128)(2,1)S(1)} %all-to-all-done.own_ref, ...), custom_call_target="tpu_custom_call" | custom-call | tf_op jit(solution)/shard_map/attend_far/pallas_call | solution.py:306
  60.2 9.3 %all_to_all.15.attended_ref = bf16[8,144,128]{2,1,0:T(8,128)(2,1)S(1)} all-to-all(bf16[8,144,128]{2,1,0:T(8,128)(2,1)S(1)} %attend_far.1), channel_id=1, replica_groups={{0,2,4,6,8,10,12,14},{16,18,20,22,24,26,28,30},{1,3,5,7,9,11,13,15},{17..., dimensions={0} | all-to-all | bytes 589824 | tf_op jit(solution)/shard_map/all_to_all | solution.py:315
  69.5 0.0 copy-start
  69.5 0.0 copy-start.1
  69.5 0.0 copy-start.2
  69.5 0.0 copy-start.4
  69.5 0.0 copy-start.5
  69.5 0.0 copy-start.6
  69.6 0.0 copy-start.7
  69.6 0.0 copy-start.9
  69.6 0.0 copy-start.10
  69.6 3.4 %project.1.own_ref = bf16[144,3072]{1,0:T(8,128)(2,1)S(1)} custom-call(bf16[8,144,128]{2,1,0:T(8,128)(2,1)S(1)} %all_to_all.15.attended_ref, bf16[1024,3072]{1,0:T(8,128)(2,1)} %weight_ref.1), custom_call_target="tpu_custom_call" | custom-call | tf_op jit(solution)/shard_map/project/pallas_call | solution.py:317
  73.0 2.7 %collective-permute-start.2 = (bf16[144,3072]{1,0:T(8,128)(2,1)S(1)}, bf16[144,3072]{1,0:T(8,128)(2,1)S(1)}, u32[]{:S(2)}, u32[]{:S(2)}) collective-permute-start(bf16[144,3072]{1,0:T(8,128)(2,1)S(1)} %project.1.own_ref), channel_id=1, source_target_pairs={{0,1},{1,0},{2,3},{3,2},{4,5},{5,4},{6,7},{7,6},{8,9},{9,8},{10,11... | collective-permute-start | bytes 2654216 | tf_op jit(solution)/shard_map/ppermute | solution.py:326
  76.3 1.4 %collective-permute-done.2.other_ref = bf16[144,3072]{1,0:T(8,128)(2,1)S(1)} collective-permute-done((bf16[144,3072]{1,0:T(8,128)(2,1)S(1)}, bf16[144,3072]{1,0:T(8,128)(2,1)S(1)}, u32[]{:S(2)}, u32[]{:S(2)}) %collective-permute-start.2) | collective-permute-done | bytes 884768 | tf_op jit(solution)/shard_map/ppermute | solution.py:326
  77.7 0.0 copy-done
  77.7 0.0 copy-done.1
  77.7 0.0 copy-done.2
  77.7 0.0 copy-done.4
  77.7 0.0 copy-done.5
  77.8 0.0 copy-done.6
  77.8 0.0 copy-done.7
  77.8 0.0 copy-done.9
  77.8 0.0 copy-done.10
  77.8 2.5 %final_layer.1 = (f32[64,144]{1,0:T(8,128)}, f32[64,144]{1,0:T(8,128)}) custom-call(s32[1]{0:T(128)} %bitcast.tile_ref, s32[2]{0:T(128)S(1)} %copy-done.8, s32[1]{0:T(128)S(6)} %copy.22.timestep_ref, s32[2,144]{1,0:T(2,128)S(1)} %copy-done.9, bf16[144,3072]{1,0:T(8,128)(2,1)S(1)} %project.1.own_ref, bf16[144,3072]{1,0:T(8,128)(2,1)S(1)} %collective-permute-done.2.other_ref, ...), custom_call_target="tpu_custom_call" | custom-call | tf_op jit(solution)/shard_map/final_layer/pallas_call | solution.py:329
Async XLA Ops:
  0.6 31.1 %copy-start.3 = (s32[3,1408]{1,0:T(4,128)S(1)}, s32[3,1408]{1,0:T(4,128)}, u32[]{:S(2)}) copy-start(s32[3,1408]{1,0:T(4,128)} %constant.35.clone.table_ref) | copy-start | bytes 50692
  0.6 31.1 %copy-start.8 = (s32[2]{0:T(128)S(1)}, s32[2]{0:T(128)}, u32[]{:S(2)}) copy-start(s32[2]{0:T(128)} %size_ref.5) | copy-start | bytes 28
  5.4 24.4 %all-to-all-start = ((bf16[8,496,128]{2,1,0:T(8,128)(2,1)}), bf16[8,496,128]{2,1,0:T(8,128)(2,1)S(1)}, u32[]{:S(2)}, u32[]{:S(2)}) async-start(bf16[8,496,128]{2,1,0:T(8,128)(2,1)} %get-tuple-element.10), calls=%async_computation | async-start | bytes 2031616 | tf_op jit(solution)/shard_map/all_to_all | solution.py:289
  11.8 23.3 %collective-permute-start.1 = (bf16[8,128,128]{2,1,0:T(8,128)(2,1)}, bf16[8,128,128]{2,1,0:T(8,128)(2,1)S(1)}, u32[]{:S(2)}, u32[]{:S(2)}) collective-permute-start(bf16[8,128,128]{2,1,0:T(8,128)(2,1)} %get-tuple-element.11), channel_id=1, source_target_pairs={{0,16},{2,18},{4,20},{6,22},{8,24},{10,26},{12,28},{14,30},{16,0},... | collective-permute-start | bytes 786440 | tf_op jit(solution)/shard_map/ppermute | solution.py:288
  30.6 22.8 %collective-permute-start = (bf16[8,224,128]{2,1,0:T(8,128)(2,1)}, bf16[8,224,128]{2,1,0:T(8,128)(2,1)S(1)}, u32[]{:S(2)}, u32[]{:S(2)}) collective-permute-start(bf16[8,224,128]{2,1,0:T(8,128)(2,1)} %slice.4), channel_id=1, source_target_pairs={{0,16},{2,18},{4,20},{6,22},{8,24},{10,26},{12,28},{14,30},{16,0},... | collective-permute-start | bytes 1376264 | tf_op jit(solution)/shard_map/ppermute | solution.py:290
  35.1 0.7 copy-start.11
  35.8 21.0 %all-to-all-start.1 = ((bf16[8,128,128]{2,1,0:T(8,128)(2,1)}), bf16[8,128,128]{2,1,0:T(8,128)(2,1)S(1)}, u32[]{:S(2)}, u32[]{:S(2)}) async-start(bf16[8,128,128]{2,1,0:T(8,128)(2,1)} %copy-done.11), calls=%async_computation.1 | async-start | bytes 524288 | tf_op jit(solution)/shard_map/all_to_all | solution.py:305
  69.5 8.2 %copy-start = (bf16[1,144,3072]{2,1,0:T(8,128)(2,1)S(1)}, bf16[1,144,3072]{2,1,0:T(8,128)(2,1)}, u32[]{:S(2)}) copy-start(bf16[1,144,3072]{2,1,0:T(8,128)(2,1)} %param.24) | copy-start | bytes 2654212
  69.5 8.2 %copy-start.1 = (bf16[1,144,3072]{2,1,0:T(8,128)(2,1)S(1)}, bf16[1,144,3072]{2,1,0:T(8,128)(2,1)}, u32[]{:S(2)}) copy-start(bf16[1,144,3072]{2,1,0:T(8,128)(2,1)} %param.25) | copy-start | bytes 2654212
  69.5 8.2 %copy-start.2 = (bf16[3072,64]{0,1:T(8,128)(2,1)S(1)}, bf16[3072,64]{0,1:T(8,128)(2,1)}, u32[]{:S(2)}) copy-start(bf16[3072,64]{0,1:T(8,128)(2,1)} %param.29) | copy-start | bytes 1179652
  69.5 8.2 %copy-start.4 = (f32[1,144,64]{1,2,0:T(8,128)S(1)}, f32[1,144,64]{1,2,0:T(8,128)}, u32[]{:S(2)}) copy-start(f32[1,144,64]{1,2,0:T(8,128)} %param.31) | copy-start | bytes 110596
  69.5 8.2 %copy-start.5 = (f32[3072]{0:T(1024)S(1)}, f32[3072]{0:T(1024)}, u32[]{:S(2)}) copy-start(f32[3072]{0:T(1024)} %param.26) | copy-start | bytes 36868
  69.5 8.2 %copy-start.6 = (f32[3072]{0:T(1024)S(1)}, f32[3072]{0:T(1024)}, u32[]{:S(2)}) copy-start(f32[3072]{0:T(1024)} %param.27) | copy-start | bytes 36868
  69.6 8.2 %copy-start.7 = (f32[3072]{0:T(1024)S(1)}, f32[3072]{0:T(1024)}, u32[]{:S(2)}) copy-start(f32[3072]{0:T(1024)} %param.28) | copy-start | bytes 36868
  69.6 8.2 %copy-start.9 = (s32[2,144]{1,0:T(2,128)S(1)}, s32[2,144]{1,0:T(2,128)}, u32[]{:S(2)}) copy-start(s32[2,144]{1,0:T(2,128)} %constant.36.clone.local_ref) | copy-start | bytes 3460
  69.6 8.2 %copy-start.10 = (f32[64]{0:T(128)S(1)}, f32[64]{0:T(128)}, u32[]{:S(2)}) copy-start(f32[64]{0:T(128)} %param.30) | copy-start | bytes 772
  73.0 4.7 %collective-permute-start.2 = (bf16[144,3072]{1,0:T(8,128)(2,1)S(1)}, bf16[144,3072]{1,0:T(8,128)(2,1)S(1)}, u32[]{:S(2)}, u32[]{:S(2)}) collective-permute-start(bf16[144,3072]{1,0:T(8,128)(2,1)S(1)} %project.1.own_ref), channel_id=1, source_target_pairs={{0,1},{1,0},{2,3},{3,2},{4,5},{5,4},{6,7},{7,6},{8,9},{9,8},{10,11... | collective-permute-start | bytes 2654216 | tf_op jit(solution)/shard_map/ppermute | solution.py:326

commit v4 on v3

--- a/solution.py
+++ b/solution.py
@@ -18,9 +18,6 @@
 PIX = TILE_H * TILE_W
 SLOTS = 32
 KEYS = PIX + SLOTS
-EARLY = 128
-LATE = PIX - EARLY
-SENT = KEYS + SLOTS + LATE
 GROUP = 8
 HALF_KEYS = GROUP * KEYS
 DEAD = -1e30
@@ -55,16 +52,30 @@
     return np.stack([cosine, sine], axis=1).astype(np.float32)
 
 
+def group_tiles():
+    lows = np.arange(TILES // GRID_X)[:, None] * GRID_X
+    kinds = [
+        [np.arange(GROUP), np.arange(GROUP) + GROUP],
+        [(lows + np.array([0, 1])).reshape(-1), (lows + np.array([3, 2])).reshape(-1)],
+    ]
+    partners = np.zeros((2, TILES), np.int64)
+    for kind, (near, far) in enumerate(kinds):
+        partners[kind, near] = far
+        partners[kind, far] = near
+    return kinds, partners
+
+
 def key_tables():
     row, col = position_tables()
-    row = row[:GROUP]
-    col = col[:GROUP]
     far = np.full((GROUP, SLOTS), 1 << 20)
-    slot = np.arange(GROUP * SLOTS).reshape(GROUP, SLOTS)
-    key_row = np.concatenate([row, far], axis=1).reshape(1, HALF_KEYS)
-    key_col = np.concatenate([col, far], axis=1).reshape(1, HALF_KEYS)
-    key_slot = np.concatenate([np.full((GROUP, PIX), 1 << 20), slot], axis=1).reshape(1, HALF_KEYS)
-    return np.concatenate([key_row, key_col, key_slot], axis=0).astype(np.int32)
+    beyond = np.full((GROUP, PIX), 1 << 20)
+    tables = []
+    for kind in group_tiles()[0]:
+        for tiles in kind:
+            slot = tiles[:, None] * SLOTS + np.arange(SLOTS)[None, :]
+            parts = ((row[tiles], far), (col[tiles], far), (beyond, slot))
+            tables.append(np.stack([np.concatenate(part, axis=1).reshape(HALF_KEYS) for part in parts]))
+    return np.stack(tables).astype(np.int32)
 
 
 def normed(vectors, gain):
@@ -73,7 +84,7 @@
 
 
 def prepare_kernel(
-    tile_ref, image_ref, text_ref, q_gain_ref, k_gain_ref, table_ref, out_ref, value_ref
+    tile_ref, image_ref, text_ref, q_gain_ref, k_gain_ref, table_ref, out_ref
 ):
     cosine = table_ref[0, 0]
     sine = table_ref[0, 1]
@@ -92,16 +103,13 @@
         out_ref[head, 0:PIX, :] = rotated(image_ref[0, :, lanes], q_gain_ref[...])
         out_ref[head, PIX : 2 * PIX, :] = rotated(image_ref[1, :, lanes], k_gain_ref[...])
         out_ref[head, 2 * PIX : PIX + KEYS, :] = normed(text_keys[:, lanes], k_gain_ref[...]).astype(jnp.bfloat16)
-        out_ref[head, PIX + KEYS : PIX + KEYS + SLOTS, :] = text_values[:, lanes]
-        out_ref[head, PIX + KEYS + SLOTS :, :] = image_ref[2, :, lanes]
-        value_ref[head] = image_ref[2, LATE:, lanes]
-
-
-def key_bias(table_ref, size_ref, text_len_ref, half):
-    rows = size_ref[0] - half * (CANVAS // 2)
-    slots = text_len_ref[0] - half * (GROUP * SLOTS)
-    image_ok = (table_ref[0:1, :] < rows) & (table_ref[1:2, :] < size_ref[1])
-    text_ok = table_ref[2:3, :] < slots
+        out_ref[head, PIX + KEYS : 2 * PIX + KEYS, :] = image_ref[2, :, lanes]
+        out_ref[head, 2 * PIX + KEYS :, :] = text_values[:, lanes]
+
+
+def key_bias(table_ref, size_ref, text_len_ref, group):
+    image_ok = (table_ref[group, 0:1, :] < size_ref[0]) & (table_ref[group, 1:2, :] < size_ref[1])
+    text_ok = table_ref[group, 2:3, :] < text_len_ref[0]
     return jnp.where(image_ok | text_ok, 0.0, DEAD)
 
 
@@ -110,21 +118,17 @@
     return scores + bias
 
 
-def stage(keys_ref, key_start, values_ref, value_start, key_s, value_s):
-    text_start = key_start + KEYS
-    late_start = text_start + SLOTS
+def stage(source_ref, start, key_s, value_s):
     for tile in range(GROUP):
-        at = tile * KEYS
-        key_s[at : at + KEYS, :] = keys_ref[tile, key_start:text_start, :]
-        value_s[at : at + LATE, 0:HEAD] = keys_ref[tile, late_start : late_start + LATE, :]
-        value_s[at + LATE : at + PIX, 0:HEAD] = values_ref[tile, value_start : value_start + EARLY, :]
-        value_s[at + PIX : at + KEYS, 0:HEAD] = keys_ref[tile, text_start:late_start, :]
+        rows = slice(tile * KEYS, (tile + 1) * KEYS)
+        key_s[rows, :] = source_ref[tile, start : start + KEYS, :]
+        value_s[rows, 0:HEAD] = source_ref[tile, start + KEYS : start + 2 * KEYS, :]
     value_s[:, HEAD:] = jnp.ones((HALF_KEYS, HEAD), jnp.bfloat16)
 
 
-def local_kernel(half_ref, size_ref, text_len_ref, table_ref, own_ref, acc_ref, peak_ref, key_s, value_s):
-    bias = key_bias(table_ref, size_ref, text_len_ref, half_ref[0])
-    stage(own_ref, PIX, own_ref, PIX + SENT, key_s, value_s)
+def local_kernel(group_ref, size_ref, text_len_ref, table_ref, own_ref, acc_ref, peak_ref, key_s, value_s):
+    bias = key_bias(table_ref, size_ref, text_len_ref, group_ref[0])
+    stage(own_ref, PIX, key_s, value_s)
     for tile in range(GROUP):
         scores = scores_of(own_ref[tile, 0:PIX, :], key_s[...], bias)
         peak = jnp.max(scores, axis=1, keepdims=True)
@@ -134,10 +138,10 @@
 
 
 def remote_kernel(
-    half_ref, size_ref, text_len_ref, table_ref, own_ref, keys_ref, values_ref, acc_ref, peak_ref, out_ref, key_s, value_s
+    group_ref, size_ref, text_len_ref, table_ref, own_ref, far_ref, acc_ref, peak_ref, out_ref, key_s, value_s
 ):
-    bias = key_bias(table_ref, size_ref, text_len_ref, 1 - half_ref[0])
-    stage(keys_ref, 0, values_ref, 0, key_s, value_s)
+    bias = key_bias(table_ref, size_ref, text_len_ref, group_ref[1])
+    stage(far_ref, 0, key_s, value_s)
     for tile in range(GROUP):
         scores = scores_of(own_ref[tile, 0:PIX, :], key_s[...], bias)
         before = peak_ref[tile]
@@ -256,13 +260,17 @@
     model = hidden.shape[2]
     latents = final_weight.shape[1]
     tile = lax.axis_index("tile").astype(jnp.int32).reshape(1)
-    half = tile // GROUP
+    kind = lax.axis_index("tp").astype(jnp.int32)
+    which = jnp.where(kind == 0, tile[0] // GROUP, tile[0] % GRID_X // 2)
+    group = jnp.stack([2 * kind + which, 2 * kind + 1 - which])
     triple = image_qkv.reshape(PIX, 3, width).transpose(1, 0, 2)
-    groups = [list(range(GROUP)), list(range(GROUP, 2 * GROUP))]
-    across = [(t, (t + GROUP) % TILES) for t in range(TILES)]
+    kinds, partners = group_tiles()
+    mesh_axes = ("tile", "tp")
+    groups = [[int(t) * 2 + kind for t in tiles] for kind in range(2) for tiles in kinds[kind]]
+    across = [(t * 2 + kind, int(partners[kind, t]) * 2 + kind) for t in range(TILES) for kind in range(2)]
 
     per_step = 2
-    prepared, values = pl.pallas_call(
+    prepared = pl.pallas_call(
         prepare_kernel,
         grid_spec=pltpu.PrefetchScalarGridSpec(
             num_scalar_prefetch=1,
@@ -274,20 +282,14 @@
                 pl.BlockSpec((1, HEAD), lambda i, tile_ref: (0, 0)),
                 pl.BlockSpec((1, 2, PIX, HEAD), lambda i, tile_ref: (tile_ref[0], 0, 0, 0)),
             ],
-            out_specs=(
-                pl.BlockSpec((per_step, PIX + 2 * KEYS, HEAD), lambda i, tile_ref: (i, 0, 0)),
-                pl.BlockSpec((per_step, EARLY, HEAD), lambda i, tile_ref: (i, 0, 0)),
-            ),
+            out_specs=pl.BlockSpec((per_step, PIX + 2 * KEYS, HEAD), lambda i, tile_ref: (i, 0, 0)),
         ),
-        out_shape=(
-            jax.ShapeDtypeStruct((GROUP, PIX + 2 * KEYS, HEAD), bf16),
-            jax.ShapeDtypeStruct((GROUP, EARLY, HEAD), bf16),
-        ),
+        out_shape=jax.ShapeDtypeStruct((GROUP, PIX + 2 * KEYS, HEAD), bf16),
         name="prepare",
     )(tile, triple, text_kv, q_gain.reshape(1, HEAD), k_gain.reshape(1, HEAD), jnp.asarray(rope_tables()))
-    far_values = lax.ppermute(values, "tile", across)
-    own = lax.all_to_all(prepared, "tile", 0, 0, axis_index_groups=groups, tiled=True)
-    far_keys = lax.ppermute(own[:, PIX : PIX + SENT, :], "tile", across)
+    own = lax.all_to_all(prepared, mesh_axes, 0, 0, axis_index_groups=groups, tiled=True)
+    far = lax.ppermute(own[:, PIX:, :], mesh_axes, across)
+
     table = jnp.asarray(key_tables())
     acc, peak = pl.pallas_call(
         local_kernel,
@@ -300,19 +302,17 @@
         scratch_shapes=[pltpu.VMEM((HALF_KEYS, HEAD), bf16), pltpu.VMEM((HALF_KEYS, 2 * HEAD), bf16)],
         compiler_params=params(16),
         name="attend_local",
-    )(half, image_size, text_len, table, own)
-    far_values, peak = lax.optimization_barrier((far_values, peak))
-    far_values = lax.all_to_all(far_values, "tile", 0, 0, axis_index_groups=groups, tiled=True)
+    )(group, image_size, text_len, table, own)
     attended = pl.pallas_call(
         remote_kernel,
-        in_specs=[SMEM, SMEM, SMEM] + [VMEM] * 6,
+        in_specs=[SMEM, SMEM, SMEM] + [VMEM] * 5,
         out_specs=VMEM,
         out_shape=jax.ShapeDtypeStruct((GROUP, PIX, HEAD), bf16),
         scratch_shapes=[pltpu.VMEM((HALF_KEYS, HEAD), bf16), pltpu.VMEM((HALF_KEYS, 2 * HEAD), bf16)],
         compiler_params=params(16),
         name="attend_far",
-    )(half, image_size, text_len, table, own, far_keys, far_values, acc, peak)
-    attended = lax.all_to_all(attended, "tile", 0, 0, axis_index_groups=groups, tiled=True)
+    )(group, image_size, text_len, table, own, far, acc, peak)
+    attended = lax.all_to_all(attended, mesh_axes, 0, 0, axis_index_groups=groups, tiled=True)
 
     partial = pl.pallas_call(
         project_kernel,

time: 80.6 us -> 73 us (0.906)
  blocking collectives: 9.3 us -> 36.2 us
  waiting for transfers between devices: 31 us -> 6.93 us
  starting transfers between devices: 18.9 us -> 9.99 us
  local copies, waits for them, and re-layouts: 1.55 us -> 0.1 us
    all_to_all x1 -> x2, blocking collectives: 9.3 us -> 36.2 us  [the longest x1 26.2 us: shards(): lax.all_to_all(prepared, mesh_axes, 0, 0, axis_index_groups=groups, tiled...]
    all_to_all x2 -> x0, waiting for transfers between devices: 17.8 us -> none  [the longest x1 14.4 us: shards(): lax.all_to_all(prepared, 'tile', 0, 0, axis_index_groups=groups, tiled=True)]
    all_to_all x2 -> x0, starting transfers between devices: 12.1 us -> none  [the longest x1 6.37 us: shards(): lax.all_to_all(prepared, 'tile', 0, 0, axis_index_groups=groups, tiled=True)]
    ppermute x2 -> x1, waiting for transfers between devices: 11.8 us -> 5.53 us  [shards(): far = lax.ppermute(own[:, PIX:, :], mesh_axes, across)]
    ppermute x1, starting transfers between devices: 2.67 us -> 8 us  [shards(): other = lax.ppermute(partial, 'tp', [(0, 1), (1, 0)])]
    ppermute x2 -> x1, starting transfers between devices: 4.12 us -> 1.99 us  [shards(): far = lax.ppermute(own[:, PIX:, :], mesh_axes, across)]
  transfers between devices with their start and end apart: 5 -> 2, of which waited for: 4 -> 2; matrix products, arithmetic and copies ran while one was open for 1% -> 0% of each run, Pallas kernels for 4% -> 5%
where the time goes in v4:
time: 73 us; the launch traced here: 72.7 us
  blocking collectives  36.2 us (50%)
  Pallas kernels  17.3 us (24%)
  starting transfers between devices  9.99 us (14%)
  waiting for transfers between devices  6.93 us (9%)
  between operations  2.06 us (3%)
    all_to_all x1, blocking collectives, shards(): lax.all_to_all(prepared, mesh_axes, 0, 0, axis_index_groups=groups, tiled...  26.2 us
    all_to_all x1, blocking collectives, shards(): lax.all_to_all(attended, mesh_axes, 0, 0, axis_index_groups=groups, tiled...  10 us
    ppermute x1, starting transfers between devices, shards(): other = lax.ppermute(partial, 'tp', [(0, 1), (1, 0)])  8 us
    ppermute x1, waiting for transfers between devices, shards(): far = lax.ppermute(own[:, PIX:, :], mesh_axes, across)  5.53 us
    pallas_call x1, Pallas kernels, shards(): pl.pallas_call(prepare_kernel, grid_spec=pltpu.PrefetchScalarGridSpec(num...  4.73 us
    pallas_call x1, Pallas kernels, shards(): pl.pallas_call(project_kernel, in_specs=[VMEM, HBM], out_specs=VMEM, out_...  3.4 us
    pallas_call x1, Pallas kernels, shards(): pl.pallas_call(remote_kernel, in_specs=[SMEM, SMEM, SMEM] + [VMEM] * 5, o...  3.37 us
    pallas_call x1, Pallas kernels, shards(): pl.pallas_call(local_kernel, in_specs=[SMEM, SMEM, SMEM] + [VMEM] * 2, ou...  3.32 us
  transfers between devices with their start and end apart: 2, of which 2 were waited for; matrix products, arithmetic and copies ran while one was open for 0% of the time, Pallas kernels for 5%

profile of v4, /device:TPU:1, one launch (start us, length us, event | category | flops | bytes accessed | tf_op | source)
XLA Modules:
  0.0 72.7 jit_solution(16986534472775490480)
XLA Ops:
  0.6 4.7 %prepare.1 = bf16[8,496,128]{2,1,0:T(8,128)(2,1)} custom-call(s32[1]{0:T(128)} %bitcast.tile_ref, bf16[3,144,1024]{2,1,0:T(8,128)(2,1)} %bitcast.32, bf16[32,2,1024]{2,1,0:T(2,128)(2,1)} %text_ref.1, f32[1,128]{1,0:T(1,128)} %bitcast.33, f32[1,128]{1,0:T(1,128)} %bitcast.34, f32[16,2,144,128]{3,2,1,0:T(8,128)} %constant.53.clone.table_ref), custom_call_target="tpu_custom_call" | custom-call | tf_op jit(solution)/shard_map/prepare/pallas_call | solution.py:273
  5.4 0.0 copy-start.3
  5.4 0.0 copy-start.8
  5.4 26.2 %all_to_all.10.own_ref = bf16[8,496,128]{2,1,0:T(8,128)(2,1)S(1)} all-to-all(bf16[8,496,128]{2,1,0:T(8,128)(2,1)} %prepare.1), channel_id=1, replica_groups={{0,2,4,6,8,10,12,14},{16,18,20,22,24,26,28,30},{1,3,9,11,17,19,25,27},{..., dimensions={0} | all-to-all | bytes 2031616 | tf_op jit(solution)/shard_map/all_to_all | solution.py:290
  31.6 2.0 %collective-permute-start = (bf16[8,352,128]{2,1,0:T(8,128)(2,1)S(1)}, bf16[8,352,128]{2,1,0:T(8,128)(2,1)S(1)}, u32[]{:S(2)}, u32[]{:S(2)}) collective-permute-start(bf16[8,352,128]{2,1,0:T(8,128)(2,1)S(1)} %slice.4), channel_id=1, source_target_pairs={{0,16},{1,7},{2,18},{3,5},{4,20},{5,3},{6,22},{7,1},{8,24},{9,15},... | collective-permute-start | bytes 2162696 | tf_op jit(solution)/shard_map/ppermute | solution.py:291
  34.3 0.1 pad_add_fusion.group_ref
  34.4 0.0 copy-done.3
  34.4 0.0 copy-done.8
  34.4 3.3 %attend_local.1 = (f32[8,144,256]{2,1,0:T(8,128)S(1)}, f32[8,144,128]{2,1,0:T(8,128)S(1)}) custom-call(s32[2]{0:T(128)S(1)} %pad_add_fusion.group_ref, s32[2]{0:T(128)S(1)} %copy-done.8, s32[1]{0:T(128)S(6)} %copy.21.text_len_ref, s32[4,3,1408]{2,1,0:T(4,128)S(1)} %copy-done.3, bf16[8,496,128]{2,1,0:T(8,128)(2,1)S(1)} %all_to_all.10.own_ref), custom_call_target="tpu_custom_call" | custom-call | tf_op jit(solution)/shard_map/attend_local/pallas_call | solution.py:294
  37.7 5.5 %collective-permute-done.far_ref = bf16[8,352,128]{2,1,0:T(8,128)(2,1)S(1)} collective-permute-done((bf16[8,352,128]{2,1,0:T(8,128)(2,1)S(1)}, bf16[8,352,128]{2,1,0:T(8,128)(2,1)S(1)}, u32[]{:S(2)}, u32[]{:S(2)}) %collective-permute-start) | collective-permute-done | bytes 720928 | tf_op jit(solution)/shard_map/ppermute | solution.py:291
  43.2 3.4 %attend_far.1 = bf16[8,144,128]{2,1,0:T(8,128)(2,1)S(1)} custom-call(s32[2]{0:T(128)S(1)} %pad_add_fusion.group_ref, s32[2]{0:T(128)S(1)} %copy-done.8, s32[1]{0:T(128)S(6)} %copy.21.text_len_ref, s32[4,3,1408]{2,1,0:T(4,128)S(1)} %copy-done.3, bf16[8,496,128]{2,1,0:T(8,128)(2,1)S(1)} %all_to_all.10.own_ref, ...), custom_call_target="tpu_custom_call" | custom-call | tf_op jit(solution)/shard_map/attend_far/pallas_call | solution.py:306
  46.6 10.0 %all_to_all.11.attended_ref = bf16[8,144,128]{2,1,0:T(8,128)(2,1)S(1)} all-to-all(bf16[8,144,128]{2,1,0:T(8,128)(2,1)S(1)} %attend_far.1), channel_id=1, replica_groups={{0,2,4,6,8,10,12,14},{16,18,20,22,24,26,28,30},{1,3,9,11,17,19,25,27},{..., dimensions={0} | all-to-all | bytes 589824 | tf_op jit(solution)/shard_map/all_to_all | solution.py:315
  56.6 0.0 copy-start
  56.6 0.0 copy-start.1
  56.6 0.0 copy-start.2
  56.6 0.0 copy-start.4
  56.6 0.0 copy-start.5
  56.6 0.0 copy-start.6
  56.6 0.0 copy-start.7
  56.7 0.0 copy-start.9
  56.7 0.0 copy-start.10
  56.7 3.4 %project.1.own_ref = bf16[144,3072]{1,0:T(8,128)(2,1)S(1)} custom-call(bf16[8,144,128]{2,1,0:T(8,128)(2,1)S(1)} %all_to_all.11.attended_ref, bf16[1024,3072]{1,0:T(8,128)(2,1)} %weight_ref.1), custom_call_target="tpu_custom_call" | custom-call | tf_op jit(solution)/shard_map/project/pallas_call | solution.py:317
  60.1 8.0 %collective-permute-start.1 = (bf16[144,3072]{1,0:T(8,128)(2,1)S(1)}, bf16[144,3072]{1,0:T(8,128)(2,1)S(1)}, u32[]{:S(2)}, u32[]{:S(2)}) collective-permute-start(bf16[144,3072]{1,0:T(8,128)(2,1)S(1)} %project.1.own_ref), channel_id=1, source_target_pairs={{0,1},{1,0},{2,3},{3,2},{4,5},{5,4},{6,7},{7,6},{8,9},{9,8},{10,11... | collective-permute-start | bytes 2654216 | tf_op jit(solution)/shard_map/ppermute | solution.py:326
  68.7 1.4 %collective-permute-done.1.other_ref = bf16[144,3072]{1,0:T(8,128)(2,1)S(1)} collective-permute-done((bf16[144,3072]{1,0:T(8,128)(2,1)S(1)}, bf16[144,3072]{1,0:T(8,128)(2,1)S(1)}, u32[]{:S(2)}, u32[]{:S(2)}) %collective-permute-start.1) | collective-permute-done | bytes 884768 | tf_op jit(solution)/shard_map/ppermute | solution.py:326
  70.1 0.0 copy-done
  70.1 0.0 copy-done.1
  70.1 0.0 copy-done.2
  70.2 0.0 copy-done.4
  70.2 0.0 copy-done.5
  70.2 0.0 copy-done.6
  70.2 0.0 copy-done.7
  70.2 0.0 copy-done.9
  70.2 0.0 copy-done.10
  70.2 2.5 %final_layer.1 = (f32[64,144]{1,0:T(8,128)}, f32[64,144]{1,0:T(8,128)}) custom-call(s32[1]{0:T(128)} %bitcast.tile_ref, s32[2]{0:T(128)S(1)} %copy-done.8, s32[1]{0:T(128)S(6)} %copy.22.timestep_ref, s32[2,144]{1,0:T(2,128)S(1)} %copy-done.9, bf16[144,3072]{1,0:T(8,128)(2,1)S(1)} %project.1.own_ref, bf16[144,3072]{1,0:T(8,128)(2,1)S(1)} %collective-permute-done.1.other_ref, ...), custom_call_target="tpu_custom_call" | custom-call | tf_op jit(solution)/shard_map/final_layer/pallas_call | solution.py:329
  (1 shorter events, 0.0 us)
Async XLA Ops:
  5.4 29.0 %copy-start.3 = (s32[4,3,1408]{2,1,0:T(4,128)S(1)}, s32[4,3,1408]{2,1,0:T(4,128)}, u32[]{:S(2)}) copy-start(s32[4,3,1408]{2,1,0:T(4,128)} %constant.54.clone.table_ref) | copy-start | bytes 202756
  5.4 29.0 %copy-start.8 = (s32[2]{0:T(128)S(1)}, s32[2]{0:T(128)}, u32[]{:S(2)}) copy-start(s32[2]{0:T(128)} %size_ref.5) | copy-start | bytes 28
  31.6 11.6 %collective-permute-start = (bf16[8,352,128]{2,1,0:T(8,128)(2,1)S(1)}, bf16[8,352,128]{2,1,0:T(8,128)(2,1)S(1)}, u32[]{:S(2)}, u32[]{:S(2)}) collective-permute-start(bf16[8,352,128]{2,1,0:T(8,128)(2,1)S(1)} %slice.4), channel_id=1, source_target_pairs={{0,16},{1,7},{2,18},{3,5},{4,20},{5,3},{6,22},{7,1},{8,24},{9,15},... | collective-permute-start | bytes 2162696 | tf_op jit(solution)/shard_map/ppermute | solution.py:291
  56.6 13.5 %copy-start = (bf16[1,144,3072]{2,1,0:T(8,128)(2,1)S(1)}, bf16[1,144,3072]{2,1,0:T(8,128)(2,1)}, u32[]{:S(2)}) copy-start(bf16[1,144,3072]{2,1,0:T(8,128)(2,1)} %param.24) | copy-start | bytes 2654212
  56.6 13.5 %copy-start.1 = (bf16[1,144,3072]{2,1,0:T(8,128)(2,1)S(1)}, bf16[1,144,3072]{2,1,0:T(8,128)(2,1)}, u32[]{:S(2)}) copy-start(bf16[1,144,3072]{2,1,0:T(8,128)(2,1)} %param.25) | copy-start | bytes 2654212
  56.6 13.5 %copy-start.2 = (bf16[3072,64]{0,1:T(8,128)(2,1)S(1)}, bf16[3072,64]{0,1:T(8,128)(2,1)}, u32[]{:S(2)}) copy-start(bf16[3072,64]{0,1:T(8,128)(2,1)} %param.29) | copy-start | bytes 1179652
  56.6 13.5 %copy-start.4 = (f32[1,144,64]{1,2,0:T(8,128)S(1)}, f32[1,144,64]{1,2,0:T(8,128)}, u32[]{:S(2)}) copy-start(f32[1,144,64]{1,2,0:T(8,128)} %param.31) | copy-start | bytes 110596
  56.6 13.5 %copy-start.5 = (f32[3072]{0:T(1024)S(1)}, f32[3072]{0:T(1024)}, u32[]{:S(2)}) copy-start(f32[3072]{0:T(1024)} %param.26) | copy-start | bytes 36868
  56.6 13.5 %copy-start.6 = (f32[3072]{0:T(1024)S(1)}, f32[3072]{0:T(1024)}, u32[]{:S(2)}) copy-start(f32[3072]{0:T(1024)} %param.27) | copy-start | bytes 36868
  56.6 13.5 %copy-start.7 = (f32[3072]{0:T(1024)S(1)}, f32[3072]{0:T(1024)}, u32[]{:S(2)}) copy-start(f32[3072]{0:T(1024)} %param.28) | copy-start | bytes 36868
  56.7 13.5 %copy-start.9 = (s32[2,144]{1,0:T(2,128)S(1)}, s32[2,144]{1,0:T(2,128)}, u32[]{:S(2)}) copy-start(s32[2,144]{1,0:T(2,128)} %constant.55.clone.local_ref) | copy-start | bytes 3460
  56.7 13.5 %copy-start.10 = (f32[64]{0:T(128)S(1)}, f32[64]{0:T(128)}, u32[]{:S(2)}) copy-start(f32[64]{0:T(128)} %param.30) | copy-start | bytes 772
  60.1 10.1 %collective-permute-start.1 = (bf16[144,3072]{1,0:T(8,128)(2,1)S(1)}, bf16[144,3072]{1,0:T(8,128)(2,1)S(1)}, u32[]{:S(2)}, u32[]{:S(2)}) collective-permute-start(bf16[144,3072]{1,0:T(8,128)(2,1)S(1)} %project.1.own_ref), channel_id=1, source_target_pairs={{0,1},{1,0},{2,3},{3,2},{4,5},{5,4},{6,7},{7,6},{8,9},{9,8},{10,11... | collective-permute-start | bytes 2654216 | tf_op jit(solution)/shard_map/ppermute | solution.py:326

commit v5 on v4

--- a/solution.py
+++ b/solution.py
@@ -83,28 +83,29 @@
     return wide * lax.rsqrt(jnp.mean(wide * wide, axis=-1, keepdims=True) + 1e-06) * gain
 
 
-def prepare_kernel(
-    tile_ref, image_ref, text_ref, q_gain_ref, k_gain_ref, table_ref, out_ref
-):
-    cosine = table_ref[0, 0]
-    sine = table_ref[0, 1]
+def rotated(vectors, gain, table_ref):
+    scaled = normed(vectors, gain)
     even = lax.broadcasted_iota(jnp.int32, (PIX, HEAD), 1) % 2 == 0
-
-    def rotated(vectors, gain):
-        scaled = normed(vectors, gain)
-        swapped = jnp.where(even, pltpu.roll(scaled, HEAD - 1, 1), pltpu.roll(scaled, 1, 1))
-        return (scaled * cosine + swapped * sine).astype(jnp.bfloat16)
-
+    swapped = jnp.where(even, pltpu.roll(scaled, HEAD - 1, 1), pltpu.roll(scaled, 1, 1))
+    return (scaled * table_ref[0, 0] + swapped * table_ref[0, 1]).astype(jnp.bfloat16)
+
+
+def key_value_kernel(tile_ref, key_ref, value_ref, text_ref, gain_ref, table_ref, out_ref):
     text = text_ref[...]
     text_keys = text[:, 0, :]
     text_values = text[:, 1, :]
     for head in range(out_ref.shape[0]):
         lanes = slice(head * HEAD, (head + 1) * HEAD)
-        out_ref[head, 0:PIX, :] = rotated(image_ref[0, :, lanes], q_gain_ref[...])
-        out_ref[head, PIX : 2 * PIX, :] = rotated(image_ref[1, :, lanes], k_gain_ref[...])
-        out_ref[head, 2 * PIX : PIX + KEYS, :] = normed(text_keys[:, lanes], k_gain_ref[...]).astype(jnp.bfloat16)
-        out_ref[head, PIX + KEYS : 2 * PIX + KEYS, :] = image_ref[2, :, lanes]
-        out_ref[head, 2 * PIX + KEYS :, :] = text_values[:, lanes]
+        out_ref[head, 0:PIX, :] = rotated(key_ref[0, :, lanes], gain_ref[...], table_ref)
+        out_ref[head, PIX:KEYS, :] = normed(text_keys[:, lanes], gain_ref[...]).astype(jnp.bfloat16)
+        out_ref[head, KEYS : KEYS + PIX, :] = value_ref[0, :, lanes]
+        out_ref[head, KEYS + PIX :, :] = text_values[:, lanes]
+
+
+def query_kernel(tile_ref, query_ref, gain_ref, table_ref, out_ref):
+    for head in range(out_ref.shape[0]):
+        lanes = slice(head * HEAD, (head + 1) * HEAD)
+        out_ref[head] = rotated(query_ref[0, :, lanes], gain_ref[...], table_ref)
 
 
 def key_bias(table_ref, size_ref, text_len_ref, group):
@@ -118,19 +119,19 @@
     return scores + bias
 
 
-def stage(source_ref, start, key_s, value_s):
+def stage(source_ref, key_s, value_s):
     for tile in range(GROUP):
         rows = slice(tile * KEYS, (tile + 1) * KEYS)
-        key_s[rows, :] = source_ref[tile, start : start + KEYS, :]
-        value_s[rows, 0:HEAD] = source_ref[tile, start + KEYS : start + 2 * KEYS, :]
+        key_s[rows, :] = source_ref[tile, 0:KEYS, :]
+        value_s[rows, 0:HEAD] = source_ref[tile, KEYS:, :]
     value_s[:, HEAD:] = jnp.ones((HALF_KEYS, HEAD), jnp.bfloat16)
 
 
-def local_kernel(group_ref, size_ref, text_len_ref, table_ref, own_ref, acc_ref, peak_ref, key_s, value_s):
+def local_kernel(group_ref, size_ref, text_len_ref, table_ref, query_ref, own_ref, acc_ref, peak_ref, key_s, value_s):
     bias = key_bias(table_ref, size_ref, text_len_ref, group_ref[0])
-    stage(own_ref, PIX, key_s, value_s)
+    stage(own_ref, key_s, value_s)
     for tile in range(GROUP):
-        scores = scores_of(own_ref[tile, 0:PIX, :], key_s[...], bias)
+        scores = scores_of(query_ref[tile], key_s[...], bias)
         peak = jnp.max(scores, axis=1, keepdims=True)
         weights = jnp.exp2((scores - peak) * EXP_SCALE).astype(jnp.bfloat16)
         acc_ref[tile] = jnp.dot(weights, value_s[...], preferred_element_type=jnp.float32)
@@ -138,12 +139,12 @@
 
 
 def remote_kernel(
-    group_ref, size_ref, text_len_ref, table_ref, own_ref, far_ref, acc_ref, peak_ref, out_ref, key_s, value_s
+    group_ref, size_ref, text_len_ref, table_ref, query_ref, far_ref, acc_ref, peak_ref, out_ref, key_s, value_s
 ):
     bias = key_bias(table_ref, size_ref, text_len_ref, group_ref[1])
-    stage(far_ref, 0, key_s, value_s)
+    stage(far_ref, key_s, value_s)
     for tile in range(GROUP):
-        scores = scores_of(own_ref[tile, 0:PIX, :], key_s[...], bias)
+        scores = scores_of(query_ref[tile], key_s[...], bias)
         before = peak_ref[tile]
         peak = jnp.maximum(before[:, 0:1], jnp.max(scores, axis=1, keepdims=True))
         weights = jnp.exp2((scores - peak) * EXP_SCALE).astype(jnp.bfloat16)
@@ -154,19 +155,13 @@
         out_ref[tile] = (blended / total).astype(jnp.bfloat16)
 
 
-def project_kernel(attended_ref, weight_ref, out_ref, weight_s, sems):
-    chunks = sems.shape[0]
-    columns = weight_s.shape[1] // chunks
-    copies = []
-    for chunk in range(chunks):
-        part = pl.ds(chunk * columns, columns)
-        copies.append(pltpu.make_async_copy(weight_ref.at[:, part], weight_s.at[:, part], sems.at[chunk]))
-        copies[chunk].start()
+def residual_kernel(hidden_ref, mlp_ref, gate_ref, out_ref):
+    out_ref[...] = hidden_ref[...].astype(jnp.float32) + gate_ref[...] * mlp_ref[...].astype(jnp.float32)
+
+
+def project_kernel(attended_ref, weight_ref, out_ref):
     attended = jnp.concatenate([attended_ref[head] for head in range(GROUP)], axis=1)
-    for chunk in range(chunks):
-        part = slice(chunk * columns, (chunk + 1) * columns)
-        copies[chunk].wait()
-        out_ref[:, part] = jnp.dot(attended, weight_s[:, part], preferred_element_type=jnp.float32).astype(jnp.bfloat16)
+    out_ref[...] = jnp.dot(attended, weight_ref[...], preferred_element_type=jnp.float32).astype(jnp.bfloat16)
 
 
 def final_kernel(
@@ -176,8 +171,7 @@
     local_ref,
     own_ref,
     other_ref,
-    hidden_ref,
-    mlp_ref,
+    residual_ref,
     gate_ref,
     shift_ref,
     scale_ref,
@@ -192,9 +186,7 @@
     for start in range(0, PIX, rows):
         block = slice(start, start + rows)
         projected = own_ref[block, :].astype(jnp.float32) + other_ref[block, :].astype(jnp.float32)
-        state = hidden_ref[block, :].astype(jnp.float32) + gate_ref[...] * (
-            projected + mlp_ref[block, :].astype(jnp.float32)
-        )
+        state = residual_ref[block, :] + gate_ref[...] * projected
         centered = state - jnp.mean(state, axis=-1, keepdims=True)
         scaled = centered * lax.rsqrt(jnp.mean(centered * centered, axis=-1, keepdims=True) + 1e-06)
         modulated_s[block, :] = (scaled * (1.0 + scale_ref[...]) + shift_ref[...]).astype(jnp.bfloat16)
@@ -270,30 +262,51 @@
     across = [(t * 2 + kind, int(partners[kind, t]) * 2 + kind) for t in range(TILES) for kind in range(2)]
 
     per_step = 2
-    prepared = pl.pallas_call(
-        prepare_kernel,
+    wide = per_step * HEAD
+    rope = jnp.asarray(rope_tables())
+
+    def slab(index):
+        return pl.BlockSpec((1, PIX, wide), lambda i, tile_ref: (index, 0, i))
+
+    gain_spec = pl.BlockSpec((1, HEAD), lambda i, tile_ref: (0, 0))
+    rope_spec = pl.BlockSpec((1, 2, PIX, HEAD), lambda i, tile_ref: (tile_ref[0], 0, 0, 0))
+    key_value = pl.pallas_call(
+        key_value_kernel,
         grid_spec=pltpu.PrefetchScalarGridSpec(
             num_scalar_prefetch=1,
             grid=(GROUP // per_step,),
             in_specs=[
-                pl.BlockSpec((3, PIX, per_step * HEAD), lambda i, tile_ref: (0, 0, i)),
-                pl.BlockSpec((SLOTS, 2, per_step * HEAD), lambda i, tile_ref: (0, 0, i)),
-                pl.BlockSpec((1, HEAD), lambda i, tile_ref: (0, 0)),
-                pl.BlockSpec((1, HEAD), lambda i, tile_ref: (0, 0)),
-                pl.BlockSpec((1, 2, PIX, HEAD), lambda i, tile_ref: (tile_ref[0], 0, 0, 0)),
+                slab(1),
+                slab(2),
+                pl.BlockSpec((SLOTS, 2, wide), lambda i, tile_ref: (0, 0, i)),
+                gain_spec,
+                rope_spec,
             ],
-            out_specs=pl.BlockSpec((per_step, PIX + 2 * KEYS, HEAD), lambda i, tile_ref: (i, 0, 0)),
+            out_specs=pl.BlockSpec((per_step, 2 * KEYS, HEAD), lambda i, tile_ref: (i, 0, 0)),
         ),
-        out_shape=jax.ShapeDtypeStruct((GROUP, PIX + 2 * KEYS, HEAD), bf16),
-        name="prepare",
-    )(tile, triple, text_kv, q_gain.reshape(1, HEAD), k_gain.reshape(1, HEAD), jnp.asarray(rope_tables()))
-    own = lax.all_to_all(prepared, mesh_axes, 0, 0, axis_index_groups=groups, tiled=True)
-    far = lax.ppermute(own[:, PIX:, :], mesh_axes, across)
+        out_shape=jax.ShapeDtypeStruct((GROUP, 2 * KEYS, HEAD), bf16),
+        name="prepare_keys",
+    )(tile, triple, triple, text_kv, k_gain.reshape(1, HEAD), rope)
+    own = lax.all_to_all(key_value, mesh_axes, 0, 0, axis_index_groups=groups, tiled=True)
+    queries = pl.pallas_call(
+        query_kernel,
+        grid_spec=pltpu.PrefetchScalarGridSpec(
+            num_scalar_prefetch=1,
+            grid=(GROUP // per_step,),
+            in_specs=[slab(0), gain_spec, rope_spec],
+            out_specs=pl.BlockSpec((per_step, PIX, HEAD), lambda i, tile_ref: (i, 0, 0)),
+        ),
+        out_shape=jax.ShapeDtypeStruct((GROUP, PIX, HEAD), bf16),
+        name="prepare_queries",
+    )(tile, triple, q_gain.reshape(1, HEAD), rope)
+    own, queries = lax.optimization_barrier((own, queries))
+    far = lax.ppermute(own, mesh_axes, across)
+    queries = lax.all_to_all(queries, mesh_axes, 0, 0, axis_index_groups=groups, tiled=True)
 
     table = jnp.asarray(key_tables())
     acc, peak = pl.pallas_call(
         local_kernel,
-        in_specs=[SMEM, SMEM, SMEM] + [VMEM] * 2,
+        in_specs=[SMEM, SMEM, SMEM] + [VMEM] * 3,
         out_specs=(VMEM, VMEM),
         out_shape=(
             jax.ShapeDtypeStruct((GROUP, PIX, 2 * HEAD), jnp.float32),
@@ -302,7 +315,7 @@
         scratch_shapes=[pltpu.VMEM((HALF_KEYS, HEAD), bf16), pltpu.VMEM((HALF_KEYS, 2 * HEAD), bf16)],
         compiler_params=params(16),
         name="attend_local",
-    )(group, image_size, text_len, table, own)
+    )(group, image_size, text_len, table, queries, own)
     attended = pl.pallas_call(
         remote_kernel,
         in_specs=[SMEM, SMEM, SMEM] + [VMEM] * 5,
@@ -311,16 +324,24 @@
         scratch_shapes=[pltpu.VMEM((HALF_KEYS, HEAD), bf16), pltpu.VMEM((HALF_KEYS, 2 * HEAD), bf16)],
         compiler_params=params(16),
         name="attend_far",
-    )(group, image_size, text_len, table, own, far, acc, peak)
+    )(group, image_size, text_len, table, queries, far, acc, peak)
     attended = lax.all_to_all(attended, mesh_axes, 0, 0, axis_index_groups=groups, tiled=True)
 
+    residual = pl.pallas_call(
+        residual_kernel,
+        in_specs=[VMEM, VMEM, VMEM],
+        out_specs=VMEM,
+        out_shape=jax.ShapeDtypeStruct((PIX, model), jnp.float32),
+        compiler_params=params(8),
+        name="residual",
+    )(hidden.reshape(PIX, model), mlp_term.reshape(PIX, model), gate.reshape(1, model))
+    attended, residual = lax.optimization_barrier((attended, residual))
     partial = pl.pallas_call(
         project_kernel,
-        in_specs=[VMEM, HBM],
+        in_specs=[VMEM, VMEM],
         out_specs=VMEM,
         out_shape=jax.ShapeDtypeStruct((PIX, model), bf16),
-        scratch_shapes=[pltpu.VMEM((width, model), bf16), pltpu.SemaphoreType.DMA((6,))],
-        compiler_params=params(48),
+        compiler_params=params(12),
         name="project",
     )(attended, out_weight)
     other = lax.ppermute(partial, "tp", [(0, 1), (1, 0)])
@@ -328,7 +349,7 @@
     local = np.stack([np.arange(PIX) // TILE_W, np.arange(PIX) % TILE_W]).astype(np.int32)
     velocity, latent_next = pl.pallas_call(
         final_kernel,
-        in_specs=[SMEM, SMEM, SMEM] + [VMEM] * 11,
+        in_specs=[SMEM, SMEM, SMEM] + [VMEM] * 10,
         out_specs=(VMEM, VMEM),
         out_shape=(jax.ShapeDtypeStruct((latents, PIX), jnp.float32),) * 2,
         scratch_shapes=[pltpu.VMEM((PIX, model), bf16)],
@@ -341,8 +362,7 @@
         jnp.asarray(local),
         partial,
         other,
-        hidden.reshape(PIX, model),
-        mlp_term.reshape(PIX, model),
+        residual,
         gate.reshape(1, model),
         final_shift.reshape(1, model),
         final_scale.reshape(1, model),

time: 73 us -> 72.7 us (level)
  blocking collectives: 36.2 us -> 0 us
  waiting for transfers between devices: 6.93 us -> 27.7 us
  starting transfers between devices: 9.99 us -> 19.7 us
  local copies, waits for them, and re-layouts: 0.1 us -> 3.99 us
  Pallas kernels: 17.3 us -> 18.5 us
    all_to_all x2 -> x0, blocking collectives: 36.2 us -> none  [the longest x1 26.2 us: shards(): lax.all_to_all(prepared, mesh_axes, 0, 0, axis_index_groups=groups, tiled...]
    all_to_all x0 -> x3, waiting for transfers between devices: none -> 26.3 us  [the longest x1 10.2 us: shards(): lax.all_to_all(key_value, mesh_axes, 0, 0, axis_index_groups=groups, tile...]
    all_to_all x0 -> x3, starting transfers between devices: none -> 15.1 us  [the longest x1 7.46 us: shards(): lax.all_to_all(key_value, mesh_axes, 0, 0, axis_index_groups=groups, tile...]
    ppermute x1, waiting for transfers between devices: 5.53 us -> 0.01 us  [shards(): far = lax.ppermute(own, mesh_axes, across)]
    ppermute x1, starting transfers between devices: 8 us -> 2.72 us  [shards(): other = lax.ppermute(partial, 'tp', [(0, 1), (1, 0)])]
    unnamed x22 -> x24, local copies, waits for them, and re-layouts: 0.05 us -> 3.99 us
    pallas_call x4 -> x6, Pallas kernels: 13.9 us -> 14.5 us  [the longest x1 4 us: shards(): pl.pallas_call(key_value_kernel, grid_spec=pltpu.PrefetchScalarGridSpec(n...]
  transfers between devices with their start and end apart: 2 -> 5, of which waited for: 2 -> 4; matrix products, arithmetic and copies ran while one was open for 0% -> 0% of each run, Pallas kernels for 5% -> 10%
where the time goes in v5:
time: 72.7 us; the launch traced here: 72 us
  waiting for transfers between devices  27.7 us (38%)
  starting transfers between devices  19.7 us (27%)
  Pallas kernels  18.5 us (25%)
  local copies, waits for them, and re-layouts  3.99 us (5%)
  between operations  2.1 us (3%)
    all_to_all x1, waiting for transfers between devices, shards(): lax.all_to_all(key_value, mesh_axes, 0, 0, axis_index_groups=groups, tile...  10.2 us
    all_to_all x1, waiting for transfers between devices, shards(): lax.all_to_all(queries, mesh_axes, 0, 0, axis_index_groups=groups, tiled=...  10.1 us
    all_to_all x1, starting transfers between devices, shards(): lax.all_to_all(key_value, mesh_axes, 0, 0, axis_index_groups=groups, tile...  7.46 us
    all_to_all x1, waiting for transfers between devices, shards(): lax.all_to_all(attended, mesh_axes, 0, 0, axis_index_groups=groups, tiled...  5.88 us
    all_to_all x1, starting transfers between devices, shards(): lax.all_to_all(attended, mesh_axes, 0, 0, axis_index_groups=groups, tiled...  4.21 us
    pallas_call x1, Pallas kernels, shards(): pl.pallas_call(remote_kernel, in_specs=[SMEM, SMEM, SMEM] + [VMEM] * 5, o...  4.02 us
    pallas_call x1, Pallas kernels, shards(): pl.pallas_call(key_value_kernel, grid_spec=pltpu.PrefetchScalarGridSpec(n...  4 us
    unnamed x24, local copies, waits for them, and re-layouts  3.99 us
  transfers between devices with their start and end apart: 5, of which 4 were waited for; matrix products, arithmetic and copies ran while one was open for 0% of the time, Pallas kernels for 10%

profile of v5, /device:TPU:1, one launch (start us, length us, event | category | flops | bytes accessed | tf_op | source)
XLA Modules:
  0.0 72.0 jit_solution(7591170361403585850)
XLA Ops:
  0.6 4.0 %prepare_keys.1 = bf16[8,352,128]{2,1,0:T(8,128)(2,1)} custom-call(s32[1]{0:T(128)} %bitcast.tile_ref, bf16[3,144,1024]{2,1,0:T(8,128)(2,1)} %bitcast.33, bf16[3,144,1024]{2,1,0:T(8,128)(2,1)} %bitcast.34, bf16[32,2,1024]{2,1,0:T(2,128)(2,1)} %text_ref.1, f32[1,128]{1,0:T(1,128)} %bitcast.37, f32[16,2,144,128]{3,2,1,0:T(8,128)} %constant.53.clone.table_ref), custom_call_target="tpu_custom_call" | custom-call | tf_op jit(solution)/shard_map/prepare_keys/pallas_call | solution.py:273
  4.6 7.5 %all-to-all-start = ((bf16[8,352,128]{2,1,0:T(8,128)(2,1)}), bf16[8,352,128]{2,1,0:T(8,128)(2,1)S(1)}, u32[]{:S(2)}, u32[]{:S(2)}) async-start(bf16[8,352,128]{2,1,0:T(8,128)(2,1)} %prepare_keys.1), calls=%async_computation | async-start | bytes 1441792 | tf_op jit(solution)/shard_map/all_to_all | solution.py:290
  12.1 0.0 copy-start.4
  12.1 0.0 copy-start.9
  12.1 3.6 %prepare_queries.1 = bf16[8,144,128]{2,1,0:T(8,128)(2,1)} custom-call(s32[1]{0:T(128)} %bitcast.tile_ref, bf16[3,144,1024]{2,1,0:T(8,128)(2,1)} %bitcast.35, f32[1,128]{1,0:T(1,128)} %bitcast.36, f32[16,2,144,128]{3,2,1,0:T(8,128)} %constant.53.clone.table_ref), custom_call_target="tpu_custom_call" | custom-call | tf_op jit(solution)/shard_map/prepare_queries/pallas_call | solution.py:291
  15.7 10.2 %all-to-all-done.own_ref = bf16[8,352,128]{2,1,0:T(8,128)(2,1)S(1)} async-done(((bf16[8,352,128]{2,1,0:T(8,128)(2,1)}), bf16[8,352,128]{2,1,0:T(8,128)(2,1)S(1)}, u32[]{:S(2)}, u32[]{:S(2)}) %all-to-all-start) | async-done | bytes 720928 | tf_op jit(solution)/shard_map/all_to_all | solution.py:290
  26.0 1.9 %collective-permute-start = (bf16[8,352,128]{2,1,0:T(8,128)(2,1)S(1)}, bf16[8,352,128]{2,1,0:T(8,128)(2,1)S(1)}, u32[]{:S(2)}, u32[]{:S(2)}) collective-permute-start(bf16[8,352,128]{2,1,0:T(8,128)(2,1)S(1)} %all-to-all-done.own_ref), channel_id=1, source_target_pairs={{0,16},{1,7},{2,18},{3,5},{4,20},{5,3},{6,22},{7,1},{8,24},{9,15},... | collective-permute-start | bytes 2162696 | tf_op jit(solution)/shard_map/ppermute | solution.py:303
  27.8 3.4 %all-to-all-start.1 = ((bf16[8,144,128]{2,1,0:T(8,128)(2,1)}), bf16[8,144,128]{2,1,0:T(8,128)(2,1)S(1)}, u32[]{:S(2)}, u32[]{:S(2)}) async-start(bf16[8,144,128]{2,1,0:T(8,128)(2,1)} %prepare_queries.1), calls=%async_computation.1 | async-start | bytes 589824 | tf_op jit(solution)/shard_map/all_to_all | solution.py:304
  32.0 0.1 pad_add_fusion.group_ref
  32.0 0.0 copy-start.1
  32.0 0.0 copy-start.6
  32.0 10.1 %all-to-all-done.1.query_ref = bf16[8,144,128]{2,1,0:T(8,128)(2,1)S(1)} async-done(((bf16[8,144,128]{2,1,0:T(8,128)(2,1)}), bf16[8,144,128]{2,1,0:T(8,128)(2,1)S(1)}, u32[]{:S(2)}, u32[]{:S(2)}) %all-to-all-start.1) | async-done | bytes 294944 | tf_op jit(solution)/shard_map/all_to_all | solution.py:304
  42.2 0.0 copy-done.4
  42.2 0.0 copy-done.9
  42.2 3.3 %attend_local.1 = (f32[8,144,256]{2,1,0:T(8,128)S(1)}, f32[8,144,128]{2,1,0:T(8,128)S(1)}) custom-call(s32[2]{0:T(128)S(1)} %pad_add_fusion.group_ref, s32[2]{0:T(128)S(1)} %copy-done.9, s32[1]{0:T(128)S(6)} %copy.21.text_len_ref, s32[4,3,1408]{2,1,0:T(4,128)S(1)} %copy-done.4, bf16[8,144,128]{2,1,0:T(8,128)(2,1)S(1)} %all-to-all-done.1.query_ref, ...), custom_call_target="tpu_custom_call" | custom-call | tf_op jit(solution)/shard_map/attend_local/pallas_call | solution.py:307
  45.5 0.0 collective-permute-done.far_ref
  45.5 4.0 %attend_far.1 = bf16[8,144,128]{2,1,0:T(8,128)(2,1)} custom-call(s32[2]{0:T(128)S(1)} %pad_add_fusion.group_ref, s32[2]{0:T(128)S(1)} %copy-done.9, s32[1]{0:T(128)S(6)} %copy.21.text_len_ref, s32[4,3,1408]{2,1,0:T(4,128)S(1)} %copy-done.4, bf16[8,144,128]{2,1,0:T(8,128)(2,1)S(1)} %all-to-all-done.1.query_ref, ...), custom_call_target="tpu_custom_call" | custom-call | tf_op jit(solution)/shard_map/attend_far/pallas_call | solution.py:319
  49.5 4.2 %all-to-all-start.2 = ((bf16[8,144,128]{2,1,0:T(8,128)(2,1)}), bf16[8,144,128]{2,1,0:T(8,128)(2,1)S(1)}, u32[]{:S(2)}, u32[]{:S(2)}) async-start(bf16[8,144,128]{2,1,0:T(8,128)(2,1)} %attend_far.1), calls=%async_computation.2 | async-start | bytes 589824 | tf_op jit(solution)/shard_map/all_to_all | solution.py:328
  53.7 0.0 copy-done.1
  53.7 0.0 copy-done.6
  53.7 0.0 copy-start.2
  53.7 1.2 %copy-done.2 = bf16[1,144,3072]{2,1,0:T(8,128)(2,1)S(1)} copy-done((bf16[1,144,3072]{2,1,0:T(8,128)(2,1)S(1)}, bf16[1,144,3072]{2,1,0:T(8,128)(2,1)}, u32[]{:S(2)}) %copy-start.2) | copy-done | bytes 884760
  54.9 0.2 residual.1.residual_ref
  55.1 5.9 %all-to-all-done.2.attended_ref = bf16[8,144,128]{2,1,0:T(8,128)(2,1)S(1)} async-done(((bf16[8,144,128]{2,1,0:T(8,128)(2,1)}), bf16[8,144,128]{2,1,0:T(8,128)(2,1)S(1)}, u32[]{:S(2)}, u32[]{:S(2)}) %all-to-all-start.2) | async-done | bytes 294944 | tf_op jit(solution)/shard_map/all_to_all | solution.py:328
  61.0 0.0 copy-start
  61.0 2.8 %copy-done = bf16[1024,3072]{1,0:T(8,128)(2,1)S(1)} copy-done((bf16[1024,3072]{1,0:T(8,128)(2,1)S(1)}, bf16[1024,3072]{1,0:T(8,128)(2,1)}, u32[]{:S(2)}) %copy-start) | copy-done | bytes 6291480
  63.8 0.0 copy-start.3
  63.8 0.0 copy-start.5
  63.8 0.0 copy-start.7
  63.8 0.0 copy-start.8
  63.8 0.0 copy-start.10
  63.8 0.0 copy-start.11
  63.8 1.1 %project.1.own_ref = bf16[144,3072]{1,0:T(8,128)(2,1)S(1)} custom-call(bf16[8,144,128]{2,1,0:T(8,128)(2,1)S(1)} %all-to-all-done.2.attended_ref, bf16[1024,3072]{1,0:T(8,128)(2,1)S(1)} %copy-done), custom_call_target="tpu_custom_call" | custom-call | tf_op jit(solution)/shard_map/project/pallas_call | solution.py:339
  64.9 2.7 %collective-permute-start.1 = (bf16[144,3072]{1,0:T(8,128)(2,1)S(1)}, bf16[144,3072]{1,0:T(8,128)(2,1)S(1)}, u32[]{:S(2)}, u32[]{:S(2)}) collective-permute-start(bf16[144,3072]{1,0:T(8,128)(2,1)S(1)} %project.1.own_ref), channel_id=1, source_target_pairs={{0,1},{1,0},{2,3},{3,2},{4,5},{5,4},{6,7},{7,6},{8,9},{9,8},{10,11... | collective-permute-start | bytes 2654216 | tf_op jit(solution)/shard_map/ppermute | solution.py:347
  68.3 1.4 %collective-permute-done.1.other_ref = bf16[144,3072]{1,0:T(8,128)(2,1)S(1)} collective-permute-done((bf16[144,3072]{1,0:T(8,128)(2,1)S(1)}, bf16[144,3072]{1,0:T(8,128)(2,1)S(1)}, u32[]{:S(2)}, u32[]{:S(2)}) %collective-permute-start.1) | collective-permute-done | bytes 884768 | tf_op jit(solution)/shard_map/ppermute | solution.py:347
  69.7 0.0 copy-done.3
  69.7 0.0 copy-done.5
  69.7 0.0 copy-done.7
  69.7 0.0 copy-done.8
  69.7 0.0 copy-done.10
  69.7 0.0 copy-done.11
  69.7 2.3 %final_layer.1 = (f32[64,144]{1,0:T(8,128)}, f32[64,144]{1,0:T(8,128)}) custom-call(s32[1]{0:T(128)} %bitcast.tile_ref, s32[2]{0:T(128)S(1)} %copy-done.9, s32[1]{0:T(128)S(6)} %copy.22.timestep_ref, s32[2,144]{1,0:T(2,128)S(1)} %copy-done.10, bf16[144,3072]{1,0:T(8,128)(2,1)S(1)} %project.1.own_ref, bf16[144,3072]{1,0:T(8,128)(2,1)S(1)} %collective-permute-done.1.other_ref, ...), custom_call_target="tpu_custom_call" | custom-call | tf_op jit(solution)/shard_map/final_layer/pallas_call | solution.py:350
Async XLA Ops:
  4.6 21.3 %all-to-all-start = ((bf16[8,352,128]{2,1,0:T(8,128)(2,1)}), bf16[8,352,128]{2,1,0:T(8,128)(2,1)S(1)}, u32[]{:S(2)}, u32[]{:S(2)}) async-start(bf16[8,352,128]{2,1,0:T(8,128)(2,1)} %prepare_keys.1), calls=%async_computation | async-start | bytes 1441792 | tf_op jit(solution)/shard_map/all_to_all | solution.py:290
  12.1 30.1 %copy-start.4 = (s32[4,3,1408]{2,1,0:T(4,128)S(1)}, s32[4,3,1408]{2,1,0:T(4,128)}, u32[]{:S(2)}) copy-start(s32[4,3,1408]{2,1,0:T(4,128)} %constant.54.clone.table_ref) | copy-start | bytes 202756
  12.1 30.1 %copy-start.9 = (s32[2]{0:T(128)S(1)}, s32[2]{0:T(128)}, u32[]{:S(2)}) copy-start(s32[2]{0:T(128)} %size_ref.5) | copy-start | bytes 28
  26.0 19.5 %collective-permute-start = (bf16[8,352,128]{2,1,0:T(8,128)(2,1)S(1)}, bf16[8,352,128]{2,1,0:T(8,128)(2,1)S(1)}, u32[]{:S(2)}, u32[]{:S(2)}) collective-permute-start(bf16[8,352,128]{2,1,0:T(8,128)(2,1)S(1)} %all-to-all-done.own_ref), channel_id=1, source_target_pairs={{0,16},{1,7},{2,18},{3,5},{4,20},{5,3},{6,22},{7,1},{8,24},{9,15},... | collective-permute-start | bytes 2162696 | tf_op jit(solution)/shard_map/ppermute | solution.py:303
  27.8 14.4 %all-to-all-start.1 = ((bf16[8,144,128]{2,1,0:T(8,128)(2,1)}), bf16[8,144,128]{2,1,0:T(8,128)(2,1)S(1)}, u32[]{:S(2)}, u32[]{:S(2)}) async-start(bf16[8,144,128]{2,1,0:T(8,128)(2,1)} %prepare_queries.1), calls=%async_computation.1 | async-start | bytes 589824 | tf_op jit(solution)/shard_map/all_to_all | solution.py:304
  32.0 21.7 %copy-start.1 = (bf16[1,144,3072]{2,1,0:T(8,128)(2,1)S(1)}, bf16[1,144,3072]{2,1,0:T(8,128)(2,1)}, u32[]{:S(2)}) copy-start(bf16[1,144,3072]{2,1,0:T(8,128)(2,1)} %param.24) | copy-start | bytes 2654212
  32.0 21.7 %copy-start.6 = (f32[3072]{0:T(1024)S(1)}, f32[3072]{0:T(1024)}, u32[]{:S(2)}) copy-start(f32[3072]{0:T(1024)} %param.26) | copy-start | bytes 36868
  49.5 11.5 %all-to-all-start.2 = ((bf16[8,144,128]{2,1,0:T(8,128)(2,1)}), bf16[8,144,128]{2,1,0:T(8,128)(2,1)S(1)}, u32[]{:S(2)}, u32[]{:S(2)}) async-start(bf16[8,144,128]{2,1,0:T(8,128)(2,1)} %attend_far.1), calls=%async_computation.2 | async-start | bytes 589824 | tf_op jit(solution)/shard_map/all_to_all | solution.py:328
  53.7 1.2 %copy-start.2 = (bf16[1,144,3072]{2,1,0:T(8,128)(2,1)S(1)}, bf16[1,144,3072]{2,1,0:T(8,128)(2,1)}, u32[]{:S(2)}) copy-start(bf16[1,144,3072]{2,1,0:T(8,128)(2,1)} %param.25) | copy-start | bytes 2654212
  61.0 2.8 %copy-start = (bf16[1024,3072]{1,0:T(8,128)(2,1)S(1)}, bf16[1024,3072]{1,0:T(8,128)(2,1)}, u32[]{:S(2)}) copy-start(bf16[1024,3072]{1,0:T(8,128)(2,1)} %weight_ref.1) | copy-start | bytes 18874372
  63.8 5.9 %copy-start.3 = (bf16[3072,64]{0,1:T(8,128)(2,1)S(1)}, bf16[3072,64]{0,1:T(8,128)(2,1)}, u32[]{:S(2)}) copy-start(bf16[3072,64]{0,1:T(8,128)(2,1)} %param.29) | copy-start | bytes 1179652
  63.8 5.9 %copy-start.5 = (f32[1,144,64]{1,2,0:T(8,128)S(1)}, f32[1,144,64]{1,2,0:T(8,128)}, u32[]{:S(2)}) copy-start(f32[1,144,64]{1,2,0:T(8,128)} %param.31) | copy-start | bytes 110596
  63.8 5.9 %copy-start.7 = (f32[3072]{0:T(1024)S(1)}, f32[3072]{0:T(1024)}, u32[]{:S(2)}) copy-start(f32[3072]{0:T(1024)} %param.27) | copy-start | bytes 36868
  63.8 5.9 %copy-start.8 = (f32[3072]{0:T(1024)S(1)}, f32[3072]{0:T(1024)}, u32[]{:S(2)}) copy-start(f32[3072]{0:T(1024)} %param.28) | copy-start | bytes 36868
  63.8 5.9 %copy-start.10 = (s32[2,144]{1,0:T(2,128)S(1)}, s32[2,144]{1,0:T(2,128)}, u32[]{:S(2)}) copy-start(s32[2,144]{1,0:T(2,128)} %constant.55.clone.local_ref) | copy-start | bytes 3460
  63.8 5.9 %copy-start.11 = (f32[64]{0:T(128)S(1)}, f32[64]{0:T(128)}, u32[]{:S(2)}) copy-start(f32[64]{0:T(128)} %param.30) | copy-start | bytes 772
  64.9 4.8 %collective-permute-start.1 = (bf16[144,3072]{1,0:T(8,128)(2,1)S(1)}, bf16[144,3072]{1,0:T(8,128)(2,1)S(1)}, u32[]{:S(2)}, u32[]{:S(2)}) collective-permute-start(bf16[144,3072]{1,0:T(8,128)(2,1)S(1)} %project.1.own_ref), channel_id=1, source_target_pairs={{0,1},{1,0},{2,3},{3,2},{4,5},{5,4},{6,7},{7,6},{8,9},{9,8},{10,11... | collective-permute-start | bytes 2654216 | tf_op jit(solution)/shard_map/ppermute | solution.py:347

commit v6 on v5

--- a/solution.py
+++ b/solution.py
@@ -78,34 +78,55 @@
     return np.stack(tables).astype(np.int32)
 
 
-def normed(vectors, gain):
+def inverse_rms(vectors):
     wide = vectors.astype(jnp.float32)
-    return wide * lax.rsqrt(jnp.mean(wide * wide, axis=-1, keepdims=True) + 1e-06) * gain
-
-
-def rotated(vectors, gain, table_ref):
-    scaled = normed(vectors, gain)
-    even = lax.broadcasted_iota(jnp.int32, (PIX, HEAD), 1) % 2 == 0
-    swapped = jnp.where(even, pltpu.roll(scaled, HEAD - 1, 1), pltpu.roll(scaled, 1, 1))
-    return (scaled * table_ref[0, 0] + swapped * table_ref[0, 1]).astype(jnp.bfloat16)
+    square = wide * wide
+    high = square.astype(jnp.bfloat16)
+    low = (square - high.astype(jnp.float32)).astype(jnp.bfloat16)
+    ones = jnp.ones((2 * HEAD, HEAD), jnp.bfloat16)
+    total = jnp.dot(jnp.concatenate([high, low], axis=1), ones, preferred_element_type=jnp.float32)
+    return lax.rsqrt(total * (1.0 / HEAD) + 1e-06)
+
+
+def swap_pairs(rows):
+    even = lax.broadcasted_iota(jnp.int32, rows.shape, 1) % 2 == 0
+    return jnp.where(even, pltpu.roll(rows, HEAD - 1, 1), pltpu.roll(rows, 1, 1))
+
+
+def rotate_heads(source_ref, gain_ref, table_ref, out_ref):
+    heads = out_ref.shape[0]
+    gain = jnp.broadcast_to(gain_ref[...], (8, HEAD))
+    along = table_ref[0, 0] * gain[0:1]
+    across = table_ref[0, 1] * swap_pairs(gain)[0:1]
+    stacked = jnp.concatenate([source_ref[0, :, h * HEAD : (h + 1) * HEAD] for h in range(heads)], axis=0)
+    row = lax.broadcasted_iota(jnp.int32, (HEAD, HEAD), 0)
+    col = lax.broadcasted_iota(jnp.int32, (HEAD, HEAD), 1)
+    pairs = jnp.where(row + 1 - 2 * (row % 2) == col, 1.0, 0.0).astype(jnp.bfloat16)
+    swapped = jnp.dot(stacked, pairs, preferred_element_type=jnp.float32)
+    inverse = inverse_rms(stacked)
+    for head in range(heads):
+        rows = slice(head * PIX, (head + 1) * PIX)
+        turned = stacked[rows].astype(jnp.float32) * along + swapped[rows] * across
+        out_ref[head, 0:PIX, :] = (turned * inverse[rows]).astype(jnp.bfloat16)
 
 
 def key_value_kernel(tile_ref, key_ref, value_ref, text_ref, gain_ref, table_ref, out_ref):
+    rotate_heads(key_ref, gain_ref, table_ref, out_ref)
     text = text_ref[...]
+    heads = out_ref.shape[0]
     text_keys = text[:, 0, :]
     text_values = text[:, 1, :]
-    for head in range(out_ref.shape[0]):
+    stacked = jnp.concatenate([text_keys[:, h * HEAD : (h + 1) * HEAD] for h in range(heads)], axis=0)
+    text_keys = (stacked.astype(jnp.float32) * inverse_rms(stacked) * gain_ref[...]).astype(jnp.bfloat16)
+    for head in range(heads):
         lanes = slice(head * HEAD, (head + 1) * HEAD)
-        out_ref[head, 0:PIX, :] = rotated(key_ref[0, :, lanes], gain_ref[...], table_ref)
-        out_ref[head, PIX:KEYS, :] = normed(text_keys[:, lanes], gain_ref[...]).astype(jnp.bfloat16)
+        out_ref[head, PIX:KEYS, :] = text_keys[head * SLOTS : (head + 1) * SLOTS]
         out_ref[head, KEYS : KEYS + PIX, :] = value_ref[0, :, lanes]
         out_ref[head, KEYS + PIX :, :] = text_values[:, lanes]
 
 
 def query_kernel(tile_ref, query_ref, gain_ref, table_ref, out_ref):
-    for head in range(out_ref.shape[0]):
-        lanes = slice(head * HEAD, (head + 1) * HEAD)
-        out_ref[head] = rotated(query_ref[0, :, lanes], gain_ref[...], table_ref)
+    rotate_heads(query_ref, gain_ref, table_ref, out_ref)
 
 
 def key_bias(table_ref, size_ref, text_len_ref, group):
@@ -155,13 +176,32 @@
         out_ref[tile] = (blended / total).astype(jnp.bfloat16)
 
 
-def residual_kernel(hidden_ref, mlp_ref, gate_ref, out_ref):
-    out_ref[...] = hidden_ref[...].astype(jnp.float32) + gate_ref[...] * mlp_ref[...].astype(jnp.float32)
-
-
-def project_kernel(attended_ref, weight_ref, out_ref):
+def fetch_kernel(weight_ref, out_ref, sem):
+    copy = pltpu.make_async_copy(weight_ref.at[:, pl.ds(0, out_ref.shape[1])], out_ref, sem)
+    copy.start()
+    copy.wait()
+
+
+def project_kernel(attended_ref, ready_ref, weight_ref, out_ref, weight_s, sems):
+    ready = ready_ref.shape[1]
+    chunks = sems.shape[0]
+    columns = weight_s.shape[1] // chunks
+    copies = []
+    for chunk in range(chunks):
+        start = chunk * columns
+        source = weight_ref.at[:, pl.ds(ready + start, columns)]
+        copies.append(pltpu.make_async_copy(source, weight_s.at[:, pl.ds(start, columns)], sems.at[chunk]))
+        copies[chunk].start()
     attended = jnp.concatenate([attended_ref[head] for head in range(GROUP)], axis=1)
-    out_ref[...] = jnp.dot(attended, weight_ref[...], preferred_element_type=jnp.float32).astype(jnp.bfloat16)
+
+    def projected(weight):
+        return jnp.dot(attended, weight, preferred_element_type=jnp.float32).astype(jnp.bfloat16)
+
+    out_ref[:, 0:ready] = projected(ready_ref[...])
+    for chunk in range(chunks):
+        start = chunk * columns
+        copies[chunk].wait()
+        out_ref[:, ready + start : ready + start + columns] = projected(weight_s[:, start : start + columns])
 
 
 def final_kernel(
@@ -171,7 +211,8 @@
     local_ref,
     own_ref,
     other_ref,
-    residual_ref,
+    hidden_ref,
+    mlp_ref,
     gate_ref,
     shift_ref,
     scale_ref,
@@ -186,7 +227,9 @@
     for start in range(0, PIX, rows):
         block = slice(start, start + rows)
         projected = own_ref[block, :].astype(jnp.float32) + other_ref[block, :].astype(jnp.float32)
-        state = residual_ref[block, :] + gate_ref[...] * projected
+        state = hidden_ref[block, :].astype(jnp.float32) + gate_ref[...] * (
+            projected + mlp_ref[block, :].astype(jnp.float32)
+        )
         centered = state - jnp.mean(state, axis=-1, keepdims=True)
         scaled = centered * lax.rsqrt(jnp.mean(centered * centered, axis=-1, keepdims=True) + 1e-06)
         modulated_s[block, :] = (scaled * (1.0 + scale_ref[...]) + shift_ref[...]).astype(jnp.bfloat16)
@@ -261,7 +304,7 @@
     groups = [[int(t) * 2 + kind for t in tiles] for kind in range(2) for tiles in kinds[kind]]
     across = [(t * 2 + kind, int(partners[kind, t]) * 2 + kind) for t in range(TILES) for kind in range(2)]
 
-    per_step = 2
+    per_step = 4
     wide = per_step * HEAD
     rope = jnp.asarray(rope_tables())
 
@@ -327,29 +370,31 @@
     )(group, image_size, text_len, table, queries, far, acc, peak)
     attended = lax.all_to_all(attended, mesh_axes, 0, 0, axis_index_groups=groups, tiled=True)
 
-    residual = pl.pallas_call(
-        residual_kernel,
-        in_specs=[VMEM, VMEM, VMEM],
+    ready = model // 2
+    first_half = pl.pallas_call(
+        fetch_kernel,
+        in_specs=[HBM],
         out_specs=VMEM,
-        out_shape=jax.ShapeDtypeStruct((PIX, model), jnp.float32),
-        compiler_params=params(8),
-        name="residual",
-    )(hidden.reshape(PIX, model), mlp_term.reshape(PIX, model), gate.reshape(1, model))
-    attended, residual = lax.optimization_barrier((attended, residual))
+        out_shape=jax.ShapeDtypeStruct((width, ready), bf16),
+        scratch_shapes=[pltpu.SemaphoreType.DMA],
+        compiler_params=params(48),
+        name="fetch_weight",
+    )(out_weight)
     partial = pl.pallas_call(
         project_kernel,
-        in_specs=[VMEM, VMEM],
+        in_specs=[VMEM, VMEM, HBM],
         out_specs=VMEM,
         out_shape=jax.ShapeDtypeStruct((PIX, model), bf16),
-        compiler_params=params(12),
+        scratch_shapes=[pltpu.VMEM((width, model - ready), bf16), pltpu.SemaphoreType.DMA((3,))],
+        compiler_params=params(48),
         name="project",
-    )(attended, out_weight)
+    )(attended, first_half, out_weight)
     other = lax.ppermute(partial, "tp", [(0, 1), (1, 0)])
 
     local = np.stack([np.arange(PIX) // TILE_W, np.arange(PIX) % TILE_W]).astype(np.int32)
     velocity, latent_next = pl.pallas_call(
         final_kernel,
-        in_specs=[SMEM, SMEM, SMEM] + [VMEM] * 10,
+        in_specs=[SMEM, SMEM, SMEM] + [VMEM] * 11,
         out_specs=(VMEM, VMEM),
         out_shape=(jax.ShapeDtypeStruct((latents, PIX), jnp.float32),) * 2,
         scratch_shapes=[pltpu.VMEM((PIX, model), bf16)],
@@ -362,7 +407,8 @@
         jnp.asarray(local),
         partial,
         other,
-        residual,
+        hidden.reshape(PIX, model),
+        mlp_term.reshape(PIX, model),
         gate.reshape(1, model),
         final_shift.reshape(1, model),
         final_scale.reshape(1, model),

time: 72.7 us -> 70.3 us (0.967)
  local copies, waits for them, and re-layouts: 3.99 us -> 0.06 us
  waiting for transfers between devices: 27.7 us -> 28.5 us
    unnamed x24 -> x22, local copies, waits for them, and re-layouts: 3.99 us -> 0.06 us
    pallas_call x3, Pallas kernels: 3.6 us -> 6.81 us  [the longest x1 2.47 us: shards(): pl.pallas_call(project_kernel, in_specs=[VMEM, VMEM, HBM], out_specs=VMEM...]
    all_to_all x1, waiting for transfers between devices: 10.2 us -> 11.6 us  [shards(): lax.all_to_all(key_value, mesh_axes, 0, 0, axis_index_groups=groups, tile...]
    pallas_call x1, Pallas kernels: 3.62 us -> 2.28 us  [shards(): pl.pallas_call(query_kernel, grid_spec=pltpu.PrefetchScalarGridSpec(num_s...]
    pallas_call x1, Pallas kernels: 4 us -> 2.87 us  [shards(): pl.pallas_call(key_value_kernel, grid_spec=pltpu.PrefetchScalarGridSpec(n...]
  transfers between devices with their start and end apart: 5 -> 5, of which waited for: 4 -> 4; matrix products, arithmetic and copies ran while one was open for 0% -> 0% of each run, Pallas kernels for 10% -> 11%
where the time goes in v6:
time: 70.3 us; the launch traced here: 69.8 us
  waiting for transfers between devices  28.5 us (41%)
  starting transfers between devices  19.8 us (28%)
  Pallas kernels  19.2 us (27%)
  between operations  2.13 us (3%)
    all_to_all x1, waiting for transfers between devices, shards(): lax.all_to_all(key_value, mesh_axes, 0, 0, axis_index_groups=groups, tile...  11.6 us
    all_to_all x1, waiting for transfers between devices, shards(): lax.all_to_all(queries, mesh_axes, 0, 0, axis_index_groups=groups, tiled=...  10.2 us
    all_to_all x1, starting transfers between devices, shards(): lax.all_to_all(key_value, mesh_axes, 0, 0, axis_index_groups=groups, tile...  7.61 us
    all_to_all x1, waiting for transfers between devices, shards(): lax.all_to_all(attended, mesh_axes, 0, 0, axis_index_groups=groups, tiled...  5.32 us
    all_to_all x1, starting transfers between devices, shards(): lax.all_to_all(attended, mesh_axes, 0, 0, axis_index_groups=groups, tiled...  4.21 us
    pallas_call x1, Pallas kernels, shards(): pl.pallas_call(remote_kernel, in_specs=[SMEM, SMEM, SMEM] + [VMEM] * 5, o...  4.01 us
    all_to_all x1, starting transfers between devices, shards(): lax.all_to_all(queries, mesh_axes, 0, 0, axis_index_groups=groups, tiled=...  3.42 us
    pallas_call x1, Pallas kernels, shards(): pl.pallas_call(local_kernel, in_specs=[SMEM, SMEM, SMEM] + [VMEM] * 3, ou...  3.26 us
  transfers between devices with their start and end apart: 5, of which 4 were waited for; matrix products, arithmetic and copies ran while one was open for 0% of the time, Pallas kernels for 11%

profile of v6, /device:TPU:1, one launch (start us, length us, event | category | flops | bytes accessed | tf_op | source)
XLA Modules:
  0.0 69.8 jit_solution(10139316242617100664)
XLA Ops:
  0.6 2.9 %prepare_keys.1 = bf16[8,352,128]{2,1,0:T(8,128)(2,1)} custom-call(s32[1]{0:T(128)} %bitcast.tile_ref, bf16[3,144,1024]{2,1,0:T(8,128)(2,1)} %bitcast.32, bf16[3,144,1024]{2,1,0:T(8,128)(2,1)} %bitcast.33, bf16[32,2,1024]{2,1,0:T(2,128)(2,1)} %text_ref.1, f32[1,128]{1,0:T(1,128)} %bitcast.36, f32[16,2,144,128]{3,2,1,0:T(8,128)} %constant.53.clone.table_ref), custom_call_target="tpu_custom_call" | custom-call | tf_op jit(solution)/shard_map/prepare_keys/pallas_call | solution.py:316
  3.5 0.0 copy-start.3
  3.5 0.0 copy-start.8
  3.5 7.6 %all-to-all-start = ((bf16[8,352,128]{2,1,0:T(8,128)(2,1)}), bf16[8,352,128]{2,1,0:T(8,128)(2,1)S(1)}, u32[]{:S(2)}, u32[]{:S(2)}) async-start(bf16[8,352,128]{2,1,0:T(8,128)(2,1)} %prepare_keys.1), calls=%async_computation | async-start | bytes 1441792 | tf_op jit(solution)/shard_map/all_to_all | solution.py:333
  11.1 2.3 %prepare_queries.1 = bf16[8,144,128]{2,1,0:T(8,128)(2,1)} custom-call(s32[1]{0:T(128)} %bitcast.tile_ref, bf16[3,144,1024]{2,1,0:T(8,128)(2,1)} %bitcast.34, f32[1,128]{1,0:T(1,128)} %bitcast.35, f32[16,2,144,128]{3,2,1,0:T(8,128)} %constant.53.clone.table_ref), custom_call_target="tpu_custom_call" | custom-call | tf_op jit(solution)/shard_map/prepare_queries/pallas_call | solution.py:334
  13.4 11.6 %all-to-all-done.own_ref = bf16[8,352,128]{2,1,0:T(8,128)(2,1)S(1)} async-done(((bf16[8,352,128]{2,1,0:T(8,128)(2,1)}), bf16[8,352,128]{2,1,0:T(8,128)(2,1)S(1)}, u32[]{:S(2)}, u32[]{:S(2)}) %all-to-all-start) | async-done | bytes 720928 | tf_op jit(solution)/shard_map/all_to_all | solution.py:333
  25.0 1.9 %collective-permute-start = (bf16[8,352,128]{2,1,0:T(8,128)(2,1)S(1)}, bf16[8,352,128]{2,1,0:T(8,128)(2,1)S(1)}, u32[]{:S(2)}, u32[]{:S(2)}) collective-permute-start(bf16[8,352,128]{2,1,0:T(8,128)(2,1)S(1)} %all-to-all-done.own_ref), channel_id=1, source_target_pairs={{0,16},{1,7},{2,18},{3,5},{4,20},{5,3},{6,22},{7,1},{8,24},{9,15},... | collective-permute-start | bytes 2162696 | tf_op jit(solution)/shard_map/ppermute | solution.py:346
  26.9 3.4 %all-to-all-start.1 = ((bf16[8,144,128]{2,1,0:T(8,128)(2,1)}), bf16[8,144,128]{2,1,0:T(8,128)(2,1)S(1)}, u32[]{:S(2)}, u32[]{:S(2)}) async-start(bf16[8,144,128]{2,1,0:T(8,128)(2,1)} %prepare_queries.1), calls=%async_computation.1 | async-start | bytes 589824 | tf_op jit(solution)/shard_map/all_to_all | solution.py:347
  31.0 0.1 pad_add_fusion.group_ref
  31.1 10.2 %all-to-all-done.1.query_ref = bf16[8,144,128]{2,1,0:T(8,128)(2,1)S(1)} async-done(((bf16[8,144,128]{2,1,0:T(8,128)(2,1)}), bf16[8,144,128]{2,1,0:T(8,128)(2,1)S(1)}, u32[]{:S(2)}, u32[]{:S(2)}) %all-to-all-start.1) | async-done | bytes 294944 | tf_op jit(solution)/shard_map/all_to_all | solution.py:347
  41.2 0.0 copy-done.3
  41.2 0.0 copy-done.8
  41.2 3.3 %attend_local.1 = (f32[8,144,256]{2,1,0:T(8,128)S(1)}, f32[8,144,128]{2,1,0:T(8,128)S(1)}) custom-call(s32[2]{0:T(128)S(1)} %pad_add_fusion.group_ref, s32[2]{0:T(128)S(1)} %copy-done.8, s32[1]{0:T(128)S(6)} %copy.21.text_len_ref, s32[4,3,1408]{2,1,0:T(4,128)S(1)} %copy-done.3, bf16[8,144,128]{2,1,0:T(8,128)(2,1)S(1)} %all-to-all-done.1.query_ref, ...), custom_call_target="tpu_custom_call" | custom-call | tf_op jit(solution)/shard_map/attend_local/pallas_call | solution.py:350
  44.5 0.0 collective-permute-done.far_ref
  44.5 4.0 %attend_far.1 = bf16[8,144,128]{2,1,0:T(8,128)(2,1)} custom-call(s32[2]{0:T(128)S(1)} %pad_add_fusion.group_ref, s32[2]{0:T(128)S(1)} %copy-done.8, s32[1]{0:T(128)S(6)} %copy.21.text_len_ref, s32[4,3,1408]{2,1,0:T(4,128)S(1)} %copy-done.3, bf16[8,144,128]{2,1,0:T(8,128)(2,1)S(1)} %all-to-all-done.1.query_ref, ...), custom_call_target="tpu_custom_call" | custom-call | tf_op jit(solution)/shard_map/attend_far/pallas_call | solution.py:362
  48.5 4.2 %all-to-all-start.2 = ((bf16[8,144,128]{2,1,0:T(8,128)(2,1)}), bf16[8,144,128]{2,1,0:T(8,128)(2,1)S(1)}, u32[]{:S(2)}, u32[]{:S(2)}) async-start(bf16[8,144,128]{2,1,0:T(8,128)(2,1)} %attend_far.1), calls=%async_computation.2 | async-start | bytes 589824 | tf_op jit(solution)/shard_map/all_to_all | solution.py:371
  52.7 1.9 %fetch_weight.1.ready_ref = bf16[1024,1536]{1,0:T(8,128)(2,1)S(1)} custom-call(bf16[1024,3072]{1,0:T(8,128)(2,1)} %weight_ref.3), custom_call_target="tpu_custom_call" | custom-call | tf_op jit(solution)/shard_map/fetch_weight/pallas_call | solution.py:374
  54.6 0.0 copy-start.4
  54.6 0.0 copy-start.5
  54.7 0.0 copy-start.6
  54.7 0.0 copy-start.7
  54.7 0.0 copy-start.9
  54.7 0.0 copy-start.10
  54.7 5.3 %all-to-all-done.2.attended_ref = bf16[8,144,128]{2,1,0:T(8,128)(2,1)S(1)} async-done(((bf16[8,144,128]{2,1,0:T(8,128)(2,1)}), bf16[8,144,128]{2,1,0:T(8,128)(2,1)S(1)}, u32[]{:S(2)}, u32[]{:S(2)}) %all-to-all-start.2) | async-done | bytes 294944 | tf_op jit(solution)/shard_map/all_to_all | solution.py:371
  60.0 0.0 copy-start
  60.0 0.0 copy-start.1
  60.0 0.0 copy-start.2
  60.0 2.5 %project.1.own_ref = bf16[144,3072]{1,0:T(8,128)(2,1)S(1)} custom-call(bf16[8,144,128]{2,1,0:T(8,128)(2,1)S(1)} %all-to-all-done.2.attended_ref, bf16[1024,1536]{1,0:T(8,128)(2,1)S(1)} %fetch_weight.1.ready_ref, bf16[1024,3072]{1,0:T(8,128)(2,1)} %weight_ref.3), custom_call_target="tpu_custom_call" | custom-call | tf_op jit(solution)/shard_map/project/pallas_call | solution.py:383
  62.5 2.7 %collective-permute-start.1 = (bf16[144,3072]{1,0:T(8,128)(2,1)S(1)}, bf16[144,3072]{1,0:T(8,128)(2,1)S(1)}, u32[]{:S(2)}, u32[]{:S(2)}) collective-permute-start(bf16[144,3072]{1,0:T(8,128)(2,1)S(1)} %project.1.own_ref), channel_id=1, source_target_pairs={{0,1},{1,0},{2,3},{3,2},{4,5},{5,4},{6,7},{7,6},{8,9},{9,8},{10,11... | collective-permute-start | bytes 2654216 | tf_op jit(solution)/shard_map/ppermute | solution.py:392
  65.9 1.4 %collective-permute-done.1.other_ref = bf16[144,3072]{1,0:T(8,128)(2,1)S(1)} collective-permute-done((bf16[144,3072]{1,0:T(8,128)(2,1)S(1)}, bf16[144,3072]{1,0:T(8,128)(2,1)S(1)}, u32[]{:S(2)}, u32[]{:S(2)}) %collective-permute-start.1) | collective-permute-done | bytes 884768 | tf_op jit(solution)/shard_map/ppermute | solution.py:392
  67.3 0.0 copy-done.4
  67.3 0.0 copy-done.5
  67.3 0.0 copy-done.6
  67.3 0.0 copy-done.7
  67.3 0.0 copy-done.9
  67.3 0.0 copy-done.10
  67.3 0.0 copy-done
  67.3 0.0 copy-done.1
  67.3 0.0 copy-done.2
  67.3 2.5 %final_layer.1 = (f32[64,144]{1,0:T(8,128)}, f32[64,144]{1,0:T(8,128)}) custom-call(s32[1]{0:T(128)} %bitcast.tile_ref, s32[2]{0:T(128)S(1)} %copy-done.8, s32[1]{0:T(128)S(6)} %copy.22.timestep_ref, s32[2,144]{1,0:T(2,128)S(1)} %copy-done.9, bf16[144,3072]{1,0:T(8,128)(2,1)S(1)} %project.1.own_ref, bf16[144,3072]{1,0:T(8,128)(2,1)S(1)} %collective-permute-done.1.other_ref, ...), custom_call_target="tpu_custom_call" | custom-call | tf_op jit(solution)/shard_map/final_layer/pallas_call | solution.py:395
Async XLA Ops:
  3.5 37.7 %copy-start.3 = (s32[4,3,1408]{2,1,0:T(4,128)S(1)}, s32[4,3,1408]{2,1,0:T(4,128)}, u32[]{:S(2)}) copy-start(s32[4,3,1408]{2,1,0:T(4,128)} %constant.54.clone.table_ref) | copy-start | bytes 202756
  3.5 37.7 %copy-start.8 = (s32[2]{0:T(128)S(1)}, s32[2]{0:T(128)}, u32[]{:S(2)}) copy-start(s32[2]{0:T(128)} %size_ref.5) | copy-start | bytes 28
  3.5 21.5 %all-to-all-start = ((bf16[8,352,128]{2,1,0:T(8,128)(2,1)}), bf16[8,352,128]{2,1,0:T(8,128)(2,1)S(1)}, u32[]{:S(2)}, u32[]{:S(2)}) async-start(bf16[8,352,128]{2,1,0:T(8,128)(2,1)} %prepare_keys.1), calls=%async_computation | async-start | bytes 1441792 | tf_op jit(solution)/shard_map/all_to_all | solution.py:333
  25.0 19.5 %collective-permute-start = (bf16[8,352,128]{2,1,0:T(8,128)(2,1)S(1)}, bf16[8,352,128]{2,1,0:T(8,128)(2,1)S(1)}, u32[]{:S(2)}, u32[]{:S(2)}) collective-permute-start(bf16[8,352,128]{2,1,0:T(8,128)(2,1)S(1)} %all-to-all-done.own_ref), channel_id=1, source_target_pairs={{0,16},{1,7},{2,18},{3,5},{4,20},{5,3},{6,22},{7,1},{8,24},{9,15},... | collective-permute-start | bytes 2162696 | tf_op jit(solution)/shard_map/ppermute | solution.py:346
  26.9 14.4 %all-to-all-start.1 = ((bf16[8,144,128]{2,1,0:T(8,128)(2,1)}), bf16[8,144,128]{2,1,0:T(8,128)(2,1)S(1)}, u32[]{:S(2)}, u32[]{:S(2)}) async-start(bf16[8,144,128]{2,1,0:T(8,128)(2,1)} %prepare_queries.1), calls=%async_computation.1 | async-start | bytes 589824 | tf_op jit(solution)/shard_map/all_to_all | solution.py:347
  48.5 11.5 %all-to-all-start.2 = ((bf16[8,144,128]{2,1,0:T(8,128)(2,1)}), bf16[8,144,128]{2,1,0:T(8,128)(2,1)S(1)}, u32[]{:S(2)}, u32[]{:S(2)}) async-start(bf16[8,144,128]{2,1,0:T(8,128)(2,1)} %attend_far.1), calls=%async_computation.2 | async-start | bytes 589824 | tf_op jit(solution)/shard_map/all_to_all | solution.py:371
  54.6 12.6 %copy-start.4 = (f32[1,144,64]{1,2,0:T(8,128)S(1)}, f32[1,144,64]{1,2,0:T(8,128)}, u32[]{:S(2)}) copy-start(f32[1,144,64]{1,2,0:T(8,128)} %param.31) | copy-start | bytes 110596
  54.6 12.6 %copy-start.5 = (f32[3072]{0:T(1024)S(1)}, f32[3072]{0:T(1024)}, u32[]{:S(2)}) copy-start(f32[3072]{0:T(1024)} %param.26) | copy-start | bytes 36868
  54.7 12.6 %copy-start.6 = (f32[3072]{0:T(1024)S(1)}, f32[3072]{0:T(1024)}, u32[]{:S(2)}) copy-start(f32[3072]{0:T(1024)} %param.27) | copy-start | bytes 36868
  54.7 12.6 %copy-start.7 = (f32[3072]{0:T(1024)S(1)}, f32[3072]{0:T(1024)}, u32[]{:S(2)}) copy-start(f32[3072]{0:T(1024)} %param.28) | copy-start | bytes 36868
  54.7 12.6 %copy-start.9 = (s32[2,144]{1,0:T(2,128)S(1)}, s32[2,144]{1,0:T(2,128)}, u32[]{:S(2)}) copy-start(s32[2,144]{1,0:T(2,128)} %constant.55.clone.local_ref) | copy-start | bytes 3460
  54.7 12.6 %copy-start.10 = (f32[64]{0:T(128)S(1)}, f32[64]{0:T(128)}, u32[]{:S(2)}) copy-start(f32[64]{0:T(128)} %param.30) | copy-start | bytes 772
  60.0 7.3 %copy-start = (bf16[1,144,3072]{2,1,0:T(8,128)(2,1)S(1)}, bf16[1,144,3072]{2,1,0:T(8,128)(2,1)}, u32[]{:S(2)}) copy-start(bf16[1,144,3072]{2,1,0:T(8,128)(2,1)} %param.24) | copy-start | bytes 2654212
  60.0 7.3 %copy-start.1 = (bf16[1,144,3072]{2,1,0:T(8,128)(2,1)S(1)}, bf16[1,144,3072]{2,1,0:T(8,128)(2,1)}, u32[]{:S(2)}) copy-start(bf16[1,144,3072]{2,1,0:T(8,128)(2,1)} %param.25) | copy-start | bytes 2654212
  60.0 7.3 %copy-start.2 = (bf16[3072,64]{0,1:T(8,128)(2,1)S(1)}, bf16[3072,64]{0,1:T(8,128)(2,1)}, u32[]{:S(2)}) copy-start(bf16[3072,64]{0,1:T(8,128)(2,1)} %param.29) | copy-start | bytes 1179652
  62.5 4.8 %collective-permute-start.1 = (bf16[144,3072]{1,0:T(8,128)(2,1)S(1)}, bf16[144,3072]{1,0:T(8,128)(2,1)S(1)}, u32[]{:S(2)}, u32[]{:S(2)}) collective-permute-start(bf16[144,3072]{1,0:T(8,128)(2,1)S(1)} %project.1.own_ref), channel_id=1, source_target_pairs={{0,1},{1,0},{2,3},{3,2},{4,5},{5,4},{6,7},{7,6},{8,9},{9,8},{10,11... | collective-permute-start | bytes 2654216 | tf_op jit(solution)/shard_map/ppermute | solution.py:392

commit v7 on v6

--- a/solution.py
+++ b/solution.py
@@ -20,6 +20,11 @@
 KEYS = PIX + SLOTS
 GROUP = 8
 HALF_KEYS = GROUP * KEYS
+QUERIES = GROUP * PIX
+QUERY_BLOCK = QUERIES // 2
+FAR_BLOCK = QUERIES // 4
+KEY_CHUNK = 256
+READY = (1536,)
 DEAD = -1e30
 EXP_SCALE = HEAD ** (-0.5) * math.log2(math.e)
 
@@ -135,9 +140,34 @@
     return jnp.where(image_ok | text_ok, 0.0, DEAD)
 
 
-def scores_of(queries, keys, bias):
-    scores = lax.dot_general(queries, keys, (((1,), (1,)), ((), ())), preferred_element_type=jnp.float32)
-    return scores + bias
+def score_chunks(queries, key_s, bias):
+    chunks = []
+    for start in range(0, key_s.shape[0], KEY_CHUNK):
+        part = slice(start, min(start + KEY_CHUNK, key_s.shape[0]))
+        scores = lax.dot_general(
+            queries, key_s[part, :], (((1,), (1,)), ((), ())), preferred_element_type=jnp.float32
+        )
+        chunks.append(scores + bias[:, part])
+    return chunks
+
+
+def peak_of(chunks):
+    peak = jnp.max(chunks[0], axis=1, keepdims=True)
+    for scores in chunks[1:]:
+        peak = jnp.maximum(peak, jnp.max(scores, axis=1, keepdims=True))
+    return peak
+
+
+def weighted(chunks, peak, value_s):
+    blended = None
+    start = 0
+    for scores in chunks:
+        stop = start + scores.shape[1]
+        weights = jnp.exp2((scores - peak) * EXP_SCALE).astype(jnp.bfloat16)
+        added = jnp.dot(weights, value_s[start:stop, :], preferred_element_type=jnp.float32)
+        blended = added if blended is None else blended + added
+        start = stop
+    return blended
 
 
 def stage(source_ref, key_s, value_s):
@@ -148,15 +178,17 @@
     value_s[:, HEAD:] = jnp.ones((HALF_KEYS, HEAD), jnp.bfloat16)
 
 
-def local_kernel(group_ref, size_ref, text_len_ref, table_ref, query_ref, own_ref, acc_ref, peak_ref, key_s, value_s):
+def local_kernel(
+    group_ref, size_ref, text_len_ref, table_ref, query_ref, own_ref, acc_ref, peak_ref, key_s, value_s
+):
     bias = key_bias(table_ref, size_ref, text_len_ref, group_ref[0])
     stage(own_ref, key_s, value_s)
-    for tile in range(GROUP):
-        scores = scores_of(query_ref[tile], key_s[...], bias)
-        peak = jnp.max(scores, axis=1, keepdims=True)
-        weights = jnp.exp2((scores - peak) * EXP_SCALE).astype(jnp.bfloat16)
-        acc_ref[tile] = jnp.dot(weights, value_s[...], preferred_element_type=jnp.float32)
-        peak_ref[tile] = jnp.broadcast_to(peak, (PIX, HEAD))
+    for start in range(0, QUERIES, QUERY_BLOCK):
+        block = slice(start, start + QUERY_BLOCK)
+        chunks = score_chunks(query_ref[block, :], key_s, bias)
+        peak = peak_of(chunks)
+        acc_ref[block, :] = weighted(chunks, peak, value_s)
+        peak_ref[block, :] = jnp.broadcast_to(peak, (QUERY_BLOCK, HEAD))
 
 
 def remote_kernel(
@@ -164,44 +196,58 @@
 ):
     bias = key_bias(table_ref, size_ref, text_len_ref, group_ref[1])
     stage(far_ref, key_s, value_s)
-    for tile in range(GROUP):
-        scores = scores_of(query_ref[tile], key_s[...], bias)
-        before = peak_ref[tile]
-        peak = jnp.maximum(before[:, 0:1], jnp.max(scores, axis=1, keepdims=True))
-        weights = jnp.exp2((scores - peak) * EXP_SCALE).astype(jnp.bfloat16)
+    blocks = [slice(start, start + FAR_BLOCK) for start in range(0, QUERIES, FAR_BLOCK)]
+    ahead = score_chunks(query_ref[blocks[0], :], key_s, bias)
+    for index, block in enumerate(blocks):
+        chunks = ahead
+        if index + 1 < len(blocks):
+            ahead = score_chunks(query_ref[blocks[index + 1], :], key_s, bias)
+        before = peak_ref[block, :]
+        peak = jnp.maximum(before[:, 0:1], peak_of(chunks))
         factor = jnp.exp2((before - peak) * EXP_SCALE)
-        added = jnp.dot(weights, value_s[...], preferred_element_type=jnp.float32)
-        blended = acc_ref[tile, :, 0:HEAD] * factor + added[:, 0:HEAD]
-        total = acc_ref[tile, :, HEAD:] * factor + added[:, HEAD:]
-        out_ref[tile] = (blended / total).astype(jnp.bfloat16)
-
-
-def fetch_kernel(weight_ref, out_ref, sem):
-    copy = pltpu.make_async_copy(weight_ref.at[:, pl.ds(0, out_ref.shape[1])], out_ref, sem)
-    copy.start()
-    copy.wait()
-
-
-def project_kernel(attended_ref, ready_ref, weight_ref, out_ref, weight_s, sems):
-    ready = ready_ref.shape[1]
+        added = weighted(chunks, peak, value_s)
+        blended = acc_ref[block, 0:HEAD] * factor + added[:, 0:HEAD]
+        total = acc_ref[block, HEAD:] * factor + added[:, HEAD:]
+        out_ref[block, :] = (blended / total).astype(jnp.bfloat16)
+
+
+def fetch_kernel(weight_ref, *refs):
+    sems = refs[-1]
+    copies = []
+    start = 0
+    for index, part_ref in enumerate(refs[:-1]):
+        columns = part_ref.shape[1]
+        copies.append(pltpu.make_async_copy(weight_ref.at[:, pl.ds(start, columns)], part_ref, sems.at[index]))
+        copies[index].start()
+        start += columns
+    for copy in copies:
+        copy.wait()
+
+
+def project_kernel(attended_ref, *refs):
+    ready_refs = refs[: len(READY)]
+    weight_ref, out_ref, weight_s, sems = refs[len(READY) :]
     chunks = sems.shape[0]
     columns = weight_s.shape[1] // chunks
     copies = []
     for chunk in range(chunks):
-        start = chunk * columns
-        source = weight_ref.at[:, pl.ds(ready + start, columns)]
-        copies.append(pltpu.make_async_copy(source, weight_s.at[:, pl.ds(start, columns)], sems.at[chunk]))
+        part = pl.ds(chunk * columns, columns)
+        source = weight_ref.at[:, pl.ds(sum(READY) + chunk * columns, columns)]
+        copies.append(pltpu.make_async_copy(source, weight_s.at[:, part], sems.at[chunk]))
         copies[chunk].start()
     attended = jnp.concatenate([attended_ref[head] for head in range(GROUP)], axis=1)
 
     def projected(weight):
         return jnp.dot(attended, weight, preferred_element_type=jnp.float32).astype(jnp.bfloat16)
 
-    out_ref[:, 0:ready] = projected(ready_ref[...])
+    start = 0
+    for ready_ref in ready_refs:
+        out_ref[:, start : start + ready_ref.shape[1]] = projected(ready_ref[...])
+        start += ready_ref.shape[1]
     for chunk in range(chunks):
-        start = chunk * columns
         copies[chunk].wait()
-        out_ref[:, ready + start : ready + start + columns] = projected(weight_s[:, start : start + columns])
+        out_ref[:, start : start + columns] = projected(weight_s[:, chunk * columns : (chunk + 1) * columns])
+        start += columns
 
 
 def final_kernel(
@@ -304,7 +350,7 @@
     groups = [[int(t) * 2 + kind for t in tiles] for kind in range(2) for tiles in kinds[kind]]
     across = [(t * 2 + kind, int(partners[kind, t]) * 2 + kind) for t in range(TILES) for kind in range(2)]
 
-    per_step = 4
+    per_step = 8
     wide = per_step * HEAD
     rope = jnp.asarray(rope_tables())
 
@@ -346,14 +392,15 @@
     far = lax.ppermute(own, mesh_axes, across)
     queries = lax.all_to_all(queries, mesh_axes, 0, 0, axis_index_groups=groups, tiled=True)
 
+    queries = queries.reshape(QUERIES, HEAD)
     table = jnp.asarray(key_tables())
     acc, peak = pl.pallas_call(
         local_kernel,
         in_specs=[SMEM, SMEM, SMEM] + [VMEM] * 3,
         out_specs=(VMEM, VMEM),
         out_shape=(
-            jax.ShapeDtypeStruct((GROUP, PIX, 2 * HEAD), jnp.float32),
-            jax.ShapeDtypeStruct((GROUP, PIX, HEAD), jnp.float32),
+            jax.ShapeDtypeStruct((QUERIES, 2 * HEAD), jnp.float32),
+            jax.ShapeDtypeStruct((QUERIES, HEAD), jnp.float32),
         ),
         scratch_shapes=[pltpu.VMEM((HALF_KEYS, HEAD), bf16), pltpu.VMEM((HALF_KEYS, 2 * HEAD), bf16)],
         compiler_params=params(16),
@@ -363,32 +410,32 @@
         remote_kernel,
         in_specs=[SMEM, SMEM, SMEM] + [VMEM] * 5,
         out_specs=VMEM,
-        out_shape=jax.ShapeDtypeStruct((GROUP, PIX, HEAD), bf16),
+        out_shape=jax.ShapeDtypeStruct((QUERIES, HEAD), bf16),
         scratch_shapes=[pltpu.VMEM((HALF_KEYS, HEAD), bf16), pltpu.VMEM((HALF_KEYS, 2 * HEAD), bf16)],
         compiler_params=params(16),
         name="attend_far",
     )(group, image_size, text_len, table, queries, far, acc, peak)
+    attended = attended.reshape(GROUP, PIX, HEAD)
     attended = lax.all_to_all(attended, mesh_axes, 0, 0, axis_index_groups=groups, tiled=True)
 
-    ready = model // 2
-    first_half = pl.pallas_call(
+    ready = pl.pallas_call(
         fetch_kernel,
         in_specs=[HBM],
-        out_specs=VMEM,
-        out_shape=jax.ShapeDtypeStruct((width, ready), bf16),
-        scratch_shapes=[pltpu.SemaphoreType.DMA],
+        out_specs=(VMEM,) * len(READY),
+        out_shape=tuple(jax.ShapeDtypeStruct((width, columns), bf16) for columns in READY),
+        scratch_shapes=[pltpu.SemaphoreType.DMA((len(READY),))],
         compiler_params=params(48),
         name="fetch_weight",
     )(out_weight)
     partial = pl.pallas_call(
         project_kernel,
-        in_specs=[VMEM, VMEM, HBM],
+        in_specs=[VMEM] * (1 + len(READY)) + [HBM],
         out_specs=VMEM,
         out_shape=jax.ShapeDtypeStruct((PIX, model), bf16),
-        scratch_shapes=[pltpu.VMEM((width, model - ready), bf16), pltpu.SemaphoreType.DMA((3,))],
+        scratch_shapes=[pltpu.VMEM((width, model - sum(READY)), bf16), pltpu.SemaphoreType.DMA((2,))],
         compiler_params=params(48),
         name="project",
-    )(attended, first_half, out_weight)
+    )(attended, *ready, out_weight)
     other = lax.ppermute(partial, "tp", [(0, 1), (1, 0)])
 
     local = np.stack([np.arange(PIX) // TILE_W, np.arange(PIX) % TILE_W]).astype(np.int32)

time: 70.3 us -> 70 us (level)
  transfers between devices with their start and end apart: 5 -> 5, of which waited for: 4 -> 4; matrix products, arithmetic and copies ran while one was open for 0% -> 0% of each run, Pallas kernels for 11% -> 10%
where the time goes in v7:
time: 70 us; the launch traced here: 69.5 us
  waiting for transfers between devices  28.6 us (41%)
  starting transfers between devices  20.1 us (29%)
  Pallas kernels  18.6 us (27%)
  between operations  2.13 us (3%)
    all_to_all x1, waiting for transfers between devices, shards(): lax.all_to_all(key_value, mesh_axes, 0, 0, axis_index_groups=groups, tile...  11.7 us
    all_to_all x1, waiting for transfers between devices, shards(): lax.all_to_all(queries, mesh_axes, 0, 0, axis_index_groups=groups, tiled=...  10.2 us
    all_to_all x1, starting transfers between devices, shards(): lax.all_to_all(key_value, mesh_axes, 0, 0, axis_index_groups=groups, tile...  7.59 us
    all_to_all x1, waiting for transfers between devices, shards(): lax.all_to_all(attended, mesh_axes, 0, 0, axis_index_groups=groups, tiled...  5.32 us
    all_to_all x1, starting transfers between devices, shards(): lax.all_to_all(attended, mesh_axes, 0, 0, axis_index_groups=groups, tiled...  4.22 us
    pallas_call x1, Pallas kernels, shards(): pl.pallas_call(remote_kernel, in_specs=[SMEM, SMEM, SMEM] + [VMEM] * 5, o...  3.82 us
    all_to_all x1, starting transfers between devices, shards(): lax.all_to_all(queries, mesh_axes, 0, 0, axis_index_groups=groups, tiled=...  3.42 us
    ppermute x1, starting transfers between devices, shards(): other = lax.ppermute(partial, 'tp', [(0, 1), (1, 0)])  3.02 us
  transfers between devices with their start and end apart: 5, of which 4 were waited for; matrix products, arithmetic and copies ran while one was open for 0% of the time, Pallas kernels for 10%

profile of v7, /device:TPU:1, one launch (start us, length us, event | category | flops | bytes accessed | tf_op | source)
XLA Modules:
  0.0 69.5 jit_solution(11050000997040764384)
XLA Ops:
  0.6 2.9 %prepare_keys.1 = bf16[8,352,128]{2,1,0:T(8,128)(2,1)} custom-call(s32[1]{0:T(128)} %bitcast.tile_ref, bf16[3,144,1024]{2,1,0:T(8,128)(2,1)} %bitcast.36, bf16[3,144,1024]{2,1,0:T(8,128)(2,1)} %bitcast.37, bf16[32,2,1024]{2,1,0:T(2,128)(2,1)} %text_ref.1, f32[1,128]{1,0:T(1,128)} %bitcast.40, f32[16,2,144,128]{3,2,1,0:T(8,128)} %constant.53.clone.table_ref), custom_call_target="tpu_custom_call" | custom-call | tf_op jit(solution)/shard_map/prepare_keys/pallas_call | solution.py:362
  3.5 0.0 copy-start.3
  3.5 0.0 copy-start.8
  3.5 7.6 %all-to-all-start = ((bf16[8,352,128]{2,1,0:T(8,128)(2,1)}), bf16[8,352,128]{2,1,0:T(8,128)(2,1)S(1)}, u32[]{:S(2)}, u32[]{:S(2)}) async-start(bf16[8,352,128]{2,1,0:T(8,128)(2,1)} %prepare_keys.1), calls=%async_computation | async-start | bytes 1441792 | tf_op jit(solution)/shard_map/all_to_all | solution.py:379
  11.1 2.1 %prepare_queries.1 = bf16[8,144,128]{2,1,0:T(8,128)(2,1)} custom-call(s32[1]{0:T(128)} %bitcast.tile_ref, bf16[3,144,1024]{2,1,0:T(8,128)(2,1)} %bitcast.38, f32[1,128]{1,0:T(1,128)} %bitcast.39, f32[16,2,144,128]{3,2,1,0:T(8,128)} %constant.53.clone.table_ref), custom_call_target="tpu_custom_call" | custom-call | tf_op jit(solution)/shard_map/prepare_queries/pallas_call | solution.py:380
  13.3 11.7 %all-to-all-done.own_ref = bf16[8,352,128]{2,1,0:T(8,128)(2,1)S(1)} async-done(((bf16[8,352,128]{2,1,0:T(8,128)(2,1)}), bf16[8,352,128]{2,1,0:T(8,128)(2,1)S(1)}, u32[]{:S(2)}, u32[]{:S(2)}) %all-to-all-start) | async-done | bytes 720928 | tf_op jit(solution)/shard_map/all_to_all | solution.py:379
  25.0 1.9 %collective-permute-start = (bf16[8,352,128]{2,1,0:T(8,128)(2,1)S(1)}, bf16[8,352,128]{2,1,0:T(8,128)(2,1)S(1)}, u32[]{:S(2)}, u32[]{:S(2)}) collective-permute-start(bf16[8,352,128]{2,1,0:T(8,128)(2,1)S(1)} %all-to-all-done.own_ref), channel_id=1, source_target_pairs={{0,16},{1,7},{2,18},{3,5},{4,20},{5,3},{6,22},{7,1},{8,24},{9,15},... | collective-permute-start | bytes 2162696 | tf_op jit(solution)/shard_map/ppermute | solution.py:392
  26.9 3.4 %all-to-all-start.1 = ((bf16[8,144,128]{2,1,0:T(8,128)(2,1)}), bf16[8,144,128]{2,1,0:T(8,128)(2,1)S(1)}, u32[]{:S(2)}, u32[]{:S(2)}) async-start(bf16[8,144,128]{2,1,0:T(8,128)(2,1)} %prepare_queries.1), calls=%async_computation.1 | async-start | bytes 589824 | tf_op jit(solution)/shard_map/all_to_all | solution.py:393
  31.0 0.1 pad_add_fusion.group_ref
  31.1 10.2 %all-to-all-done.1 = bf16[8,144,128]{2,1,0:T(8,128)(2,1)S(1)} async-done(((bf16[8,144,128]{2,1,0:T(8,128)(2,1)}), bf16[8,144,128]{2,1,0:T(8,128)(2,1)S(1)}, u32[]{:S(2)}, u32[]{:S(2)}) %all-to-all-start.1) | async-done | bytes 294944 | tf_op jit(solution)/shard_map/all_to_all | solution.py:393
  41.2 0.0 copy-done.3
  41.2 0.0 copy-done.8
  41.2 2.8 %attend_local.1 = (f32[1152,256]{1,0:T(8,128)S(1)}, f32[1152,128]{1,0:T(8,128)S(1)}) custom-call(s32[2]{0:T(128)S(1)} %pad_add_fusion.group_ref, s32[2]{0:T(128)S(1)} %copy-done.8, s32[1]{0:T(128)S(6)} %copy.21.text_len_ref, s32[4,3,1408]{2,1,0:T(4,128)S(1)} %copy-done.3, bf16[1152,128]{1,0:T(8,128)(2,1)S(1)} %bitcast.26, ...), custom_call_target="tpu_custom_call" | custom-call | tf_op jit(solution)/shard_map/attend_local/pallas_call | solution.py:397
  44.1 0.0 collective-permute-done.far_ref
  44.1 3.8 %attend_far.1 = bf16[1152,128]{1,0:T(8,128)(2,1)} custom-call(s32[2]{0:T(128)S(1)} %pad_add_fusion.group_ref, s32[2]{0:T(128)S(1)} %copy-done.8, s32[1]{0:T(128)S(6)} %copy.21.text_len_ref, s32[4,3,1408]{2,1,0:T(4,128)S(1)} %copy-done.3, bf16[1152,128]{1,0:T(8,128)(2,1)S(1)} %bitcast.27, bf16[8,352,128]{2,1,0:T(8,128)(2,1)S(1)} %collective-permute-done.far_ref, ...), custom_call_target="tpu_custom_call" | custom-call | tf_op jit(solution)/shard_map/attend_far/pallas_call | solution.py:409
  47.9 4.2 %all-to-all-start.2 = ((bf16[8,144,128]{2,1,0:T(8,128)(2,1)}), bf16[8,144,128]{2,1,0:T(8,128)(2,1)S(1)}, u32[]{:S(2)}, u32[]{:S(2)}) async-start(bf16[8,144,128]{2,1,0:T(8,128)(2,1)} %bitcast.9), calls=%async_computation.2 | async-start | bytes 589824 | tf_op jit(solution)/shard_map/all_to_all | solution.py:419
  52.1 1.9 %fetch_weight.1.refs_0_ = bf16[1024,1536]{1,0:T(8,128)(2,1)S(1)} custom-call(bf16[1024,3072]{1,0:T(8,128)(2,1)} %refs_1_.1), custom_call_target="tpu_custom_call" | custom-call | tf_op jit(solution)/shard_map/fetch_weight/pallas_call | solution.py:421
  54.0 0.0 copy-start.4
  54.0 0.0 copy-start.5
  54.0 0.0 copy-start.6
  54.0 0.0 copy-start.7
  54.1 0.0 copy-start.9
  54.1 0.0 copy-start.10
  54.1 5.3 %all-to-all-done.2.attended_ref = bf16[8,144,128]{2,1,0:T(8,128)(2,1)S(1)} async-done(((bf16[8,144,128]{2,1,0:T(8,128)(2,1)}), bf16[8,144,128]{2,1,0:T(8,128)(2,1)S(1)}, u32[]{:S(2)}, u32[]{:S(2)}) %all-to-all-start.2) | async-done | bytes 294944 | tf_op jit(solution)/shard_map/all_to_all | solution.py:419
  59.4 0.0 copy-start
  59.4 0.0 copy-start.1
  59.4 0.0 copy-start.2
  59.4 2.5 %project.1.own_ref = bf16[144,3072]{1,0:T(8,128)(2,1)S(1)} custom-call(bf16[8,144,128]{2,1,0:T(8,128)(2,1)S(1)} %all-to-all-done.2.attended_ref, bf16[1024,1536]{1,0:T(8,128)(2,1)S(1)} %fetch_weight.1.refs_0_, bf16[1024,3072]{1,0:T(8,128)(2,1)} %refs_1_.1), custom_call_target="tpu_custom_call" | custom-call | tf_op jit(solution)/shard_map/project/pallas_call | solution.py:430
  62.0 3.0 %collective-permute-start.1 = (bf16[144,3072]{1,0:T(8,128)(2,1)S(1)}, bf16[144,3072]{1,0:T(8,128)(2,1)S(1)}, u32[]{:S(2)}, u32[]{:S(2)}) collective-permute-start(bf16[144,3072]{1,0:T(8,128)(2,1)S(1)} %project.1.own_ref), channel_id=1, source_target_pairs={{0,1},{1,0},{2,3},{3,2},{4,5},{5,4},{6,7},{7,6},{8,9},{9,8},{10,11... | collective-permute-start | bytes 2654216 | tf_op jit(solution)/shard_map/ppermute | solution.py:439
  65.6 1.4 %collective-permute-done.1.other_ref = bf16[144,3072]{1,0:T(8,128)(2,1)S(1)} collective-permute-done((bf16[144,3072]{1,0:T(8,128)(2,1)S(1)}, bf16[144,3072]{1,0:T(8,128)(2,1)S(1)}, u32[]{:S(2)}, u32[]{:S(2)}) %collective-permute-start.1) | collective-permute-done | bytes 884768 | tf_op jit(solution)/shard_map/ppermute | solution.py:439
  67.0 0.0 copy-done.4
  67.0 0.0 copy-done.5
  67.0 0.0 copy-done.6
  67.0 0.0 copy-done.7
  67.0 0.0 copy-done.9
  67.1 0.0 copy-done.10
  67.1 0.0 copy-done
  67.1 0.0 copy-done.1
  67.1 0.0 copy-done.2
  67.1 2.4 %final_layer.1 = (f32[64,144]{1,0:T(8,128)}, f32[64,144]{1,0:T(8,128)}) custom-call(s32[1]{0:T(128)} %bitcast.tile_ref, s32[2]{0:T(128)S(1)} %copy-done.8, s32[1]{0:T(128)S(6)} %copy.22.timestep_ref, s32[2,144]{1,0:T(2,128)S(1)} %copy-done.9, bf16[144,3072]{1,0:T(8,128)(2,1)S(1)} %project.1.own_ref, bf16[144,3072]{1,0:T(8,128)(2,1)S(1)} %collective-permute-done.1.other_ref, ...), custom_call_target="tpu_custom_call" | custom-call | tf_op jit(solution)/shard_map/final_layer/pallas_call | solution.py:442
Async XLA Ops:
  3.5 37.7 %copy-start.3 = (s32[4,3,1408]{2,1,0:T(4,128)S(1)}, s32[4,3,1408]{2,1,0:T(4,128)}, u32[]{:S(2)}) copy-start(s32[4,3,1408]{2,1,0:T(4,128)} %constant.54.clone.table_ref) | copy-start | bytes 202756
  3.5 37.7 %copy-start.8 = (s32[2]{0:T(128)S(1)}, s32[2]{0:T(128)}, u32[]{:S(2)}) copy-start(s32[2]{0:T(128)} %size_ref.5) | copy-start | bytes 28
  3.5 21.5 %all-to-all-start = ((bf16[8,352,128]{2,1,0:T(8,128)(2,1)}), bf16[8,352,128]{2,1,0:T(8,128)(2,1)S(1)}, u32[]{:S(2)}, u32[]{:S(2)}) async-start(bf16[8,352,128]{2,1,0:T(8,128)(2,1)} %prepare_keys.1), calls=%async_computation | async-start | bytes 1441792 | tf_op jit(solution)/shard_map/all_to_all | solution.py:379
  25.0 19.0 %collective-permute-start = (bf16[8,352,128]{2,1,0:T(8,128)(2,1)S(1)}, bf16[8,352,128]{2,1,0:T(8,128)(2,1)S(1)}, u32[]{:S(2)}, u32[]{:S(2)}) collective-permute-start(bf16[8,352,128]{2,1,0:T(8,128)(2,1)S(1)} %all-to-all-done.own_ref), channel_id=1, source_target_pairs={{0,16},{1,7},{2,18},{3,5},{4,20},{5,3},{6,22},{7,1},{8,24},{9,15},... | collective-permute-start | bytes 2162696 | tf_op jit(solution)/shard_map/ppermute | solution.py:392
  26.9 14.4 %all-to-all-start.1 = ((bf16[8,144,128]{2,1,0:T(8,128)(2,1)}), bf16[8,144,128]{2,1,0:T(8,128)(2,1)S(1)}, u32[]{:S(2)}, u32[]{:S(2)}) async-start(bf16[8,144,128]{2,1,0:T(8,128)(2,1)} %prepare_queries.1), calls=%async_computation.1 | async-start | bytes 589824 | tf_op jit(solution)/shard_map/all_to_all | solution.py:393
  47.9 11.5 %all-to-all-start.2 = ((bf16[8,144,128]{2,1,0:T(8,128)(2,1)}), bf16[8,144,128]{2,1,0:T(8,128)(2,1)S(1)}, u32[]{:S(2)}, u32[]{:S(2)}) async-start(bf16[8,144,128]{2,1,0:T(8,128)(2,1)} %bitcast.9), calls=%async_computation.2 | async-start | bytes 589824 | tf_op jit(solution)/shard_map/all_to_all | solution.py:419
  54.0 13.0 %copy-start.4 = (f32[1,144,64]{1,2,0:T(8,128)S(1)}, f32[1,144,64]{1,2,0:T(8,128)}, u32[]{:S(2)}) copy-start(f32[1,144,64]{1,2,0:T(8,128)} %param.31) | copy-start | bytes 110596
  54.0 13.0 %copy-start.5 = (f32[3072]{0:T(1024)S(1)}, f32[3072]{0:T(1024)}, u32[]{:S(2)}) copy-start(f32[3072]{0:T(1024)} %param.26) | copy-start | bytes 36868
  54.0 13.0 %copy-start.6 = (f32[3072]{0:T(1024)S(1)}, f32[3072]{0:T(1024)}, u32[]{:S(2)}) copy-start(f32[3072]{0:T(1024)} %param.27) | copy-start | bytes 36868
  54.0 13.0 %copy-start.7 = (f32[3072]{0:T(1024)S(1)}, f32[3072]{0:T(1024)}, u32[]{:S(2)}) copy-start(f32[3072]{0:T(1024)} %param.28) | copy-start | bytes 36868
  54.1 13.0 %copy-start.9 = (s32[2,144]{1,0:T(2,128)S(1)}, s32[2,144]{1,0:T(2,128)}, u32[]{:S(2)}) copy-start(s32[2,144]{1,0:T(2,128)} %constant.55.clone.local_ref) | copy-start | bytes 3460
  54.1 13.0 %copy-start.10 = (f32[64]{0:T(128)S(1)}, f32[64]{0:T(128)}, u32[]{:S(2)}) copy-start(f32[64]{0:T(128)} %param.30) | copy-start | bytes 772
  59.4 7.7 %copy-start = (bf16[1,144,3072]{2,1,0:T(8,128)(2,1)S(1)}, bf16[1,144,3072]{2,1,0:T(8,128)(2,1)}, u32[]{:S(2)}) copy-start(bf16[1,144,3072]{2,1,0:T(8,128)(2,1)} %param.24) | copy-start | bytes 2654212
  59.4 7.7 %copy-start.1 = (bf16[1,144,3072]{2,1,0:T(8,128)(2,1)S(1)}, bf16[1,144,3072]{2,1,0:T(8,128)(2,1)}, u32[]{:S(2)}) copy-start(bf16[1,144,3072]{2,1,0:T(8,128)(2,1)} %param.25) | copy-start | bytes 2654212
  59.4 7.7 %copy-start.2 = (bf16[3072,64]{0,1:T(8,128)(2,1)S(1)}, bf16[3072,64]{0,1:T(8,128)(2,1)}, u32[]{:S(2)}) copy-start(bf16[3072,64]{0,1:T(8,128)(2,1)} %param.29) | copy-start | bytes 1179652
  62.0 5.1 %collective-permute-start.1 = (bf16[144,3072]{1,0:T(8,128)(2,1)S(1)}, bf16[144,3072]{1,0:T(8,128)(2,1)S(1)}, u32[]{:S(2)}, u32[]{:S(2)}) collective-permute-start(bf16[144,3072]{1,0:T(8,128)(2,1)S(1)} %project.1.own_ref), channel_id=1, source_target_pairs={{0,1},{1,0},{2,3},{3,2},{4,5},{5,4},{6,7},{7,6},{8,9},{9,8},{10,11... | collective-permute-start | bytes 2654216 | tf_op jit(solution)/shard_map/ppermute | solution.py:439

commit v8 on v7

--- a/solution.py
+++ b/solution.py
@@ -60,8 +60,8 @@
 def group_tiles():
     lows = np.arange(TILES // GRID_X)[:, None] * GRID_X
     kinds = [
+        [(lows + np.array([0, 1])).reshape(-1), (lows + np.array([3, 2])).reshape(-1)],
         [np.arange(GROUP), np.arange(GROUP) + GROUP],
-        [(lows + np.array([0, 1])).reshape(-1), (lows + np.array([3, 2])).reshape(-1)],
     ]
     partners = np.zeros((2, TILES), np.int64)
     for kind, (near, far) in enumerate(kinds):
@@ -342,7 +342,7 @@
     latents = final_weight.shape[1]
     tile = lax.axis_index("tile").astype(jnp.int32).reshape(1)
     kind = lax.axis_index("tp").astype(jnp.int32)
-    which = jnp.where(kind == 0, tile[0] // GROUP, tile[0] % GRID_X // 2)
+    which = jnp.where(kind == 1, tile[0] // GROUP, tile[0] % GRID_X // 2)
     group = jnp.stack([2 * kind + which, 2 * kind + 1 - which])
     triple = image_qkv.reshape(PIX, 3, width).transpose(1, 0, 2)
     kinds, partners = group_tiles()

time: 70 us -> 68.8 us (0.983)
  waiting for transfers between devices: 28.6 us -> 24.9 us
  starting transfers between devices: 20.1 us -> 22.7 us
    ppermute x1, waiting for transfers between devices: 0.01 us -> 5.91 us  [shards(): far = lax.ppermute(own, mesh_axes, across)]
    all_to_all x1, waiting for transfers between devices: 11.7 us -> 6.39 us  [shards(): lax.all_to_all(key_value, mesh_axes, 0, 0, axis_index_groups=groups, tile...]
    all_to_all x1, waiting for transfers between devices: 10.2 us -> 5.71 us  [shards(): lax.all_to_all(queries, mesh_axes, 0, 0, axis_index_groups=groups, tiled=...]
    ppermute x1, starting transfers between devices: 1.87 us -> 5.01 us  [shards(): far = lax.ppermute(own, mesh_axes, across)]
    all_to_all x1, starting transfers between devices: 3.42 us -> 5.75 us  [shards(): lax.all_to_all(queries, mesh_axes, 0, 0, axis_index_groups=groups, tiled=...]
    ppermute x1, starting transfers between devices: 3.02 us -> 1.61 us  [shards(): other = lax.ppermute(partial, 'tp', [(0, 1), (1, 0)])]
    all_to_all x1, starting transfers between devices: 7.59 us -> 6.51 us  [shards(): lax.all_to_all(key_value, mesh_axes, 0, 0, axis_index_groups=groups, tile...]
  transfers between devices with their start and end apart: 5 -> 5, of which waited for: 4 -> 5; matrix products, arithmetic and copies ran while one was open for 0% -> 0% of each run, Pallas kernels for 10% -> 10%
where the time goes in v8:
time: 68.8 us; the launch traced here: 68.3 us
  waiting for transfers between devices  24.9 us (36%)
  starting transfers between devices  22.7 us (33%)
  Pallas kernels  18.6 us (27%)
  between operations  2.06 us (3%)
    all_to_all x1, starting transfers between devices, shards(): lax.all_to_all(key_value, mesh_axes, 0, 0, axis_index_groups=groups, tile...  6.51 us
    all_to_all x1, waiting for transfers between devices, shards(): lax.all_to_all(key_value, mesh_axes, 0, 0, axis_index_groups=groups, tile...  6.39 us
    ppermute x1, waiting for transfers between devices, shards(): far = lax.ppermute(own, mesh_axes, across)  5.91 us
    all_to_all x1, starting transfers between devices, shards(): lax.all_to_all(queries, mesh_axes, 0, 0, axis_index_groups=groups, tiled=...  5.75 us
    all_to_all x1, waiting for transfers between devices, shards(): lax.all_to_all(queries, mesh_axes, 0, 0, axis_index_groups=groups, tiled=...  5.71 us
    all_to_all x1, waiting for transfers between devices, shards(): lax.all_to_all(attended, mesh_axes, 0, 0, axis_index_groups=groups, tiled...  5.44 us
    ppermute x1, starting transfers between devices, shards(): far = lax.ppermute(own, mesh_axes, across)  5.01 us
    pallas_call x1, Pallas kernels, shards(): pl.pallas_call(remote_kernel, in_specs=[SMEM, SMEM, SMEM] + [VMEM] * 5, o...  3.81 us
  transfers between devices with their start and end apart: 5, of which 5 were waited for; matrix products, arithmetic and copies ran while one was open for 0% of the time, Pallas kernels for 10%

profile of v8, /device:TPU:1, one launch (start us, length us, event | category | flops | bytes accessed | tf_op | source)
XLA Modules:
  0.0 68.3 jit_solution(12612802897464750713)
XLA Ops:
  0.6 2.9 %prepare_keys.1 = bf16[8,352,128]{2,1,0:T(8,128)(2,1)} custom-call(s32[1]{0:T(128)} %bitcast.tile_ref, bf16[3,144,1024]{2,1,0:T(8,128)(2,1)} %bitcast.36, bf16[3,144,1024]{2,1,0:T(8,128)(2,1)} %bitcast.37, bf16[32,2,1024]{2,1,0:T(2,128)(2,1)} %text_ref.1, f32[1,128]{1,0:T(1,128)} %bitcast.40, f32[16,2,144,128]{3,2,1,0:T(8,128)} %constant.52.clone.table_ref), custom_call_target="tpu_custom_call" | custom-call | tf_op jit(solution)/shard_map/prepare_keys/pallas_call | solution.py:362
  3.5 0.0 copy-start.3
  3.5 0.0 copy-start.8
  3.5 6.5 %all-to-all-start = ((bf16[8,352,128]{2,1,0:T(8,128)(2,1)}), bf16[8,352,128]{2,1,0:T(8,128)(2,1)S(1)}, u32[]{:S(2)}, u32[]{:S(2)}) async-start(bf16[8,352,128]{2,1,0:T(8,128)(2,1)} %prepare_keys.1), calls=%async_computation | async-start | bytes 1441792 | tf_op jit(solution)/shard_map/all_to_all | solution.py:379
  10.1 2.1 %prepare_queries.1 = bf16[8,144,128]{2,1,0:T(8,128)(2,1)} custom-call(s32[1]{0:T(128)} %bitcast.tile_ref, bf16[3,144,1024]{2,1,0:T(8,128)(2,1)} %bitcast.38, f32[1,128]{1,0:T(1,128)} %bitcast.39, f32[16,2,144,128]{3,2,1,0:T(8,128)} %constant.52.clone.table_ref), custom_call_target="tpu_custom_call" | custom-call | tf_op jit(solution)/shard_map/prepare_queries/pallas_call | solution.py:380
  12.2 6.4 %all-to-all-done.own_ref = bf16[8,352,128]{2,1,0:T(8,128)(2,1)S(1)} async-done(((bf16[8,352,128]{2,1,0:T(8,128)(2,1)}), bf16[8,352,128]{2,1,0:T(8,128)(2,1)S(1)}, u32[]{:S(2)}, u32[]{:S(2)}) %all-to-all-start) | async-done | bytes 720928 | tf_op jit(solution)/shard_map/all_to_all | solution.py:379
  18.6 5.0 %collective-permute-start = (bf16[8,352,128]{2,1,0:T(8,128)(2,1)S(1)}, bf16[8,352,128]{2,1,0:T(8,128)(2,1)S(1)}, u32[]{:S(2)}, u32[]{:S(2)}) collective-permute-start(bf16[8,352,128]{2,1,0:T(8,128)(2,1)S(1)} %all-to-all-done.own_ref), channel_id=1, source_target_pairs={{0,6},{1,17},{2,4},{3,19},{4,2},{5,21},{6,0},{7,23},{8,14},{9,25},... | collective-permute-start | bytes 2162696 | tf_op jit(solution)/shard_map/ppermute | solution.py:392
  23.6 5.8 %all-to-all-start.1 = ((bf16[8,144,128]{2,1,0:T(8,128)(2,1)}), bf16[8,144,128]{2,1,0:T(8,128)(2,1)S(1)}, u32[]{:S(2)}, u32[]{:S(2)}) async-start(bf16[8,144,128]{2,1,0:T(8,128)(2,1)} %prepare_queries.1), calls=%async_computation.1 | async-start | bytes 589824 | tf_op jit(solution)/shard_map/all_to_all | solution.py:393
  30.0 0.1 pad_add_fusion.group_ref
  30.1 5.7 %all-to-all-done.1 = bf16[8,144,128]{2,1,0:T(8,128)(2,1)S(1)} async-done(((bf16[8,144,128]{2,1,0:T(8,128)(2,1)}), bf16[8,144,128]{2,1,0:T(8,128)(2,1)S(1)}, u32[]{:S(2)}, u32[]{:S(2)}) %all-to-all-start.1) | async-done | bytes 294944 | tf_op jit(solution)/shard_map/all_to_all | solution.py:393
  35.8 0.0 copy-done.3
  35.8 0.0 copy-done.8
  35.8 2.8 %attend_local.1 = (f32[1152,256]{1,0:T(8,128)S(1)}, f32[1152,128]{1,0:T(8,128)S(1)}) custom-call(s32[2]{0:T(128)S(1)} %pad_add_fusion.group_ref, s32[2]{0:T(128)S(1)} %copy-done.8, s32[1]{0:T(128)S(6)} %copy.21.text_len_ref, s32[4,3,1408]{2,1,0:T(4,128)S(1)} %copy-done.3, bf16[1152,128]{1,0:T(8,128)(2,1)S(1)} %bitcast.26, ...), custom_call_target="tpu_custom_call" | custom-call | tf_op jit(solution)/shard_map/attend_local/pallas_call | solution.py:397
  38.6 5.9 %collective-permute-done.far_ref = bf16[8,352,128]{2,1,0:T(8,128)(2,1)S(1)} collective-permute-done((bf16[8,352,128]{2,1,0:T(8,128)(2,1)S(1)}, bf16[8,352,128]{2,1,0:T(8,128)(2,1)S(1)}, u32[]{:S(2)}, u32[]{:S(2)}) %collective-permute-start) | collective-permute-done | bytes 720928 | tf_op jit(solution)/shard_map/ppermute | solution.py:392
  44.5 3.8 %attend_far.1 = bf16[1152,128]{1,0:T(8,128)(2,1)} custom-call(s32[2]{0:T(128)S(1)} %pad_add_fusion.group_ref, s32[2]{0:T(128)S(1)} %copy-done.8, s32[1]{0:T(128)S(6)} %copy.21.text_len_ref, s32[4,3,1408]{2,1,0:T(4,128)S(1)} %copy-done.3, bf16[1152,128]{1,0:T(8,128)(2,1)S(1)} %bitcast.27, bf16[8,352,128]{2,1,0:T(8,128)(2,1)S(1)} %collective-permute-done.far_ref, ...), custom_call_target="tpu_custom_call" | custom-call | tf_op jit(solution)/shard_map/attend_far/pallas_call | solution.py:409
  48.3 3.8 %all-to-all-start.2 = ((bf16[8,144,128]{2,1,0:T(8,128)(2,1)}), bf16[8,144,128]{2,1,0:T(8,128)(2,1)S(1)}, u32[]{:S(2)}, u32[]{:S(2)}) async-start(bf16[8,144,128]{2,1,0:T(8,128)(2,1)} %bitcast.9), calls=%async_computation.2 | async-start | bytes 589824 | tf_op jit(solution)/shard_map/all_to_all | solution.py:419
  52.1 1.9 %fetch_weight.1.refs_0_ = bf16[1024,1536]{1,0:T(8,128)(2,1)S(1)} custom-call(bf16[1024,3072]{1,0:T(8,128)(2,1)} %refs_1_.1), custom_call_target="tpu_custom_call" | custom-call | tf_op jit(solution)/shard_map/fetch_weight/pallas_call | solution.py:421
  54.0 0.0 copy-start.4
  54.1 0.0 copy-start.5
  54.1 0.0 copy-start.6
  54.1 0.0 copy-start.7
  54.1 0.0 copy-start.9
  54.1 0.0 copy-start.10
  54.1 5.4 %all-to-all-done.2.attended_ref = bf16[8,144,128]{2,1,0:T(8,128)(2,1)S(1)} async-done(((bf16[8,144,128]{2,1,0:T(8,128)(2,1)}), bf16[8,144,128]{2,1,0:T(8,128)(2,1)S(1)}, u32[]{:S(2)}, u32[]{:S(2)}) %all-to-all-start.2) | async-done | bytes 294944 | tf_op jit(solution)/shard_map/all_to_all | solution.py:419
  59.6 0.0 copy-start
  59.6 0.0 copy-start.1
  59.6 0.0 copy-start.2
  59.6 2.6 %project.1.own_ref = bf16[144,3072]{1,0:T(8,128)(2,1)S(1)} custom-call(bf16[8,144,128]{2,1,0:T(8,128)(2,1)S(1)} %all-to-all-done.2.attended_ref, bf16[1024,1536]{1,0:T(8,128)(2,1)S(1)} %fetch_weight.1.refs_0_, bf16[1024,3072]{1,0:T(8,128)(2,1)} %refs_1_.1), custom_call_target="tpu_custom_call" | custom-call | tf_op jit(solution)/shard_map/project/pallas_call | solution.py:430
  62.1 1.6 %collective-permute-start.1 = (bf16[144,3072]{1,0:T(8,128)(2,1)S(1)}, bf16[144,3072]{1,0:T(8,128)(2,1)S(1)}, u32[]{:S(2)}, u32[]{:S(2)}) collective-permute-start(bf16[144,3072]{1,0:T(8,128)(2,1)S(1)} %project.1.own_ref), channel_id=1, source_target_pairs={{0,1},{1,0},{2,3},{3,2},{4,5},{5,4},{6,7},{7,6},{8,9},{9,8},{10,11... | collective-permute-start | bytes 2654216 | tf_op jit(solution)/shard_map/ppermute | solution.py:439
  64.4 1.4 %collective-permute-done.1.other_ref = bf16[144,3072]{1,0:T(8,128)(2,1)S(1)} collective-permute-done((bf16[144,3072]{1,0:T(8,128)(2,1)S(1)}, bf16[144,3072]{1,0:T(8,128)(2,1)S(1)}, u32[]{:S(2)}, u32[]{:S(2)}) %collective-permute-start.1) | collective-permute-done | bytes 884768 | tf_op jit(solution)/shard_map/ppermute | solution.py:439
  65.8 0.0 copy-done.4
  65.8 0.0 copy-done.5
  65.8 0.0 copy-done.6
  65.8 0.0 copy-done.7
  65.8 0.0 copy-done.9
  65.8 0.0 copy-done.10
  65.8 0.0 copy-done
  65.8 0.0 copy-done.1
  65.8 0.0 copy-done.2
  65.8 2.4 %final_layer.1 = (f32[64,144]{1,0:T(8,128)}, f32[64,144]{1,0:T(8,128)}) custom-call(s32[1]{0:T(128)} %bitcast.tile_ref, s32[2]{0:T(128)S(1)} %copy-done.8, s32[1]{0:T(128)S(6)} %copy.22.timestep_ref, s32[2,144]{1,0:T(2,128)S(1)} %copy-done.9, bf16[144,3072]{1,0:T(8,128)(2,1)S(1)} %project.1.own_ref, bf16[144,3072]{1,0:T(8,128)(2,1)S(1)} %collective-permute-done.1.other_ref, ...), custom_call_target="tpu_custom_call" | custom-call | tf_op jit(solution)/shard_map/final_layer/pallas_call | solution.py:442
Async XLA Ops:
  3.5 32.3 %copy-start.3 = (s32[4,3,1408]{2,1,0:T(4,128)S(1)}, s32[4,3,1408]{2,1,0:T(4,128)}, u32[]{:S(2)}) copy-start(s32[4,3,1408]{2,1,0:T(4,128)} %constant.53.clone.table_ref) | copy-start | bytes 202756
  3.5 32.3 %copy-start.8 = (s32[2]{0:T(128)S(1)}, s32[2]{0:T(128)}, u32[]{:S(2)}) copy-start(s32[2]{0:T(128)} %size_ref.5) | copy-start | bytes 28
  3.5 15.0 %all-to-all-start = ((bf16[8,352,128]{2,1,0:T(8,128)(2,1)}), bf16[8,352,128]{2,1,0:T(8,128)(2,1)S(1)}, u32[]{:S(2)}, u32[]{:S(2)}) async-start(bf16[8,352,128]{2,1,0:T(8,128)(2,1)} %prepare_keys.1), calls=%async_computation | async-start | bytes 1441792 | tf_op jit(solution)/shard_map/all_to_all | solution.py:379
  18.6 25.9 %collective-permute-start = (bf16[8,352,128]{2,1,0:T(8,128)(2,1)S(1)}, bf16[8,352,128]{2,1,0:T(8,128)(2,1)S(1)}, u32[]{:S(2)}, u32[]{:S(2)}) collective-permute-start(bf16[8,352,128]{2,1,0:T(8,128)(2,1)S(1)} %all-to-all-done.own_ref), channel_id=1, source_target_pairs={{0,6},{1,17},{2,4},{3,19},{4,2},{5,21},{6,0},{7,23},{8,14},{9,25},... | collective-permute-start | bytes 2162696 | tf_op jit(solution)/shard_map/ppermute | solution.py:392
  23.6 12.2 %all-to-all-start.1 = ((bf16[8,144,128]{2,1,0:T(8,128)(2,1)}), bf16[8,144,128]{2,1,0:T(8,128)(2,1)S(1)}, u32[]{:S(2)}, u32[]{:S(2)}) async-start(bf16[8,144,128]{2,1,0:T(8,128)(2,1)} %prepare_queries.1), calls=%async_computation.1 | async-start | bytes 589824 | tf_op jit(solution)/shard_map/all_to_all | solution.py:393
  48.3 11.2 %all-to-all-start.2 = ((bf16[8,144,128]{2,1,0:T(8,128)(2,1)}), bf16[8,144,128]{2,1,0:T(8,128)(2,1)S(1)}, u32[]{:S(2)}, u32[]{:S(2)}) async-start(bf16[8,144,128]{2,1,0:T(8,128)(2,1)} %bitcast.9), calls=%async_computation.2 | async-start | bytes 589824 | tf_op jit(solution)/shard_map/all_to_all | solution.py:419
  54.0 11.7 %copy-start.4 = (f32[1,144,64]{1,2,0:T(8,128)S(1)}, f32[1,144,64]{1,2,0:T(8,128)}, u32[]{:S(2)}) copy-start(f32[1,144,64]{1,2,0:T(8,128)} %param.31) | copy-start | bytes 110596
  54.1 11.7 %copy-start.5 = (f32[3072]{0:T(1024)S(1)}, f32[3072]{0:T(1024)}, u32[]{:S(2)}) copy-start(f32[3072]{0:T(1024)} %param.26) | copy-start | bytes 36868
  54.1 11.7 %copy-start.6 = (f32[3072]{0:T(1024)S(1)}, f32[3072]{0:T(1024)}, u32[]{:S(2)}) copy-start(f32[3072]{0:T(1024)} %param.27) | copy-start | bytes 36868
  54.1 11.7 %copy-start.7 = (f32[3072]{0:T(1024)S(1)}, f32[3072]{0:T(1024)}, u32[]{:S(2)}) copy-start(f32[3072]{0:T(1024)} %param.28) | copy-start | bytes 36868
  54.1 11.7 %copy-start.9 = (s32[2,144]{1,0:T(2,128)S(1)}, s32[2,144]{1,0:T(2,128)}, u32[]{:S(2)}) copy-start(s32[2,144]{1,0:T(2,128)} %constant.54.clone.local_ref) | copy-start | bytes 3460
  54.1 11.7 %copy-start.10 = (f32[64]{0:T(128)S(1)}, f32[64]{0:T(128)}, u32[]{:S(2)}) copy-start(f32[64]{0:T(128)} %param.30) | copy-start | bytes 772
  59.6 6.3 %copy-start = (bf16[1,144,3072]{2,1,0:T(8,128)(2,1)S(1)}, bf16[1,144,3072]{2,1,0:T(8,128)(2,1)}, u32[]{:S(2)}) copy-start(bf16[1,144,3072]{2,1,0:T(8,128)(2,1)} %param.24) | copy-start | bytes 2654212
  59.6 6.3 %copy-start.1 = (bf16[1,144,3072]{2,1,0:T(8,128)(2,1)S(1)}, bf16[1,144,3072]{2,1,0:T(8,128)(2,1)}, u32[]{:S(2)}) copy-start(bf16[1,144,3072]{2,1,0:T(8,128)(2,1)} %param.25) | copy-start | bytes 2654212
  59.6 6.3 %copy-start.2 = (bf16[3072,64]{0,1:T(8,128)(2,1)S(1)}, bf16[3072,64]{0,1:T(8,128)(2,1)}, u32[]{:S(2)}) copy-start(bf16[3072,64]{0,1:T(8,128)(2,1)} %param.29) | copy-start | bytes 1179652
  62.1 3.7 %collective-permute-start.1 = (bf16[144,3072]{1,0:T(8,128)(2,1)S(1)}, bf16[144,3072]{1,0:T(8,128)(2,1)S(1)}, u32[]{:S(2)}, u32[]{:S(2)}) collective-permute-start(bf16[144,3072]{1,0:T(8,128)(2,1)S(1)} %project.1.own_ref), channel_id=1, source_target_pairs={{0,1},{1,0},{2,3},{3,2},{4,5},{5,4},{6,7},{7,6},{8,9},{9,8},{10,11... | collective-permute-start | bytes 2654216 | tf_op jit(solution)/shard_map/ppermute | solution.py:439

commit v9 on v8

--- a/solution.py
+++ b/solution.py
@@ -24,7 +24,7 @@
 QUERY_BLOCK = QUERIES // 2
 FAR_BLOCK = QUERIES // 4
 KEY_CHUNK = 256
-READY = (1536,)
+READY = (1280,)
 DEAD = -1e30
 EXP_SCALE = HEAD ** (-0.5) * math.log2(math.e)
 
@@ -192,8 +192,23 @@
 
 
 def remote_kernel(
-    group_ref, size_ref, text_len_ref, table_ref, query_ref, far_ref, acc_ref, peak_ref, out_ref, key_s, value_s
+    group_ref,
+    size_ref,
+    text_len_ref,
+    table_ref,
+    query_ref,
+    far_ref,
+    acc_ref,
+    peak_ref,
+    weight_ref,
+    out_ref,
+    ready_ref,
+    key_s,
+    value_s,
+    sem,
 ):
+    fetch = pltpu.make_async_copy(weight_ref.at[:, pl.ds(0, READY[0])], ready_ref, sem)
+    fetch.start()
     bias = key_bias(table_ref, size_ref, text_len_ref, group_ref[1])
     stage(far_ref, key_s, value_s)
     blocks = [slice(start, start + FAR_BLOCK) for start in range(0, QUERIES, FAR_BLOCK)]
@@ -209,19 +224,7 @@
         blended = acc_ref[block, 0:HEAD] * factor + added[:, 0:HEAD]
         total = acc_ref[block, HEAD:] * factor + added[:, HEAD:]
         out_ref[block, :] = (blended / total).astype(jnp.bfloat16)
-
-
-def fetch_kernel(weight_ref, *refs):
-    sems = refs[-1]
-    copies = []
-    start = 0
-    for index, part_ref in enumerate(refs[:-1]):
-        columns = part_ref.shape[1]
-        copies.append(pltpu.make_async_copy(weight_ref.at[:, pl.ds(start, columns)], part_ref, sems.at[index]))
-        copies[index].start()
-        start += columns
-    for copy in copies:
-        copy.wait()
+    fetch.wait()
 
 
 def project_kernel(attended_ref, *refs):
@@ -406,27 +409,21 @@
         compiler_params=params(16),
         name="attend_local",
     )(group, image_size, text_len, table, queries, own)
-    attended = pl.pallas_call(
+    attended, *ready = pl.pallas_call(
         remote_kernel,
-        in_specs=[SMEM, SMEM, SMEM] + [VMEM] * 5,
-        out_specs=VMEM,
-        out_shape=jax.ShapeDtypeStruct((QUERIES, HEAD), bf16),
-        scratch_shapes=[pltpu.VMEM((HALF_KEYS, HEAD), bf16), pltpu.VMEM((HALF_KEYS, 2 * HEAD), bf16)],
-        compiler_params=params(16),
+        in_specs=[SMEM, SMEM, SMEM] + [VMEM] * 5 + [HBM],
+        out_specs=(VMEM, VMEM),
+        out_shape=(
+            jax.ShapeDtypeStruct((QUERIES, HEAD), bf16),
+            jax.ShapeDtypeStruct((width, READY[0]), bf16),
+        ),
+        scratch_shapes=[pltpu.VMEM((HALF_KEYS, HEAD), bf16), pltpu.VMEM((HALF_KEYS, 2 * HEAD), bf16), pltpu.SemaphoreType.DMA],
+        compiler_params=params(48),
         name="attend_far",
-    )(group, image_size, text_len, table, queries, far, acc, peak)
+    )(group, image_size, text_len, table, queries, far, acc, peak, out_weight)
     attended = attended.reshape(GROUP, PIX, HEAD)
     attended = lax.all_to_all(attended, mesh_axes, 0, 0, axis_index_groups=groups, tiled=True)
 
-    ready = pl.pallas_call(
-        fetch_kernel,
-        in_specs=[HBM],
-        out_specs=(VMEM,) * len(READY),
-        out_shape=tuple(jax.ShapeDtypeStruct((width, columns), bf16) for columns in READY),
-        scratch_shapes=[pltpu.SemaphoreType.DMA((len(READY),))],
-        compiler_params=params(48),
-        name="fetch_weight",
-    )(out_weight)
     partial = pl.pallas_call(
         project_kernel,
         in_specs=[VMEM] * (1 + len(READY)) + [HBM],

time: 68.8 us -> 68.7 us (level)
  blocking collectives: 0 us -> 11.4 us
  waiting for transfers between devices: 24.9 us -> 19.3 us
  starting transfers between devices: 22.7 us -> 19 us
  Pallas kernels: 18.6 us -> 16.5 us
    all_to_all x0 -> x1, blocking collectives: none -> 11.4 us  [shards(): lax.all_to_all(attended, mesh_axes, 0, 0, axis_index_groups=groups, tiled...]
    all_to_all x1 -> x0, waiting for transfers between devices: 5.44 us -> none  [shards(): lax.all_to_all(attended, mesh_axes, 0, 0, axis_index_groups=groups, tiled...]
    all_to_all x1 -> x0, starting transfers between devices: 3.81 us -> none  [shards(): lax.all_to_all(attended, mesh_axes, 0, 0, axis_index_groups=groups, tiled...]
    pallas_call x2 -> x1, Pallas kernels: 5.71 us -> 3.2 us  [shards(): pl.pallas_call(remote_kernel, in_specs=[SMEM, SMEM, SMEM] + [VMEM] * 5 +...]
  transfers between devices with their start and end apart: 5 -> 4, of which waited for: 5 -> 4; matrix products, arithmetic and copies ran while one was open for 0% -> 0% of each run, Pallas kernels for 10% -> 7%
where the time goes in v9:
time: 68.7 us; the launch traced here: 68.4 us
  waiting for transfers between devices  19.3 us (28%)
  starting transfers between devices  19 us (28%)
  Pallas kernels  16.5 us (24%)
  blocking collectives  11.4 us (17%)
  between operations  2.06 us (3%)
    all_to_all x1, blocking collectives, shards(): lax.all_to_all(attended, mesh_axes, 0, 0, axis_index_groups=groups, tiled...  11.4 us
    all_to_all x1, starting transfers between devices, shards(): lax.all_to_all(key_value, mesh_axes, 0, 0, axis_index_groups=groups, tile...  6.51 us
    all_to_all x1, waiting for transfers between devices, shards(): lax.all_to_all(key_value, mesh_axes, 0, 0, axis_index_groups=groups, tile...  6.38 us
    ppermute x1, waiting for transfers between devices, shards(): far = lax.ppermute(own, mesh_axes, across)  5.8 us
    all_to_all x1, starting transfers between devices, shards(): lax.all_to_all(queries, mesh_axes, 0, 0, axis_index_groups=groups, tiled=...  5.75 us
    all_to_all x1, waiting for transfers between devices, shards(): lax.all_to_all(queries, mesh_axes, 0, 0, axis_index_groups=groups, tiled=...  5.71 us
    ppermute x1, starting transfers between devices, shards(): far = lax.ppermute(own, mesh_axes, across)  5.01 us
    pallas_call x1, Pallas kernels, shards(): pl.pallas_call(remote_kernel, in_specs=[SMEM, SMEM, SMEM] + [VMEM] * 5 +...  3.2 us
  transfers between devices with their start and end apart: 4, of which 4 were waited for; matrix products, arithmetic and copies ran while one was open for 0% of the time, Pallas kernels for 7%

profile of v9, /device:TPU:1, one launch (start us, length us, event | category | flops | bytes accessed | tf_op | source)
XLA Modules:
  0.0 68.4 jit_solution(1170301140788084556)
XLA Ops:
  0.6 2.9 %prepare_keys.1 = bf16[8,352,128]{2,1,0:T(8,128)(2,1)} custom-call(s32[1]{0:T(128)} %bitcast.tile_ref, bf16[3,144,1024]{2,1,0:T(8,128)(2,1)} %bitcast.37, bf16[3,144,1024]{2,1,0:T(8,128)(2,1)} %bitcast.38, bf16[32,2,1024]{2,1,0:T(2,128)(2,1)} %text_ref.1, f32[1,128]{1,0:T(1,128)} %bitcast.41, f32[16,2,144,128]{3,2,1,0:T(8,128)} %constant.52.clone.table_ref), custom_call_target="tpu_custom_call" | custom-call | tf_op jit(solution)/shard_map/prepare_keys/pallas_call | solution.py:365
  3.5 0.0 copy-start.3
  3.6 0.0 copy-start.8
  3.6 6.5 %all-to-all-start = ((bf16[8,352,128]{2,1,0:T(8,128)(2,1)}), bf16[8,352,128]{2,1,0:T(8,128)(2,1)S(1)}, u32[]{:S(2)}, u32[]{:S(2)}) async-start(bf16[8,352,128]{2,1,0:T(8,128)(2,1)} %prepare_keys.1), calls=%async_computation | async-start | bytes 1441792 | tf_op jit(solution)/shard_map/all_to_all | solution.py:382
  10.1 2.2 %prepare_queries.1 = bf16[8,144,128]{2,1,0:T(8,128)(2,1)} custom-call(s32[1]{0:T(128)} %bitcast.tile_ref, bf16[3,144,1024]{2,1,0:T(8,128)(2,1)} %bitcast.39, f32[1,128]{1,0:T(1,128)} %bitcast.40, f32[16,2,144,128]{3,2,1,0:T(8,128)} %constant.52.clone.table_ref), custom_call_target="tpu_custom_call" | custom-call | tf_op jit(solution)/shard_map/prepare_queries/pallas_call | solution.py:383
  12.2 6.4 %all-to-all-done.own_ref = bf16[8,352,128]{2,1,0:T(8,128)(2,1)S(1)} async-done(((bf16[8,352,128]{2,1,0:T(8,128)(2,1)}), bf16[8,352,128]{2,1,0:T(8,128)(2,1)S(1)}, u32[]{:S(2)}, u32[]{:S(2)}) %all-to-all-start) | async-done | bytes 720928 | tf_op jit(solution)/shard_map/all_to_all | solution.py:382
  18.6 5.0 %collective-permute-start = (bf16[8,352,128]{2,1,0:T(8,128)(2,1)S(1)}, bf16[8,352,128]{2,1,0:T(8,128)(2,1)S(1)}, u32[]{:S(2)}, u32[]{:S(2)}) collective-permute-start(bf16[8,352,128]{2,1,0:T(8,128)(2,1)S(1)} %all-to-all-done.own_ref), channel_id=1, source_target_pairs={{0,6},{1,17},{2,4},{3,19},{4,2},{5,21},{6,0},{7,23},{8,14},{9,25},... | collective-permute-start | bytes 2162696 | tf_op jit(solution)/shard_map/ppermute | solution.py:395
  23.6 5.8 %all-to-all-start.1 = ((bf16[8,144,128]{2,1,0:T(8,128)(2,1)}), bf16[8,144,128]{2,1,0:T(8,128)(2,1)S(1)}, u32[]{:S(2)}, u32[]{:S(2)}) async-start(bf16[8,144,128]{2,1,0:T(8,128)(2,1)} %prepare_queries.1), calls=%async_computation.1 | async-start | bytes 589824 | tf_op jit(solution)/shard_map/all_to_all | solution.py:396
  30.0 0.1 pad_add_fusion.group_ref
  30.1 5.7 %all-to-all-done.1 = bf16[8,144,128]{2,1,0:T(8,128)(2,1)S(1)} async-done(((bf16[8,144,128]{2,1,0:T(8,128)(2,1)}), bf16[8,144,128]{2,1,0:T(8,128)(2,1)S(1)}, u32[]{:S(2)}, u32[]{:S(2)}) %all-to-all-start.1) | async-done | bytes 294944 | tf_op jit(solution)/shard_map/all_to_all | solution.py:396
  35.8 0.0 copy-done.3
  35.8 0.0 copy-done.8
  35.8 2.9 %attend_local.1 = (f32[1152,256]{1,0:T(8,128)S(1)}, f32[1152,128]{1,0:T(8,128)S(1)}) custom-call(s32[2]{0:T(128)S(1)} %pad_add_fusion.group_ref, s32[2]{0:T(128)S(1)} %copy-done.8, s32[1]{0:T(128)S(6)} %copy.21.text_len_ref, s32[4,3,1408]{2,1,0:T(4,128)S(1)} %copy-done.3, bf16[1152,128]{1,0:T(8,128)(2,1)S(1)} %bitcast.26, ...), custom_call_target="tpu_custom_call" | custom-call | tf_op jit(solution)/shard_map/attend_local/pallas_call | solution.py:400
  38.7 5.8 %collective-permute-done.far_ref = bf16[8,352,128]{2,1,0:T(8,128)(2,1)S(1)} collective-permute-done((bf16[8,352,128]{2,1,0:T(8,128)(2,1)S(1)}, bf16[8,352,128]{2,1,0:T(8,128)(2,1)S(1)}, u32[]{:S(2)}, u32[]{:S(2)}) %collective-permute-start) | collective-permute-done | bytes 720928 | tf_op jit(solution)/shard_map/ppermute | solution.py:395
  44.5 3.2 %attend_far.1 = (bf16[1152,128]{1,0:T(8,128)(2,1)S(1)}, bf16[1024,1280]{1,0:T(8,128)(2,1)S(1)}) custom-call(s32[2]{0:T(128)S(1)} %pad_add_fusion.group_ref, s32[2]{0:T(128)S(1)} %copy-done.8, s32[1]{0:T(128)S(6)} %copy.21.text_len_ref, s32[4,3,1408]{2,1,0:T(4,128)S(1)} %copy-done.3, bf16[1152,128]{1,0:T(8,128)(2,1)S(1)} %bitcast.27, ...), custom_call_target="tpu_custom_call" | custom-call | tf_op jit(solution)/shard_map/attend_far/pallas_call | solution.py:412
  47.7 11.4 %all_to_all.15.attended_ref = bf16[8,144,128]{2,1,0:T(8,128)(2,1)S(1)} all-to-all(bf16[8,144,128]{2,1,0:T(8,128)(2,1)S(1)} %bitcast.31), channel_id=1, replica_groups={{0,2,8,10,16,18,24,26},{6,4,14,12,22,20,30,28},{1,3,5,7,9,11,13,15},{17..., dimensions={0} | all-to-all | bytes 589824 | tf_op jit(solution)/shard_map/all_to_all | solution.py:425
  59.1 0.0 copy-start
  59.1 0.0 copy-start.1
  59.1 0.0 copy-start.2
  59.1 0.0 copy-start.4
  59.1 0.0 copy-start.5
  59.2 0.0 copy-start.6
  59.2 0.0 copy-start.7
  59.2 0.0 copy-start.9
  59.2 0.0 copy-start.10
  59.2 2.8 %project.1.own_ref = bf16[144,3072]{1,0:T(8,128)(2,1)S(1)} custom-call(bf16[8,144,128]{2,1,0:T(8,128)(2,1)S(1)} %all_to_all.15.attended_ref, bf16[1024,1280]{1,0:T(8,128)(2,1)S(1)} %get-tuple-element.15.refs_0_, bf16[1024,3072]{1,0:T(8,128)(2,1)} %refs_1_.1), custom_call_target="tpu_custom_call" | custom-call | tf_op jit(solution)/shard_map/project/pallas_call | solution.py:427
  62.0 1.7 %collective-permute-start.1 = (bf16[144,3072]{1,0:T(8,128)(2,1)S(1)}, bf16[144,3072]{1,0:T(8,128)(2,1)S(1)}, u32[]{:S(2)}, u32[]{:S(2)}) collective-permute-start(bf16[144,3072]{1,0:T(8,128)(2,1)S(1)} %project.1.own_ref), channel_id=1, source_target_pairs={{0,1},{1,0},{2,3},{3,2},{4,5},{5,4},{6,7},{7,6},{8,9},{9,8},{10,11... | collective-permute-start | bytes 2654216 | tf_op jit(solution)/shard_map/ppermute | solution.py:436
  64.4 1.4 %collective-permute-done.1.other_ref = bf16[144,3072]{1,0:T(8,128)(2,1)S(1)} collective-permute-done((bf16[144,3072]{1,0:T(8,128)(2,1)S(1)}, bf16[144,3072]{1,0:T(8,128)(2,1)S(1)}, u32[]{:S(2)}, u32[]{:S(2)}) %collective-permute-start.1) | collective-permute-done | bytes 884768 | tf_op jit(solution)/shard_map/ppermute | solution.py:436
  65.8 0.0 copy-done
  65.8 0.0 copy-done.1
  65.8 0.0 copy-done.2
  65.8 0.0 copy-done.4
  65.8 0.0 copy-done.5
  65.8 0.0 copy-done.6
  65.9 0.0 copy-done.7
  65.9 0.0 copy-done.9
  65.9 0.0 copy-done.10
  65.9 2.5 %final_layer.1 = (f32[64,144]{1,0:T(8,128)}, f32[64,144]{1,0:T(8,128)}) custom-call(s32[1]{0:T(128)} %bitcast.tile_ref, s32[2]{0:T(128)S(1)} %copy-done.8, s32[1]{0:T(128)S(6)} %copy.22.timestep_ref, s32[2,144]{1,0:T(2,128)S(1)} %copy-done.9, bf16[144,3072]{1,0:T(8,128)(2,1)S(1)} %project.1.own_ref, bf16[144,3072]{1,0:T(8,128)(2,1)S(1)} %collective-permute-done.1.other_ref, ...), custom_call_target="tpu_custom_call" | custom-call | tf_op jit(solution)/shard_map/final_layer/pallas_call | solution.py:439
Async XLA Ops:
  3.5 32.3 %copy-start.3 = (s32[4,3,1408]{2,1,0:T(4,128)S(1)}, s32[4,3,1408]{2,1,0:T(4,128)}, u32[]{:S(2)}) copy-start(s32[4,3,1408]{2,1,0:T(4,128)} %constant.53.clone.table_ref) | copy-start | bytes 202756
  3.6 32.3 %copy-start.8 = (s32[2]{0:T(128)S(1)}, s32[2]{0:T(128)}, u32[]{:S(2)}) copy-start(s32[2]{0:T(128)} %size_ref.5) | copy-start | bytes 28
  3.6 15.0 %all-to-all-start = ((bf16[8,352,128]{2,1,0:T(8,128)(2,1)}), bf16[8,352,128]{2,1,0:T(8,128)(2,1)S(1)}, u32[]{:S(2)}, u32[]{:S(2)}) async-start(bf16[8,352,128]{2,1,0:T(8,128)(2,1)} %prepare_keys.1), calls=%async_computation | async-start | bytes 1441792 | tf_op jit(solution)/shard_map/all_to_all | solution.py:382
  18.6 25.9 %collective-permute-start = (bf16[8,352,128]{2,1,0:T(8,128)(2,1)S(1)}, bf16[8,352,128]{2,1,0:T(8,128)(2,1)S(1)}, u32[]{:S(2)}, u32[]{:S(2)}) collective-permute-start(bf16[8,352,128]{2,1,0:T(8,128)(2,1)S(1)} %all-to-all-done.own_ref), channel_id=1, source_target_pairs={{0,6},{1,17},{2,4},{3,19},{4,2},{5,21},{6,0},{7,23},{8,14},{9,25},... | collective-permute-start | bytes 2162696 | tf_op jit(solution)/shard_map/ppermute | solution.py:395
  23.6 12.2 %all-to-all-start.1 = ((bf16[8,144,128]{2,1,0:T(8,128)(2,1)}), bf16[8,144,128]{2,1,0:T(8,128)(2,1)S(1)}, u32[]{:S(2)}, u32[]{:S(2)}) async-start(bf16[8,144,128]{2,1,0:T(8,128)(2,1)} %prepare_queries.1), calls=%async_computation.1 | async-start | bytes 589824 | tf_op jit(solution)/shard_map/all_to_all | solution.py:396
  59.1 6.7 %copy-start = (bf16[1,144,3072]{2,1,0:T(8,128)(2,1)S(1)}, bf16[1,144,3072]{2,1,0:T(8,128)(2,1)}, u32[]{:S(2)}) copy-start(bf16[1,144,3072]{2,1,0:T(8,128)(2,1)} %param.24) | copy-start | bytes 2654212
  59.1 6.7 %copy-start.1 = (bf16[1,144,3072]{2,1,0:T(8,128)(2,1)S(1)}, bf16[1,144,3072]{2,1,0:T(8,128)(2,1)}, u32[]{:S(2)}) copy-start(bf16[1,144,3072]{2,1,0:T(8,128)(2,1)} %param.25) | copy-start | bytes 2654212
  59.1 6.7 %copy-start.2 = (bf16[3072,64]{0,1:T(8,128)(2,1)S(1)}, bf16[3072,64]{0,1:T(8,128)(2,1)}, u32[]{:S(2)}) copy-start(bf16[3072,64]{0,1:T(8,128)(2,1)} %param.29) | copy-start | bytes 1179652
  59.1 6.7 %copy-start.4 = (f32[1,144,64]{1,2,0:T(8,128)S(1)}, f32[1,144,64]{1,2,0:T(8,128)}, u32[]{:S(2)}) copy-start(f32[1,144,64]{1,2,0:T(8,128)} %param.31) | copy-start | bytes 110596
  59.1 6.7 %copy-start.5 = (f32[3072]{0:T(1024)S(1)}, f32[3072]{0:T(1024)}, u32[]{:S(2)}) copy-start(f32[3072]{0:T(1024)} %param.26) | copy-start | bytes 36868
  59.2 6.7 %copy-start.6 = (f32[3072]{0:T(1024)S(1)}, f32[3072]{0:T(1024)}, u32[]{:S(2)}) copy-start(f32[3072]{0:T(1024)} %param.27) | copy-start | bytes 36868
  59.2 6.7 %copy-start.7 = (f32[3072]{0:T(1024)S(1)}, f32[3072]{0:T(1024)}, u32[]{:S(2)}) copy-start(f32[3072]{0:T(1024)} %param.28) | copy-start | bytes 36868
  59.2 6.7 %copy-start.9 = (s32[2,144]{1,0:T(2,128)S(1)}, s32[2,144]{1,0:T(2,128)}, u32[]{:S(2)}) copy-start(s32[2,144]{1,0:T(2,128)} %constant.54.clone.local_ref) | copy-start | bytes 3460
  59.2 6.7 %copy-start.10 = (f32[64]{0:T(128)S(1)}, f32[64]{0:T(128)}, u32[]{:S(2)}) copy-start(f32[64]{0:T(128)} %param.30) | copy-start | bytes 772
  62.0 3.8 %collective-permute-start.1 = (bf16[144,3072]{1,0:T(8,128)(2,1)S(1)}, bf16[144,3072]{1,0:T(8,128)(2,1)S(1)}, u32[]{:S(2)}, u32[]{:S(2)}) collective-permute-start(bf16[144,3072]{1,0:T(8,128)(2,1)S(1)} %project.1.own_ref), channel_id=1, source_target_pairs={{0,1},{1,0},{2,3},{3,2},{4,5},{5,4},{6,7},{7,6},{8,9},{9,8},{10,11... | collective-permute-start | bytes 2654216 | tf_op jit(solution)/shard_map/ppermute | solution.py:436

commit v10 on v9

--- a/solution.py
+++ b/solution.py
@@ -271,6 +271,9 @@
     velocity_ref,
     next_ref,
     modulated_s,
+    velocity_s,
+    next_s,
+    sems,
 ):
     rows = 16
     for start in range(0, PIX, rows):
@@ -298,6 +301,9 @@
     tile_col = tile - tile_row * GRID_X
     live = (local_ref[0:1, :] < size_ref[0] - tile_row * TILE_H) & (local_ref[1:2, :] < size_ref[1] - tile_col * TILE_W)
     velocity = jnp.where(live, velocity, 0.0)
+    velocity_s[...] = velocity
+    send_velocity = pltpu.make_async_copy(velocity_s, velocity_ref, sems.at[0])
+    send_velocity.start()
     area = jnp.full((1, PIX), size_ref[0] * size_ref[1], jnp.int32).astype(jnp.float32)
     moment = jnp.full((1, PIX), timestep_ref[0], jnp.int32).astype(jnp.float32)
     shift_factor = jnp.exp(0.5 + 0.65 * (area - 256.0) / 3840.0)
@@ -308,8 +314,11 @@
         return shift_factor * at / (shift_factor * at + 1.0 - at)
 
     step = sigma_of(next_time) - sigma_of(now_time)
-    velocity_ref[...] = velocity
-    next_ref[...] = latent_ref[...] + step * velocity
+    next_s[...] = latent_ref[...] + step * velocity
+    send_next = pltpu.make_async_copy(next_s, next_ref, sems.at[1])
+    send_next.start()
+    send_velocity.wait()
+    send_next.wait()
 
 
 SMEM = pl.BlockSpec(memory_space=pltpu.SMEM)
@@ -439,9 +448,14 @@
     velocity, latent_next = pl.pallas_call(
         final_kernel,
         in_specs=[SMEM, SMEM, SMEM] + [VMEM] * 11,
-        out_specs=(VMEM, VMEM),
+        out_specs=(HBM, HBM),
         out_shape=(jax.ShapeDtypeStruct((latents, PIX), jnp.float32),) * 2,
-        scratch_shapes=[pltpu.VMEM((PIX, model), bf16)],
+        scratch_shapes=[
+            pltpu.VMEM((PIX, model), bf16),
+            pltpu.VMEM((latents, PIX), jnp.float32),
+            pltpu.VMEM((latents, PIX), jnp.float32),
+            pltpu.SemaphoreType.DMA((2,)),
+        ],
         compiler_params=params(12),
         name="final_layer",
     )(

time: 68.7 us -> 68.7 us (level)
  no operation moved by 1% of the time
where the time goes in v10:
time: 68.7 us; the launch traced here: 68.4 us
  waiting for transfers between devices  19.3 us (28%)
  starting transfers between devices  19 us (28%)
  Pallas kernels  16.5 us (24%)
  blocking collectives  11.4 us (17%)
  between operations  2.06 us (3%)
    all_to_all x1, blocking collectives, shards(): lax.all_to_all(attended, mesh_axes, 0, 0, axis_index_groups=groups, tiled...  11.4 us
    all_to_all x1, starting transfers between devices, shards(): lax.all_to_all(key_value, mesh_axes, 0, 0, axis_index_groups=groups, tile...  6.51 us
    all_to_all x1, waiting for transfers between devices, shards(): lax.all_to_all(key_value, mesh_axes, 0, 0, axis_index_groups=groups, tile...  6.38 us
    ppermute x1, waiting for transfers between devices, shards(): far = lax.ppermute(own, mesh_axes, across)  5.8 us
    all_to_all x1, starting transfers between devices, shards(): lax.all_to_all(queries, mesh_axes, 0, 0, axis_index_groups=groups, tiled=...  5.75 us
    all_to_all x1, waiting for transfers between devices, shards(): lax.all_to_all(queries, mesh_axes, 0, 0, axis_index_groups=groups, tiled=...  5.71 us
    ppermute x1, starting transfers between devices, shards(): far = lax.ppermute(own, mesh_axes, across)  5.01 us
    pallas_call x1, Pallas kernels, shards(): pl.pallas_call(remote_kernel, in_specs=[SMEM, SMEM, SMEM] + [VMEM] * 5 +...  3.2 us
  transfers between devices with their start and end apart: 4, of which 4 were waited for; matrix products, arithmetic and copies ran while one was open for 0% of the time, Pallas kernels for 7%

profile of v10, /device:TPU:1, one launch (start us, length us, event | category | flops | bytes accessed | tf_op | source)
XLA Modules:
  0.0 68.4 jit_solution(217536010455296799)
XLA Ops:
  0.6 2.9 %prepare_keys.1 = bf16[8,352,128]{2,1,0:T(8,128)(2,1)} custom-call(s32[1]{0:T(128)} %bitcast.tile_ref, bf16[3,144,1024]{2,1,0:T(8,128)(2,1)} %bitcast.37, bf16[3,144,1024]{2,1,0:T(8,128)(2,1)} %bitcast.38, bf16[32,2,1024]{2,1,0:T(2,128)(2,1)} %text_ref.1, f32[1,128]{1,0:T(1,128)} %bitcast.41, f32[16,2,144,128]{3,2,1,0:T(8,128)} %constant.52.clone.table_ref), custom_call_target="tpu_custom_call" | custom-call | tf_op jit(solution)/shard_map/prepare_keys/pallas_call | solution.py:374
  3.5 0.0 copy-start.3
  3.6 0.0 copy-start.8
  3.6 6.5 %all-to-all-start = ((bf16[8,352,128]{2,1,0:T(8,128)(2,1)}), bf16[8,352,128]{2,1,0:T(8,128)(2,1)S(1)}, u32[]{:S(2)}, u32[]{:S(2)}) async-start(bf16[8,352,128]{2,1,0:T(8,128)(2,1)} %prepare_keys.1), calls=%async_computation | async-start | bytes 1441792 | tf_op jit(solution)/shard_map/all_to_all | solution.py:391
  10.1 2.2 %prepare_queries.1 = bf16[8,144,128]{2,1,0:T(8,128)(2,1)} custom-call(s32[1]{0:T(128)} %bitcast.tile_ref, bf16[3,144,1024]{2,1,0:T(8,128)(2,1)} %bitcast.39, f32[1,128]{1,0:T(1,128)} %bitcast.40, f32[16,2,144,128]{3,2,1,0:T(8,128)} %constant.52.clone.table_ref), custom_call_target="tpu_custom_call" | custom-call | tf_op jit(solution)/shard_map/prepare_queries/pallas_call | solution.py:392
  12.2 6.4 %all-to-all-done.own_ref = bf16[8,352,128]{2,1,0:T(8,128)(2,1)S(1)} async-done(((bf16[8,352,128]{2,1,0:T(8,128)(2,1)}), bf16[8,352,128]{2,1,0:T(8,128)(2,1)S(1)}, u32[]{:S(2)}, u32[]{:S(2)}) %all-to-all-start) | async-done | bytes 720928 | tf_op jit(solution)/shard_map/all_to_all | solution.py:391
  18.6 5.0 %collective-permute-start = (bf16[8,352,128]{2,1,0:T(8,128)(2,1)S(1)}, bf16[8,352,128]{2,1,0:T(8,128)(2,1)S(1)}, u32[]{:S(2)}, u32[]{:S(2)}) collective-permute-start(bf16[8,352,128]{2,1,0:T(8,128)(2,1)S(1)} %all-to-all-done.own_ref), channel_id=1, source_target_pairs={{0,6},{1,17},{2,4},{3,19},{4,2},{5,21},{6,0},{7,23},{8,14},{9,25},... | collective-permute-start | bytes 2162696 | tf_op jit(solution)/shard_map/ppermute | solution.py:404
  23.6 5.8 %all-to-all-start.1 = ((bf16[8,144,128]{2,1,0:T(8,128)(2,1)}), bf16[8,144,128]{2,1,0:T(8,128)(2,1)S(1)}, u32[]{:S(2)}, u32[]{:S(2)}) async-start(bf16[8,144,128]{2,1,0:T(8,128)(2,1)} %prepare_queries.1), calls=%async_computation.1 | async-start | bytes 589824 | tf_op jit(solution)/shard_map/all_to_all | solution.py:405
  30.0 0.1 pad_add_fusion.group_ref
  30.1 5.7 %all-to-all-done.1 = bf16[8,144,128]{2,1,0:T(8,128)(2,1)S(1)} async-done(((bf16[8,144,128]{2,1,0:T(8,128)(2,1)}), bf16[8,144,128]{2,1,0:T(8,128)(2,1)S(1)}, u32[]{:S(2)}, u32[]{:S(2)}) %all-to-all-start.1) | async-done | bytes 294944 | tf_op jit(solution)/shard_map/all_to_all | solution.py:405
  35.8 0.0 copy-done.3
  35.8 0.0 copy-done.8
  35.8 2.9 %attend_local.1 = (f32[1152,256]{1,0:T(8,128)S(1)}, f32[1152,128]{1,0:T(8,128)S(1)}) custom-call(s32[2]{0:T(128)S(1)} %pad_add_fusion.group_ref, s32[2]{0:T(128)S(1)} %copy-done.8, s32[1]{0:T(128)S(6)} %copy.21.text_len_ref, s32[4,3,1408]{2,1,0:T(4,128)S(1)} %copy-done.3, bf16[1152,128]{1,0:T(8,128)(2,1)S(1)} %bitcast.26, ...), custom_call_target="tpu_custom_call" | custom-call | tf_op jit(solution)/shard_map/attend_local/pallas_call | solution.py:409
  38.7 5.8 %collective-permute-done.far_ref = bf16[8,352,128]{2,1,0:T(8,128)(2,1)S(1)} collective-permute-done((bf16[8,352,128]{2,1,0:T(8,128)(2,1)S(1)}, bf16[8,352,128]{2,1,0:T(8,128)(2,1)S(1)}, u32[]{:S(2)}, u32[]{:S(2)}) %collective-permute-start) | collective-permute-done | bytes 720928 | tf_op jit(solution)/shard_map/ppermute | solution.py:404
  44.5 3.2 %attend_far.1 = (bf16[1152,128]{1,0:T(8,128)(2,1)S(1)}, bf16[1024,1280]{1,0:T(8,128)(2,1)S(1)}) custom-call(s32[2]{0:T(128)S(1)} %pad_add_fusion.group_ref, s32[2]{0:T(128)S(1)} %copy-done.8, s32[1]{0:T(128)S(6)} %copy.21.text_len_ref, s32[4,3,1408]{2,1,0:T(4,128)S(1)} %copy-done.3, bf16[1152,128]{1,0:T(8,128)(2,1)S(1)} %bitcast.27, ...), custom_call_target="tpu_custom_call" | custom-call | tf_op jit(solution)/shard_map/attend_far/pallas_call | solution.py:421
  47.7 11.4 %all_to_all.15.attended_ref = bf16[8,144,128]{2,1,0:T(8,128)(2,1)S(1)} all-to-all(bf16[8,144,128]{2,1,0:T(8,128)(2,1)S(1)} %bitcast.31), channel_id=1, replica_groups={{0,2,8,10,16,18,24,26},{6,4,14,12,22,20,30,28},{1,3,5,7,9,11,13,15},{17..., dimensions={0} | all-to-all | bytes 589824 | tf_op jit(solution)/shard_map/all_to_all | solution.py:434
  59.1 0.0 copy-start
  59.1 0.0 copy-start.1
  59.1 0.0 copy-start.2
  59.1 0.0 copy-start.4
  59.1 0.0 copy-start.5
  59.2 0.0 copy-start.6
  59.2 0.0 copy-start.7
  59.2 0.0 copy-start.9
  59.2 0.0 copy-start.10
  59.2 2.8 %project.1.own_ref = bf16[144,3072]{1,0:T(8,128)(2,1)S(1)} custom-call(bf16[8,144,128]{2,1,0:T(8,128)(2,1)S(1)} %all_to_all.15.attended_ref, bf16[1024,1280]{1,0:T(8,128)(2,1)S(1)} %get-tuple-element.15.refs_0_, bf16[1024,3072]{1,0:T(8,128)(2,1)} %refs_1_.1), custom_call_target="tpu_custom_call" | custom-call | tf_op jit(solution)/shard_map/project/pallas_call | solution.py:436
  62.0 1.7 %collective-permute-start.1 = (bf16[144,3072]{1,0:T(8,128)(2,1)S(1)}, bf16[144,3072]{1,0:T(8,128)(2,1)S(1)}, u32[]{:S(2)}, u32[]{:S(2)}) collective-permute-start(bf16[144,3072]{1,0:T(8,128)(2,1)S(1)} %project.1.own_ref), channel_id=1, source_target_pairs={{0,1},{1,0},{2,3},{3,2},{4,5},{5,4},{6,7},{7,6},{8,9},{9,8},{10,11... | collective-permute-start | bytes 2654216 | tf_op jit(solution)/shard_map/ppermute | solution.py:445
  64.4 1.4 %collective-permute-done.1.other_ref = bf16[144,3072]{1,0:T(8,128)(2,1)S(1)} collective-permute-done((bf16[144,3072]{1,0:T(8,128)(2,1)S(1)}, bf16[144,3072]{1,0:T(8,128)(2,1)S(1)}, u32[]{:S(2)}, u32[]{:S(2)}) %collective-permute-start.1) | collective-permute-done | bytes 884768 | tf_op jit(solution)/shard_map/ppermute | solution.py:445
  65.8 0.0 copy-done
  65.8 0.0 copy-done.1
  65.8 0.0 copy-done.2
  65.8 0.0 copy-done.4
  65.8 0.0 copy-done.5
  65.8 0.0 copy-done.6
  65.9 0.0 copy-done.7
  65.9 0.0 copy-done.9
  65.9 0.0 copy-done.10
  65.9 2.5 %final_layer.1 = (f32[64,144]{1,0:T(8,128)}, f32[64,144]{1,0:T(8,128)}) custom-call(s32[1]{0:T(128)} %bitcast.tile_ref, s32[2]{0:T(128)S(1)} %copy-done.8, s32[1]{0:T(128)S(6)} %copy.22.timestep_ref, s32[2,144]{1,0:T(2,128)S(1)} %copy-done.9, bf16[144,3072]{1,0:T(8,128)(2,1)S(1)} %project.1.own_ref, bf16[144,3072]{1,0:T(8,128)(2,1)S(1)} %collective-permute-done.1.other_ref, ...), custom_call_target="tpu_custom_call" | custom-call | tf_op jit(solution)/shard_map/final_layer/pallas_call | solution.py:448
Async XLA Ops:
  3.5 32.3 %copy-start.3 = (s32[4,3,1408]{2,1,0:T(4,128)S(1)}, s32[4,3,1408]{2,1,0:T(4,128)}, u32[]{:S(2)}) copy-start(s32[4,3,1408]{2,1,0:T(4,128)} %constant.53.clone.table_ref) | copy-start | bytes 202756
  3.6 32.3 %copy-start.8 = (s32[2]{0:T(128)S(1)}, s32[2]{0:T(128)}, u32[]{:S(2)}) copy-start(s32[2]{0:T(128)} %size_ref.5) | copy-start | bytes 28
  3.6 15.0 %all-to-all-start = ((bf16[8,352,128]{2,1,0:T(8,128)(2,1)}), bf16[8,352,128]{2,1,0:T(8,128)(2,1)S(1)}, u32[]{:S(2)}, u32[]{:S(2)}) async-start(bf16[8,352,128]{2,1,0:T(8,128)(2,1)} %prepare_keys.1), calls=%async_computation | async-start | bytes 1441792 | tf_op jit(solution)/shard_map/all_to_all | solution.py:391
  18.6 25.9 %collective-permute-start = (bf16[8,352,128]{2,1,0:T(8,128)(2,1)S(1)}, bf16[8,352,128]{2,1,0:T(8,128)(2,1)S(1)}, u32[]{:S(2)}, u32[]{:S(2)}) collective-permute-start(bf16[8,352,128]{2,1,0:T(8,128)(2,1)S(1)} %all-to-all-done.own_ref), channel_id=1, source_target_pairs={{0,6},{1,17},{2,4},{3,19},{4,2},{5,21},{6,0},{7,23},{8,14},{9,25},... | collective-permute-start | bytes 2162696 | tf_op jit(solution)/shard_map/ppermute | solution.py:404
  23.6 12.2 %all-to-all-start.1 = ((bf16[8,144,128]{2,1,0:T(8,128)(2,1)}), bf16[8,144,128]{2,1,0:T(8,128)(2,1)S(1)}, u32[]{:S(2)}, u32[]{:S(2)}) async-start(bf16[8,144,128]{2,1,0:T(8,128)(2,1)} %prepare_queries.1), calls=%async_computation.1 | async-start | bytes 589824 | tf_op jit(solution)/shard_map/all_to_all | solution.py:405
  59.1 6.7 %copy-start = (bf16[1,144,3072]{2,1,0:T(8,128)(2,1)S(1)}, bf16[1,144,3072]{2,1,0:T(8,128)(2,1)}, u32[]{:S(2)}) copy-start(bf16[1,144,3072]{2,1,0:T(8,128)(2,1)} %param.24) | copy-start | bytes 2654212
  59.1 6.7 %copy-start.1 = (bf16[1,144,3072]{2,1,0:T(8,128)(2,1)S(1)}, bf16[1,144,3072]{2,1,0:T(8,128)(2,1)}, u32[]{:S(2)}) copy-start(bf16[1,144,3072]{2,1,0:T(8,128)(2,1)} %param.25) | copy-start | bytes 2654212
  59.1 6.7 %copy-start.2 = (bf16[3072,64]{0,1:T(8,128)(2,1)S(1)}, bf16[3072,64]{0,1:T(8,128)(2,1)}, u32[]{:S(2)}) copy-start(bf16[3072,64]{0,1:T(8,128)(2,1)} %param.29) | copy-start | bytes 1179652
  59.1 6.7 %copy-start.4 = (f32[1,144,64]{1,2,0:T(8,128)S(1)}, f32[1,144,64]{1,2,0:T(8,128)}, u32[]{:S(2)}) copy-start(f32[1,144,64]{1,2,0:T(8,128)} %param.31) | copy-start | bytes 110596
  59.1 6.7 %copy-start.5 = (f32[3072]{0:T(1024)S(1)}, f32[3072]{0:T(1024)}, u32[]{:S(2)}) copy-start(f32[3072]{0:T(1024)} %param.26) | copy-start | bytes 36868
  59.2 6.7 %copy-start.6 = (f32[3072]{0:T(1024)S(1)}, f32[3072]{0:T(1024)}, u32[]{:S(2)}) copy-start(f32[3072]{0:T(1024)} %param.27) | copy-start | bytes 36868
  59.2 6.7 %copy-start.7 = (f32[3072]{0:T(1024)S(1)}, f32[3072]{0:T(1024)}, u32[]{:S(2)}) copy-start(f32[3072]{0:T(1024)} %param.28) | copy-start | bytes 36868
  59.2 6.7 %copy-start.9 = (s32[2,144]{1,0:T(2,128)S(1)}, s32[2,144]{1,0:T(2,128)}, u32[]{:S(2)}) copy-start(s32[2,144]{1,0:T(2,128)} %constant.54.clone.local_ref) | copy-start | bytes 3460
  59.2 6.7 %copy-start.10 = (f32[64]{0:T(128)S(1)}, f32[64]{0:T(128)}, u32[]{:S(2)}) copy-start(f32[64]{0:T(128)} %param.30) | copy-start | bytes 772
  62.0 3.8 %collective-permute-start.1 = (bf16[144,3072]{1,0:T(8,128)(2,1)S(1)}, bf16[144,3072]{1,0:T(8,128)(2,1)S(1)}, u32[]{:S(2)}, u32[]{:S(2)}) collective-permute-start(bf16[144,3072]{1,0:T(8,128)(2,1)S(1)} %project.1.own_ref), channel_id=1, source_target_pairs={{0,1},{1,0},{2,3},{3,2},{4,5},{5,4},{6,7},{7,6},{8,9},{9,8},{10,11... | collective-permute-start | bytes 2654216 | tf_op jit(solution)/shard_map/ppermute | solution.py:445
